TPU v7x, 32 devices: a whole 2x2x4 slice. The times are simulated.
32 devices in a mesh: dp: 4 (over y, x), mp: 8 (over z, core).
Axes of the slice: x: 2, y: 2, z: 4, core: 2. Of those that a mesh axis runs over, the one named last changes fastest.
Arguments:
- layer_in: bfloat16 [2048, 4, 2048], P('mp', 'dp'), may hold values from -18 to 18
- segment_ids: int32 [4, 2048], P('dp'), may hold values from 0 to 7, never falling along the last dimension, each value on 1 to 1024 neighbouring positions
- valid_counts: int32 [4], P('dp'), may hold values from 1024 to 2048
- norm_gain: float32 [2048], replicated, may hold values from 0.1 to 1.9
- norm_shift: float32 [2048], replicated, may hold values from -1.5 to 1.5
- w_qkv: bfloat16 [2048, 3, 2048], P(None, None, 'mp'), may hold values from -0.125 to 0.125
- b_qkv: bfloat16 [3, 2048], P(None, 'mp'), may hold values from -1.5 to 1.5
- w_out: bfloat16 [2048, 2048], P('mp'), may hold values from -0.5 to 0.5
- w_gate_up: bfloat16 [2048, 2, 5632], P(None, None, 'mp'), may hold values from -0.125 to 0.125
- w_down: bfloat16 [5632, 2048], P('mp'), may hold values from -0.078125 to 0.078125
- out_grad: bfloat16 [2048, 4, 2048], P('mp', 'dp'), may hold values from -6 to 6
Outputs:
- layer_out: bfloat16 [2048, 4, 2048], P('mp', 'dp')
- input_grad: float32 [2048, 4, 2048], P('mp', 'dp')
- grad_gain: float32 [2048], replicated
- grad_shift: float32 [2048], replicated
- grad_w_qkv: float32 [2048, 3, 2048], P(None, None, 'mp')
- grad_b_qkv: float32 [3, 2048], P(None, 'mp')
- grad_w_out: float32 [2048, 2048], P('mp')
- grad_w_gate_up: float32 [2048, 2, 5632], P(None, None, 'mp')
- grad_w_down: float32 [5632, 2048], P('mp')
- branch_rms: float32 [3], replicated
Inputs may be any that keep to these rules, and one draw needn't show every extreme that they name: `segment_ids`: segment ids never fall along a row; each document has 1 to 1024 tokens.
All inputs are finite; a program needn't handle non-finite values.
Results may differ from a plain program's by a relative error of at most 0.014.
Values may be sent and summed in bfloat16 or wider, within the bound.
No kernel may reach another device: no remote copies, remote signals or barrier semaphores. Data moves between devices by JAX's collectives and lax.ppermute only.
A program may use at most 256 MiB of HBM per device.

v0:
```python
import functools

import jax
import jax.numpy as jnp
from jax import lax
from jax.experimental import pallas as pl
from jax.experimental.pallas import tpu as pltpu
from jax.sharding import PartitionSpec as P

HEAD_DIM = 64
ROT = 16
EPSILON = 1e-05
BQ = 128
BK = 256
NEG = -1e30
F32 = jnp.float32
BF16 = jnp.bfloat16


def starts_of(segment_ids):
    length = segment_ids.shape[1]
    steps_all = jnp.arange(length, dtype=jnp.int32)[None, :]
    change = jnp.concatenate(
        [
            jnp.ones_like(segment_ids[:, :1]),
            (segment_ids[:, 1:] != segment_ids[:, :-1]).astype(jnp.int32),
        ],
        axis=1,
    )
    return lax.cummax(jnp.where(change > 0, steps_all, jnp.zeros_like(change)), axis=1)


def rotary_lanes(positions):
    half_rot = ROT // 2
    lane = jnp.arange(2 * HEAD_DIM, dtype=jnp.int32) % HEAD_DIM
    power = (lane % half_rot).astype(F32)
    frequency = jnp.where(lane < ROT, 10000.0 ** (-(power * 2.0) / ROT), 0.0)
    angles = positions.astype(F32)[:, None] * frequency
    sine = jnp.sin(angles)
    low = jnp.where(lane < half_rot, -sine, 0.0)
    high = jnp.where((lane >= half_rot) & (lane < ROT), sine, 0.0)
    return jnp.cos(angles), low, high


def lane_tile(table, columns):
    return jnp.concatenate([table] * (columns // table.shape[1]), axis=1)


def turn(values, cosine, low, high):
    columns = values.shape[1]
    half_rot = ROT // 2
    return (
        values * lane_tile(cosine, columns)
        + pltpu.roll(values, columns - half_rot, 1) * lane_tile(low, columns)
        + pltpu.roll(values, half_rot, 1) * lane_tile(high, columns)
    )


def project_kernel(x_ref, w_ref, b_ref, cos_ref, low_ref, high_ref, q_ref, k_ref, v_ref):
    tables = (cos_ref[...], low_ref[...], high_ref[...])

    def part(number):
        flat = jnp.dot(x_ref[...], w_ref[number], preferred_element_type=F32)
        return flat + b_ref[number : number + 1, :].astype(F32)

    queries = turn(part(0), *tables).astype(BF16)
    q_ref[...] = (queries.astype(F32) * HEAD_DIM**-0.5).astype(BF16)
    k_ref[...] = turn(part(1), *tables).astype(BF16)
    v_ref[...] = part(2).astype(BF16)


def project(gathered, w_qkv, b_qkv, tables):
    length, width = gathered.shape
    columns = w_qkv.shape[2]
    rows = min(256, length)
    table_spec = pl.BlockSpec((rows, tables[0].shape[1]), lambda i: (i, 0))
    out_spec = pl.BlockSpec((rows, columns), lambda i: (i, 0))
    return pl.pallas_call(
        project_kernel,
        grid=(length // rows,),
        in_specs=[
            pl.BlockSpec((rows, width), lambda i: (i, 0)),
            pl.BlockSpec(w_qkv.shape, lambda i: (0, 0, 0)),
            pl.BlockSpec(b_qkv.shape, lambda i: (0, 0)),
            table_spec,
            table_spec,
            table_spec,
        ],
        out_specs=[out_spec] * 3,
        out_shape=[jax.ShapeDtypeStruct((length, columns), BF16)] * 3,
        cost_estimate=pl.CostEstimate(
            flops=6 * length * width * columns,
            bytes_accessed=2 * (length * width + 3 * width * columns + 3 * length * columns),
            transcendentals=0,
        ),
        name="project",
    )(gathered, w_qkv, b_qkv, *tables)


def stack_heads(block):
    columns = block.shape[1]
    head_of = lax.broadcasted_iota(jnp.int32, block.shape, 1) // HEAD_DIM
    return jnp.concatenate(
        [
            jnp.where(head_of == head, block, jnp.zeros_like(block))
            for head in range(columns // HEAD_DIM)
        ],
        axis=0,
    )


def unstack_heads(stacked, block):
    heads = stacked.shape[1] // block
    return jnp.concatenate(
        [
            stacked[head * HEAD_DIM : (head + 1) * HEAD_DIM, head * block : (head + 1) * block]
            for head in range(heads)
        ],
        axis=0,
    ).T


def score_block(key_block, stacked_queries, key_at, start_row, query_row):
    scores = lax.dot_general(
        key_block, stacked_queries, (((1,), (1,)), ((), ())), preferred_element_type=F32
    )
    key_pos = key_at + lax.broadcasted_iota(jnp.int32, scores.shape, 0)
    allowed = (key_pos >= start_row) & (key_pos <= query_row)
    return scores, allowed


def query_rows(start_ref, block, heads):
    start_row = jnp.concatenate([start_ref[0]] * heads, axis=1)
    query_row = pl.program_id(0) * block + lax.broadcasted_iota(jnp.int32, (1, block), 1)
    return start_row, jnp.concatenate([query_row] * heads, axis=1)


def attend_kernel(first_ref, q_ref, k_ref, v_ref, start_ref, o_ref, lse_ref, acc_ref):
    block, columns = q_ref.shape
    heads = columns // HEAD_DIM
    index = pl.program_id(0)
    stacked = stack_heads(q_ref[...])
    start_row, query_row = query_rows(start_ref, block, heads)
    acc_ref[...] = jnp.zeros_like(acc_ref)

    def body(step, carry):
        highest, total = carry
        at = pl.multiple_of(step * BK, BK)
        scores, allowed = score_block(
            k_ref[pl.ds(at, BK), :], stacked, at, start_row, query_row
        )
        scores = jnp.where(allowed, scores, NEG)
        newest = jnp.maximum(highest, jnp.max(scores, axis=0, keepdims=True))
        weights = jnp.exp(scores - newest)
        scale = jnp.exp(highest - newest)
        total = total * scale + jnp.sum(weights, axis=0, keepdims=True)
        acc_ref[...] = acc_ref[...] * scale + lax.dot_general(
            v_ref[pl.ds(at, BK), :],
            weights.astype(BF16),
            (((0,), (0,)), ((), ())),
            preferred_element_type=F32,
        )
        return newest, total

    highest, total = lax.fori_loop(
        first_ref[index],
        (index * block + block - 1) // BK + 1,
        body,
        (jnp.full((1, heads * block), NEG, F32), jnp.zeros((1, heads * block), F32)),
    )
    o_ref[...] = unstack_heads(acc_ref[...] / total, block).astype(BF16)
    lse_ref[0] = highest + jnp.log(total)


def attend(first, queries, key_rows, value_rows, start_blocks):
    length, columns = queries.shape
    blocks = length // BQ
    heads = columns // HEAD_DIM
    row_spec = pl.BlockSpec((BQ, columns), lambda i, f: (i, 0))
    whole = pl.BlockSpec((length, columns), lambda i, f: (0, 0))
    return pl.pallas_call(
        attend_kernel,
        grid_spec=pltpu.PrefetchScalarGridSpec(
            num_scalar_prefetch=1,
            grid=(blocks,),
            in_specs=[
                row_spec,
                whole,
                whole,
                pl.BlockSpec((1, 1, BQ), lambda i, f: (i, 0, 0)),
            ],
            out_specs=[
                row_spec,
                pl.BlockSpec((1, 1, heads * BQ), lambda i, f: (i, 0, 0)),
            ],
            scratch_shapes=[pltpu.VMEM((columns, heads * BQ), F32)],
        ),
        out_shape=[
            jax.ShapeDtypeStruct((length, columns), BF16),
            jax.ShapeDtypeStruct((blocks, 1, heads * BQ), F32),
        ],
        cost_estimate=pl.CostEstimate(
            flops=4 * length * 1024 * columns * heads,
            bytes_accessed=8 * length * columns,
            transcendentals=length * 1024 * heads,
        ),
        name="attend",
    )(first, queries, key_rows, value_rows, start_blocks)


def attend_back_kernel(
    first_ref,
    q_ref,
    k_ref,
    v_ref,
    do_ref,
    o_ref,
    lse_ref,
    start_ref,
    cos_ref,
    low_ref,
    high_ref,
    grad_ref,
    key_acc,
    value_acc,
    query_acc,
):
    block, columns = q_ref.shape
    heads = columns // HEAD_DIM
    length = k_ref.shape[0]
    index = pl.program_id(0)

    @pl.when(index == 0)
    def _():
        key_acc[...] = jnp.zeros_like(key_acc)
        value_acc[...] = jnp.zeros_like(value_acc)

    stacked = stack_heads(q_ref[...])
    stacked_do = stack_heads(do_ref[...])
    start_row, query_row = query_rows(start_ref, block, heads)
    lse_row = lse_ref[0]
    products = do_ref[...].astype(F32) * o_ref[...].astype(F32)
    head_rows = lax.broadcasted_iota(jnp.int32, (8, columns), 0)
    head_lanes = lax.broadcasted_iota(jnp.int32, (8, columns), 1) // HEAD_DIM
    picked = lax.dot_general(
        (head_rows == head_lanes).astype(F32),
        products,
        (((1,), (1,)), ((), ())),
        precision=lax.Precision.HIGHEST,
        preferred_element_type=F32,
    )
    inner_row = jnp.concatenate([picked[head : head + 1, :] for head in range(heads)], axis=1)
    query_acc[...] = jnp.zeros_like(query_acc)

    def body(step, carry):
        at = pl.multiple_of(step * BK, BK)
        key_block = k_ref[pl.ds(at, BK), :]
        scores, allowed = score_block(key_block, stacked, at, start_row, query_row)
        weights = jnp.where(allowed, jnp.exp(scores - lse_row), 0.0)
        grad_weights = lax.dot_general(
            v_ref[pl.ds(at, BK), :],
            stacked_do,
            (((1,), (1,)), ((), ())),
            preferred_element_type=F32,
        )
        grad_scores = (weights * (grad_weights - inner_row)).astype(BF16)
        value_acc[pl.ds(at, BK), :] += jnp.dot(
            weights.astype(BF16), stacked_do, preferred_element_type=F32
        )
        key_acc[pl.ds(at, BK), :] += jnp.dot(grad_scores, stacked, preferred_element_type=F32)
        query_acc[...] += lax.dot_general(
            key_block, grad_scores, (((0,), (0,)), ((), ())), preferred_element_type=F32
        )
        return carry

    lax.fori_loop(first_ref[index], (index * block + block - 1) // BK + 1, body, 0)

    def turn_back(grads, at, rows):
        kept = grads.astype(BF16).astype(F32)
        return turn(
            kept,
            cos_ref[pl.ds(at, rows), :],
            -low_ref[pl.ds(at, rows), :],
            -high_ref[pl.ds(at, rows), :],
        ).astype(BF16)

    at_query = pl.multiple_of(index * block, block)
    grad_ref[pl.ds(at_query, block), :columns] = turn_back(
        unstack_heads(query_acc[...], block) * HEAD_DIM**-0.5, at_query, block
    )

    @pl.when(index == pl.num_programs(0) - 1)
    def _():
        def finish(step, carry):
            at = pl.multiple_of(step * BK, BK)
            grad_ref[pl.ds(at, BK), columns : 2 * columns] = turn_back(
                key_acc[pl.ds(at, BK), :], at, BK
            )
            grad_ref[pl.ds(at, BK), 2 * columns :] = value_acc[pl.ds(at, BK), :].astype(BF16)
            return carry

        lax.fori_loop(0, length // BK, finish, 0)


def attend_back(first, queries, key_rows, value_rows, grad_att, attended, lse, start_blocks, tables):
    length, columns = queries.shape
    blocks = length // BQ
    heads = columns // HEAD_DIM
    row_spec = pl.BlockSpec((BQ, columns), lambda i, f: (i, 0))
    whole = pl.BlockSpec((length, columns), lambda i, f: (0, 0))
    table_spec = pl.BlockSpec(tables[0].shape, lambda i, f: (0, 0))
    return pl.pallas_call(
        attend_back_kernel,
        grid_spec=pltpu.PrefetchScalarGridSpec(
            num_scalar_prefetch=1,
            grid=(blocks,),
            in_specs=[
                row_spec,
                whole,
                whole,
                row_spec,
                row_spec,
                pl.BlockSpec((1, 1, heads * BQ), lambda i, f: (i, 0, 0)),
                pl.BlockSpec((1, 1, BQ), lambda i, f: (i, 0, 0)),
                table_spec,
                table_spec,
                table_spec,
            ],
            out_specs=pl.BlockSpec((length, 3 * columns), lambda i, f: (0, 0)),
            scratch_shapes=[
                pltpu.VMEM((length, columns), F32),
                pltpu.VMEM((length, columns), F32),
                pltpu.VMEM((columns, heads * BQ), F32),
            ],
        ),
        out_shape=jax.ShapeDtypeStruct((length, 3 * columns), BF16),
        cost_estimate=pl.CostEstimate(
            flops=10 * length * 1024 * columns * heads,
            bytes_accessed=16 * length * columns,
            transcendentals=length * 1024 * heads,
        ),
        name="attend_back",
    )(first, queries, key_rows, value_rows, grad_att, attended, lse, start_blocks, *tables)


def bits_of(name):
    size = lax.axis_size(name)
    count = size.bit_length() - 1
    return count if size == 1 << count else None


def swap(values, name, bit):
    size = lax.axis_size(name)
    return lax.ppermute(values, name, [(i, i ^ (1 << bit)) for i in range(size)])


def write_stacked(piece, outs):
    outs[0][0] = piece.astype(F32)


def write_rows(piece, outs):
    at = 0
    for out_ref in outs:
        size = out_ref.shape[0]
        out_ref[...] = piece[at : at + size, :].astype(F32)
        at += size


def write_lanes(piece, outs):
    parts, _, size = outs[0].shape
    for part in range(parts):
        outs[0][part] = piece[:, part * size : (part + 1) * size].astype(F32)


def place_kernel(write, count, color_ref, where_ref, *refs):
    step = pl.program_id(0)
    for number in range(count):

        @pl.when(step == number)
        def _(number=number):
            write(refs[number][...], refs[count:])


def place_blocks(write, color, where, pieces, out_shapes, out_specs):
    rows, columns = pieces[0].shape
    count = len(pieces)
    return pl.pallas_call(
        functools.partial(place_kernel, write, count),
        grid_spec=pltpu.PrefetchScalarGridSpec(
            num_scalar_prefetch=2,
            grid=(count,),
            in_specs=[pl.BlockSpec((rows, columns), lambda i, c, w: (0, 0))] * count,
            out_specs=out_specs,
        ),
        out_shape=[jax.ShapeDtypeStruct(shape, F32) for shape in out_shapes],
        cost_estimate=pl.CostEstimate(
            flops=0, bytes_accessed=6 * count * rows * columns, transcendentals=0
        ),
        name="place_blocks",
    )(color, where, *pieces)


class DpSum:
    def __init__(self, *grads, paired=False):
        self.grads = grads
        self.paired = paired
        self.count = bits_of("dp")
        pieces = (1 if paired else 2) << self.count
        self.axis = 0 if all(g.shape[0] % (8 * pieces) == 0 for g in grads) else 1
        self.sizes = [g.shape[self.axis] // pieces for g in grads]
        self.mine = lax.axis_index("dp")
        self.orders = [list(range(self.count)), list(range(self.count))[::-1]]
        self.level = 0
        if paired:
            self.state = [((grad,), self.sizes[:1], 0) for grad in grads]
        else:
            self.state = [(grads, self.sizes, color << self.count) for color in range(2)]
        self.held = None
        self.ready()

    def cut(self, color, side):
        grads, units, base = self.state[color]
        span = (1 << self.count) >> (self.level + 1)
        parts = []
        for grad, unit in zip(grads, units):
            at = (base + side * span) * unit
            parts.append(lax.dynamic_slice_in_dim(grad, at, span * unit, self.axis))
        if len(parts) == 1:
            return parts[0]
        if self.axis:
            return jnp.concatenate(parts, axis=0)
        parts = [p.reshape(span, unit, p.shape[1]) for p, unit in zip(parts, units)]
        joined = jnp.concatenate(parts, axis=1)
        return joined.reshape(-1, joined.shape[2])

    def side(self, color):
        return (self.mine >> self.orders[color][self.level]) & 1

    def ready(self):
        if self.level < self.count:
            self.out = [self.cut(color, 1 - self.side(color)) for color in range(2)]
        elif self.held is None:
            self.held = [[(self.state[color][0][0], 0)] for color in range(2)]

    def send(self):
        if self.level < self.count:
            self.got = [
                swap(self.out[color], "dp", self.orders[color][self.level])
                for color in range(2)
            ]
            return
        for color in range(2):
            bit = self.orders[color][2 * self.count - 1 - self.level]
            self.held[color] += [
                (swap(piece, "dp", bit), mask ^ (1 << bit)) for piece, mask in self.held[color]
            ]

    def arrive(self):
        if self.level < self.count:
            state = []
            for color in range(2):
                keep = self.cut(color, self.side(color))
                total = (keep.astype(F32) + self.got[color].astype(F32)).astype(BF16)
                whole = self.axis == 0 and not self.paired
                state.append(((total,), [sum(self.sizes) if whole else self.sizes[0]], 0))
            self.state = state
        self.level += 1
        self.ready()

    def moving(self):
        return self.out if self.held is None else self.held

    def result(self, write):
        pieces, colors, where = [], [], []
        for color in range(2):
            for piece, mask in self.held[color]:
                owner = self.mine ^ mask
                spot = 0 if self.paired else color
                for bit in self.orders[color]:
                    spot = spot * 2 + ((owner >> bit) & 1)
                pieces.append(piece)
                colors.append(color)
                where.append(spot)
        rows, columns = pieces[0].shape
        length, width = self.grads[0].shape
        if write is write_stacked:
            shapes = [(2, length, width)]
            blocks = [(1, rows, columns)]
        elif write is write_lanes:
            shapes = [(3, length, width // 3)]
            blocks = [(3, rows, columns // 3)]
        else:
            shapes = [g.shape for g in self.grads]
            blocks = [(rows * s[0] // sum(t[0] for t in shapes), columns) for s in shapes]
        lead = {write_stacked: lambda i, c: (c[i],), write_lanes: lambda i, c: (0,)}.get(
            write, lambda i, c: ()
        )

        def out_map(i, c, w):
            return lead(i, c) + ((w[i], 0) if self.axis == 0 else (0, w[i]))

        return place_blocks(
            write,
            jnp.array(colors, jnp.int32),
            jnp.stack(where).astype(jnp.int32),
            pieces,
            shapes,
            [pl.BlockSpec(block, out_map) for block in blocks],
        )


def fence(values, *sums):
    values, moving = lax.optimization_barrier((values, [item.moving() for item in sums]))
    for item, arrived in zip(sums, moving):
        if item.held is None:
            item.out = arrived
        else:
            item.held = arrived
    return values


def sum_small(values, name, bits=None):
    count = bits_of(name)
    if count is None:
        return lax.psum(values, name) if bits is None or 0 in bits else values
    for bit in range(count) if bits is None else bits:
        values = values + swap(values, name, bit)
    return values


def tail_kernel(x_ref, g_ref, c_ref, gain_ref, stat_ref, grad_ref, sums_ref):
    @pl.when(pl.program_id(0) == 0)
    def _():
        sums_ref[...] = jnp.zeros_like(sums_ref)
        sums_ref[2:3, :] = stat_ref[...]

    residual = x_ref[...].astype(F32)
    centered = residual - jnp.mean(residual, -1, keepdims=True)
    inv_std = lax.rsqrt(jnp.mean(centered * centered, -1, keepdims=True) + EPSILON)
    normalized = centered * inv_std
    grads = g_ref[...].astype(F32)
    sums_ref[0:1, :] += jnp.sum(grads * normalized, axis=0, keepdims=True)
    sums_ref[1:2, :] += jnp.sum(grads, axis=0, keepdims=True)
    scaled = grads * gain_ref[...]
    grad_ref[:, 0, :] = (
        inv_std
        * (
            scaled
            - jnp.mean(scaled, -1, keepdims=True)
            - normalized * jnp.mean(scaled * normalized, -1, keepdims=True)
        )
        + c_ref[...].astype(F32)
    )


def tail(layer_in, grad_normed, cot_here, norm_gain, stat_row):
    length, width = layer_in.shape
    rows = min(64, length)
    row_spec = pl.BlockSpec((rows, width), lambda i: (i, 0))
    one_spec = pl.BlockSpec((1, width), lambda i: (0, 0))
    return pl.pallas_call(
        tail_kernel,
        grid=(length // rows,),
        in_specs=[row_spec, row_spec, row_spec, one_spec, one_spec],
        out_specs=[
            pl.BlockSpec((rows, 1, width), lambda i: (i, 0, 0)),
            pl.BlockSpec((4, width), lambda i: (0, 0)),
        ],
        out_shape=[
            jax.ShapeDtypeStruct((length, 1, width), F32),
            jax.ShapeDtypeStruct((4, width), F32),
        ],
        name="tail",
    )(layer_in, grad_normed, cot_here, norm_gain.reshape(1, width), stat_row)


def back_products_kernel(p_ref, q_ref, g_ref, u_ref, w_ref, out_ref):
    turned = (((1,), (1,)), ((), ()))
    columns = q_ref.shape[2]
    total = jnp.dot(g_ref[...], w_ref[0], preferred_element_type=F32)
    total += jnp.dot(u_ref[...], w_ref[1], preferred_element_type=F32)
    for number in range(3):
        total += lax.dot_general(
            p_ref[:, number * columns : (number + 1) * columns],
            q_ref[number],
            turned,
            preferred_element_type=F32,
        )
    out_ref[...] = total.astype(BF16)


def back_products(grad_proj, w_qkv, grad_gate, grad_up, w_gate_up):
    length = grad_proj.shape[0]
    _, width, columns = w_qkv.shape
    hidden = grad_gate.shape[1]
    rows = min(256, length)
    return pl.pallas_call(
        back_products_kernel,
        grid=(length // rows,),
        in_specs=[
            pl.BlockSpec((rows, 3 * columns), lambda i: (i, 0)),
            pl.BlockSpec(w_qkv.shape, lambda i: (0, 0, 0)),
            pl.BlockSpec((rows, hidden), lambda i: (i, 0)),
            pl.BlockSpec((rows, hidden), lambda i: (i, 0)),
            pl.BlockSpec(w_gate_up.shape, lambda i: (0, 0, 0)),
        ],
        out_specs=pl.BlockSpec((rows, width), lambda i: (i, 0)),
        out_shape=jax.ShapeDtypeStruct((length, width), BF16),
        name="back_products",
    )(grad_proj, w_qkv, grad_gate, grad_up, w_gate_up)


def local(
    layer_in,
    segment_ids,
    valid_counts,
    norm_gain,
    norm_shift,
    w_qkv,
    b_qkv,
    w_out,
    w_gate_up,
    w_down,
    out_grad,
):
    local_len, row_count, model_width = layer_in.shape
    assert row_count == 1
    seq_len = local_len * lax.axis_size("mp")
    col_qkv = w_qkv.shape[2]
    ff_local = w_gate_up.shape[2]
    layer_in = layer_in[:, 0]
    position_here = lax.axis_index("mp") * local_len + jnp.arange(local_len, dtype=jnp.int32)
    valid_here = (position_here < valid_counts[0]).astype(F32)

    residual = layer_in.astype(F32)
    centered = residual - jnp.mean(residual, -1, keepdims=True)
    inv_std = lax.rsqrt(jnp.mean(centered * centered, -1, keepdims=True) + EPSILON)
    normalized = centered * inv_std
    normed = (normalized * norm_gain + norm_shift).astype(BF16)
    cot_here = jnp.where(valid_here[:, None] > 0, out_grad[:, 0], jnp.zeros((), BF16))
    gathered = lax.all_gather(normed, "mp", axis=0, tiled=True)
    cotangent = lax.all_gather(cot_here, "mp", axis=0, tiled=True)

    w_qkv = jnp.transpose(w_qkv, (1, 0, 2))
    w_gate_up = jnp.transpose(w_gate_up, (1, 2, 0))
    starts = starts_of(segment_ids)[0]
    tables = rotary_lanes(jnp.arange(seq_len, dtype=jnp.int32) - starts)
    start_blocks = starts.reshape(seq_len // BQ, 1, BQ)
    first = start_blocks[:, 0, 0] // BK
    gathered, tables, first, start_blocks = lax.optimization_barrier(
        (gathered, tables, first, start_blocks)
    )

    def product(left, right):
        return jnp.dot(left, right, preferred_element_type=F32).astype(BF16)

    def turned_product(left, right):
        return lax.dot_general(
            left, right, (((1,), (1,)), ((), ())), preferred_element_type=F32
        )

    def token_sum(left, right):
        return lax.dot_general(
            left, right, (((0,), (0,)), ((), ())), preferred_element_type=F32
        ).astype(BF16)

    def scattered(partial):
        return lax.psum_scatter(partial, "mp", scatter_dimension=0, tiled=True)

    gate = turned_product(gathered, w_gate_up[0])
    up = turned_product(gathered, w_gate_up[1])
    sigmoid_gate = jax.nn.sigmoid(gate)
    hidden = (gate * sigmoid_gate * up).astype(BF16)
    mlp_partial = product(hidden, w_down)
    mlp_sum = scattered(mlp_partial)
    gathered_next, mlp_partial = lax.optimization_barrier((gathered, mlp_partial))
    queries, key_rows, value_rows = project(gathered_next, w_qkv, b_qkv, tables)
    attended, lse = attend(first, queries, key_rows, value_rows, start_blocks)
    attn_partial = product(attended, w_out)
    attn_sum = scattered(attn_partial)

    cotangent, attn_partial = lax.optimization_barrier((cotangent, attn_partial))
    grad_hid = turned_product(cotangent, w_down).astype(BF16).astype(F32)
    grad_gate = (
        grad_hid * up * sigmoid_gate * (1.0 + gate * (1.0 - sigmoid_gate))
    ).astype(BF16)
    grad_up = (grad_hid * gate * sigmoid_gate).astype(BF16)
    sum_down = DpSum(token_sum(hidden, cotangent), token_sum(attended, cotangent))
    gathered_next = fence(gathered, sum_down)
    sum_down.send()
    sum_gate_up = DpSum(
        token_sum(grad_gate, gathered_next), token_sum(grad_up, gathered_next), paired=True
    )
    sum_down.arrive()
    cotangent = fence(cotangent, sum_gate_up, sum_down)
    grad_att = turned_product(cotangent, w_out).astype(BF16)
    sum_gate_up.send()
    sum_down.send()
    grad_proj = attend_back(
        first, queries, key_rows, value_rows, grad_att, attended, lse, start_blocks, tables
    )
    sum_gate_up.arrive()
    sum_down.arrive()
    grad_proj, mlp_sum = fence((grad_proj, mlp_sum), sum_gate_up, sum_down)
    sum_gate_up.send()
    sum_down.send()
    normed_partial = back_products(grad_proj, w_qkv, grad_gate, grad_up, w_gate_up)
    sum_gate_up.arrive()
    sum_down.arrive()
    grad_proj, normed_partial = fence((grad_proj, normed_partial), sum_gate_up, sum_down)
    while sum_down.level < 2 * sum_down.count:
        sum_down.send()
        sum_down.arrive()
    sum_qkv = DpSum(fence(token_sum(gathered, grad_proj), sum_down))
    bias_sums = jnp.sum(grad_proj, axis=0, dtype=F32).reshape(-1, 128)
    sum_qkv.send()
    sum_qkv.arrive()
    normed_partial, attn_sum, bias_sums = fence(
        (normed_partial, attn_sum, bias_sums), sum_gate_up, sum_qkv
    )
    grad_normed = scattered(normed_partial)
    sum_gate_up.send()
    sum_qkv.send()
    bias_sums = sum_small(bias_sums, "dp", [0])
    mlp_part = mlp_sum.astype(F32)
    attn_part = attn_sum.astype(F32)
    layer_out = (residual + attn_part + mlp_part).astype(BF16)
    statistics = jnp.stack(
        [
            jnp.sum(valid_here * jnp.sum(residual * residual, -1)),
            jnp.sum(valid_here * jnp.sum(attn_part * attn_part, -1)),
            jnp.sum(valid_here * jnp.sum(mlp_part * mlp_part, -1)),
            jnp.sum(valid_here),
        ]
    )
    stat_row = jnp.pad(statistics, (0, model_width - 4)).reshape(1, model_width)
    sum_gate_up.arrive()
    sum_qkv.arrive()
    bias_sums, layer_out, stat_row = fence(
        (bias_sums, layer_out, stat_row), sum_gate_up, sum_qkv
    )
    sum_gate_up.send()
    sum_qkv.send()
    bias_sums = sum_small(bias_sums, "dp", range(1, sum_qkv.count))
    down_sums = sum_down.result(write_rows)
    sum_gate_up.arrive()
    sum_qkv.arrive()
    down_sums, bias_sums = fence((down_sums, bias_sums), sum_gate_up, sum_qkv)
    for item in (sum_gate_up, sum_qkv):
        while item.level < 2 * item.count:
            item.send()
            item.arrive()
    (grad_w_gate_up,) = sum_gate_up.result(write_stacked)
    grad_normed, grad_w_gate_up = fence((grad_normed, grad_w_gate_up), sum_qkv)
    (grad_w_qkv,) = sum_qkv.result(write_lanes)
    grad_w_down, grad_w_out = down_sums
    input_grad, small = tail(layer_in, grad_normed, cot_here, norm_gain, stat_row)
    small = sum_small(sum_small(small, "mp"), "dp")
    totals = small[2]
    return (
        layer_out[:, None],
        input_grad,
        small[0],
        small[1],
        jnp.transpose(grad_w_qkv, (1, 0, 2)),
        bias_sums.reshape(3, col_qkv),
        grad_w_out,
        jnp.transpose(grad_w_gate_up, (2, 0, 1)),
        grad_w_down,
        jnp.sqrt(totals[:3] / (totals[3] * model_width)),
    )


def solution(mesh):
    placed = (
        P("mp", "dp", None),
        P("dp", None),
        P("dp"),
        P(),
        P(),
        P(None, None, "mp"),
        P(None, "mp"),
        P("mp", None),
        P(None, None, "mp"),
        P("mp", None),
        P("mp", "dp", None),
    )
    return jax.shard_map(
        local,
        mesh=mesh,
        in_specs=placed,
        out_specs=(
            P("mp", "dp", None),
            P("mp", "dp", None),
            P(),
            P(),
            P(None, None, "mp"),
            P(None, "mp"),
            P("mp", None),
            P(None, None, "mp"),
            P("mp", None),
            P(),
        ),
        check_vma=False,
    )
```

profile of v0, /device:TPU:0, one launch (start us, length us, event | category | flops | bytes accessed | tf_op | source)
XLA Modules:
  0.0 502.9 jit_solution(14202585296829917326)
XLA Ops:
  7.2 2.3 fusion.16
  11.2 2.7 fusion.12
  15.2 2.3 bitcast_select_fusion.c_ref
  19.6 5.9 %fusion.19 = (f32[2048,128]{1,0:T(8,128)}, f32[2048,128]{1,0:T(8,128)}, f32[2048,128]{1,0:T(8,128)}) fusion(f32[128]{0:T(128)S(1)} %compare_select_fusion.5, f32[2048]{0:T(1024)S(1)} %fusion.23, pred[128]{0:T(512)(128)(4,1)S(1)} %get-tuple-element.308, pred[128]{0:T(512)(128)(4,1)S(1)} %get-tuple-element.309), kind=kLoop, calls=%fused_computation.50 | loop fusion | flops 1048576 | bytes 3154688 | tf_op jit(solution)/shard_map/jit(_where)/select_n | solution.py:41
  25.5 73.4 %all-gather.3.cloned.1.call-done.x_ref = bf16[2048,2048]{1,0:T(8,128)(2,1)} async-done(((bf16[256,2048]{1,0:T(8,128)(2,1)}), bf16[2048,2048]{1,0:T(8,128)(2,1)}) %all-gather.3.cloned.1.call-update) | async-done | bytes 8388624 | tf_op jit(solution)/shard_map/all_gather | solution.py:641
  98.9 10.1 %fusion.6 = f32[2048,704]{1,0:T(8,128)S(1)} fusion(bf16[2048,2048]{1,0:T(8,128)(2,1)} %all-gather.3.cloned.1.call-done.x_ref, bf16[2,704,2048]{2,1,0:T(8,128)(2,1)} %bitcast.113), kind=kOutput, calls=%fused_computation.24 | convolution fusion | flops 5905580032 | bytes 17039360 | tf_op jit(solution)/shard_map/dot_general | solution.py:658
  109.0 13.1 %multiply_convert_fusion = (bf16[2048,704]{1,0:T(8,128)(2,1)S(1)}, f32[2048,704]{1,0:T(8,128)}) fusion(f32[2048,704]{1,0:T(8,128)S(1)} %fusion.6, bf16[2048,2048]{1,0:T(8,128)(2,1)S(1)} %copy-done.28, bf16[2,704,2048]{2,1,0:T(8,128)(2,1)} %bitcast.114), kind=kOutput, calls=%fused_computation.10 | convolution fusion | flops 5914230784 | bytes 25690112 | tf_op jit(solution)/shard_map/dot_general | solution.py:658
  123.8 8.9 %convolution_convert_fusion.1 = bf16[2048,2048]{1,0:T(8,128)(2,1)} fusion(bf16[2048,704]{1,0:T(8,128)(2,1)S(1)} %get-tuple-element.306, bf16[704,2048]{1,0:T(8,128)(2,1)S(1)} %copy-done), kind=kOutput, calls=%fused_computation.3 | convolution fusion | flops 5909774336 | bytes 14155776 | tf_op jit(solution)/shard_map/dot_general | solution.py:655
  133.2 13.2 %project.1 = (bf16[2048,256]{1,0:T(8,128)(2,1)}, bf16[2048,256]{1,0:T(8,128)(2,1)}, bf16[2048,256]{1,0:T(8,128)(2,1)}) custom-call(bf16[2048,2048]{1,0:T(8,128)(2,1)} %all-gather.3.cloned.1.call-done.x_ref, bf16[3,2048,256]{2,1,0:T(8,128)(2,1)} %bitcast.116, bf16[3,256]{1,0:T(4,128)(2,1)} %b_ref.1, f32[2048,128]{1,0:T(8,128)} %get-tuple-element.146.cos_ref, ...), custom_call_target="tpu_custom_call" | custom-call | flops 6442450944 | bytes 14680064 | tf_op jit(solution)/shard_map/project/pallas_call | solution.py:78
  146.4 29.2 %attend.1 = (bf16[2048,256]{1,0:T(8,128)(2,1)}, f32[16,1,512]{2,1,0:T(1,128)}) custom-call(s32[16]{0:T(128)} %and_select_fusion.first_ref, bf16[2048,256]{1,0:T(8,128)(2,1)} %get-tuple-element.149.q_ref, bf16[2048,256]{1,0:T(8,128)(2,1)} %get-tuple-element.150.k_ref, bf16[2048,256]{1,0:T(8,128)(2,1)} %get-tuple-element.151.v_ref, s32[16,1,128]{2,1,0:T(1,128)} %copy-done.25), custom_call_target="tpu_custom_call" | custom-call | flops 8589934592 | bytes 4194304 | tf_op jit(solution)/shard_map/attend/pallas_call | solution.py:181
  175.6 7.3 %convolution_convert_fusion = bf16[2048,2048]{1,0:T(8,128)(2,1)} fusion(bf16[2048,256]{1,0:T(8,128)(2,1)} %get-tuple-element.153.o_ref, bf16[256,2048]{1,0:T(8,128)(2,1)} %param.21), kind=kOutput, calls=%fused_computation.2 | convolution fusion | flops 2151677952 | bytes 10485760 | tf_op jit(solution)/shard_map/dot_general | solution.py:655
  182.9 7.2 %convolution_convert_fusion.8 = bf16[256,2048]{1,0:T(8,128)(2,1)} fusion(bf16[2048,256]{1,0:T(8,128)(2,1)} %get-tuple-element.153.o_ref, bf16[2048,2048]{1,0:T(8,128)(2,1)} %all-gather.5.cloned.1.call-done), kind=kOutput, calls=%fused_computation.31 | convolution fusion | flops 2148007936 | bytes 10485760 | tf_op jit(solution)/shard_map/dot_general | solution.py:663
  191.1 7.6 %convolution_convert_fusion.6 = bf16[704,2048]{1,0:T(8,128)(2,1)} fusion(bf16[2048,704]{1,0:T(8,128)(2,1)S(1)} %copy-done.30, bf16[2048,2048]{1,0:T(8,128)(2,1)S(1)} %copy-done.3), kind=kOutput, calls=%fused_computation.20 | convolution fusion | flops 5907021824 | bytes 14155776 | tf_op jit(solution)/shard_map/dot_general | solution.py:663
  198.7 13.2 %fusion.4 = (bf16[2048,704]{1,0:T(8,128)(2,1)}, bf16[2048,704]{1,0:T(8,128)(2,1)}) fusion(f32[2048,704]{1,0:T(8,128)} %copy-done.31, f32[2048,704]{1,0:T(8,128)} %get-tuple-element.307, bf16[2048,2048]{1,0:T(8,128)(2,1)S(1)} %copy-done.3, bf16[704,2048]{1,0:T(8,128)(2,1)S(1)} %copy-done), kind=kOutput, calls=%fused_computation.8 | convolution fusion | flops 5927206912 | bytes 28573696 | tf_op jit(solution)/shard_map/dot_general | solution.py:658
  213.2 2.1 constant_dynamic-slice_fusion.8
  217.2 8.9 %convolution_convert_fusion.4 = bf16[704,2048]{1,0:T(8,128)(2,1)S(1)} fusion(bf16[2048,704]{1,0:T(8,128)(2,1)S(1)} %copy-done.7, bf16[2048,2048]{1,0:T(8,128)(2,1)} %all-gather.3.cloned.1.call-done.x_ref), kind=kOutput, calls=%fused_computation.18 | convolution fusion | flops 5907021824 | bytes 14155776 | tf_op jit(solution)/shard_map/dot_general | solution.py:663
  226.1 9.7 %convolution_convert_fusion.5 = bf16[704,2048]{1,0:T(8,128)(2,1)S(1)} fusion(bf16[2048,704]{1,0:T(8,128)(2,1)S(1)} %copy-done.8, bf16[2048,2048]{1,0:T(8,128)(2,1)} %all-gather.3.cloned.1.call-done.x_ref), kind=kOutput, calls=%fused_computation.19 | convolution fusion | flops 5907021824 | bytes 14155776 | tf_op jit(solution)/shard_map/dot_general | solution.py:663
  243.7 2.0 collective-permute-start.3
  245.7 3.4 convolution_convert_fusion.7.do_ref
  249.1 40.1 %attend_back.1.p_ref = bf16[2048,768]{1,0:T(8,128)(2,1)} custom-call(s32[16]{0:T(128)} %and_select_fusion.first_ref, bf16[2048,256]{1,0:T(8,128)(2,1)} %get-tuple-element.149.q_ref, bf16[2048,256]{1,0:T(8,128)(2,1)} %get-tuple-element.150.k_ref, bf16[2048,256]{1,0:T(8,128)(2,1)} %get-tuple-element.151.v_ref, ...), custom_call_target="tpu_custom_call" | custom-call | flops 21474836480 | bytes 8388608 | tf_op jit(solution)/shard_map/attend_back/pallas_call | solution.py:312
  290.6 2.1 add_convert_fusion.6.refs_4_
  292.7 2.0 add_convert_fusion.1
  298.5 2.0 collective-permute-start.8
  300.5 2.0 collective-permute-start.9
  302.5 26.3 %back_products.1 = bf16[2048,2048]{1,0:T(8,128)(2,1)} custom-call(bf16[2048,768]{1,0:T(8,128)(2,1)} %attend_back.1.p_ref, bf16[3,2048,256]{2,1,0:T(8,128)(2,1)} %bitcast.117, bf16[2048,704]{1,0:T(8,128)(2,1)} %get-tuple-element.285.g_ref, bf16[2048,704]{1,0:T(8,128)(2,1)} %get-tuple-element.284.u_ref, bf16[2,704,2048]{2,1,0:T(8,128)(2,1)} %bitcast.115), custom_call_target="tpu_custom_call" | custom-call | tf_op jit(solution)/shard_map/back_products/pallas_call | solution.py:597
  328.8 2.2 add_convert_fusion.5.refs_0_
  331.0 2.3 add_convert_fusion.4.refs_4_
  333.4 2.0 collective-permute-start.11
  335.4 2.0 collective-permute-start.13
  337.4 11.5 %convolution_convert_fusion.3 = bf16[2048,768]{1,0:T(8,128)(2,1)} fusion(bf16[2048,2048]{1,0:T(8,128)(2,1)} %all-gather.3.cloned.1.call-done.x_ref, bf16[2048,768]{1,0:T(8,128)(2,1)} %attend_back.1.p_ref), kind=kOutput, calls=%fused_computation.17 | convolution fusion | flops 6444023808 | bytes 14680064 | tf_op jit(solution)/shard_map/dot_general | solution.py:663
  348.9 5.6 %collective-permute-done.11.refs_3_ = bf16[120,2048]{1,0:T(8,128)(2,1)S(1)} collective-permute-done((bf16[120,2048]{1,0:T(8,128)(2,1)}, bf16[120,2048]{1,0:T(8,128)(2,1)S(1)}, u32[]{:S(2)}, u32[]{:S(2)}) %collective-permute-start.11) | collective-permute-done | bytes 491552 | tf_op jit(solution)/shard_map/ppermute | solution.py:354
  358.4 2.5 convert_reduce_fusion
  360.9 12.8 %collective-permute-done.15 = bf16[512,768]{1,0:T(8,128)(2,1)S(1)} collective-permute-done((bf16[512,768]{1,0:T(8,128)(2,1)S(1)}, bf16[512,768]{1,0:T(8,128)(2,1)S(1)}, u32[]{:S(2)}, u32[]{:S(2)}) %collective-permute-start.15) | collective-permute-done | bytes 786464 | tf_op jit(solution)/shard_map/ppermute | solution.py:354
  374.2 2.0 add_convert_fusion.2
  381.9 3.0 fusion.13
  385.5 3.3 select_maximum_fusion
  392.5 9.9 %collective-permute-done.17.refs_1_ = bf16[176,2048]{1,0:T(8,128)(2,1)} collective-permute-done((bf16[176,2048]{1,0:T(8,128)(2,1)}, bf16[176,2048]{1,0:T(8,128)(2,1)}, u32[]{:S(2)}, u32[]{:S(2)}) %collective-permute-start.17) | collective-permute-done | bytes 720928 | tf_op jit(solution)/shard_map/ppermute | solution.py:354
  407.2 7.3 %collective-permute-done.21 = f32[6,128]{1,0:T(8,128)S(1)} collective-permute-done((f32[6,128]{1,0:T(8,128)S(1)}, f32[6,128]{1,0:T(8,128)S(1)}, u32[]{:S(2)}, u32[]{:S(2)}) %collective-permute-start.21) | collective-permute-done | bytes 3104 | tf_op jit(solution)/shard_map/ppermute | solution.py:354
  417.9 7.4 %place_blocks.3 = (f32[704,2048]{1,0:T(8,128)}, f32[256,2048]{1,0:T(8,128)}) custom-call(s32[8]{0:T(128)} %constant.128.clone.color_ref, s32[8]{0:T(128)} %stack.109.where_ref, bf16[120,2048]{1,0:T(8,128)(2,1)} %copy-done.13, bf16[120,2048]{1,0:T(8,128)(2,1)} %collective-permute-done.8.refs_1_, bf16[120,2048]{1,0:T(8,128)(2,1)} %copy-done.20, ...), custom_call_target="tpu_custom_call" | custom-call | bytes 11796480 | tf_op jit(solution)/shard_map/place_blocks/pallas_call | solution.py:387
  425.3 18.8 %collective-permute-done.27.refs_5_ = bf16[256,768]{1,0:T(8,128)(2,1)} collective-permute-done((bf16[256,768]{1,0:T(8,128)(2,1)S(1)}, bf16[256,768]{1,0:T(8,128)(2,1)}, u32[]{:S(2)}, u32[]{:S(2)}) %collective-permute-start.27) | collective-permute-done | bytes 393248 | tf_op jit(solution)/shard_map/ppermute | solution.py:354
  444.2 2.0 collective-permute-start.28
  448.9 8.7 %place_blocks.4 = f32[2,704,2048]{2,1,0:T(8,128)} custom-call(s32[8]{0:T(128)} %constant.128.clone.color_ref, s32[8]{0:T(128)} %stack.118.where_ref, bf16[176,2048]{1,0:T(8,128)(2,1)} %add_convert_fusion.5.refs_0_, bf16[176,2048]{1,0:T(8,128)(2,1)} %collective-permute-done.17.refs_1_, bf16[176,2048]{1,0:T(8,128)(2,1)} %copy-done.17, ...), custom_call_target="tpu_custom_call" | custom-call | bytes 17301504 | tf_op jit(solution)/shard_map/place_blocks/pallas_call | solution.py:387
  458.4 5.5 %reduce-scatter.8.cloned.1.call-done.g_ref = bf16[256,2048]{1,0:T(8,128)(2,1)} async-done(((bf16[2048,2048]{1,0:T(8,128)(2,1)}), bf16[256,2048]{1,0:T(8,128)(2,1)}) %reduce-scatter.8.cloned.1.call-update) | async-done | bytes 1048592 | tf_op jit(solution)/shard_map/reduce_scatter | solution.py:668
  463.9 5.1 %tail.1 = (f32[256,1,2048]{2,1,0:T(1,128)}, f32[4,2048]{1,0:T(4,128)}) custom-call(bf16[256,2048]{1,0:T(8,128)(2,1)} %bitcast.108, bf16[256,2048]{1,0:T(8,128)(2,1)} %reduce-scatter.8.cloned.1.call-done.g_ref, bf16[256,2048]{1,0:T(8,128)(2,1)} %bitcast_select_fusion.c_ref, f32[1,2048]{1,0:T(1,128)} %bitcast.130, f32[1,2048]{1,0:T(1,128)} %bitcast.131), custom_call_target="tpu_custom_call" | custom-call | tf_op jit(solution)/shard_map/tail/pallas_call | solution.py:561
  471.3 3.9 collective-permute-done.33
  475.6 4.4 collective-permute-done.34
  481.6 2.5 collective-permute-done.35
  486.8 6.7 %place_blocks.5 = f32[3,2048,256]{2,1,0:T(8,128)} custom-call(s32[8]{0:T(128)} %constant.128.clone.color_ref, s32[8]{0:T(128)} %stack.127.where_ref, bf16[256,768]{1,0:T(8,128)(2,1)} %copy-done.14, bf16[256,768]{1,0:T(8,128)(2,1)} %copy-done.23, bf16[256,768]{1,0:T(8,128)(2,1)} %collective-permute-done.28.refs_2_, ...), custom_call_target="tpu_custom_call" | custom-call | bytes 9437184 | tf_op jit(solution)/shard_map/place_blocks/pallas_call | solution.py:387
  (195 shorter events, 58.4 us)
Async XLA Ops:
  7.2 116.6 %copy-start = (bf16[704,2048]{1,0:T(8,128)(2,1)S(1)}, bf16[704,2048]{1,0:T(8,128)(2,1)}, u32[]{:S(2)}) copy-start(bf16[704,2048]{1,0:T(8,128)(2,1)} %param.23) | copy-start | bytes 8650756
  7.2 91.7 %all-gather.3.cloned.1.call-start = ((), (), s32[]{:S(2)}) async-start(), calls=%async_computation.3 | async-start | bytes 9437184 | tf_op jit(solution)/shard_map/all_gather | solution.py:641
  13.9 169.0 %all-gather.5.cloned.1.call-start = ((), (), s32[]{:S(2)}) async-start(), calls=%async_computation.4 | async-start | bytes 9437184 | tf_op jit(solution)/shard_map/all_gather | solution.py:642
  17.5 281.0 %reduce-scatter.4.cloned.1.call-start = ((), (), s32[]{:S(2)}) async-start(), calls=%async_computation.5 | async-start | bytes 9437184 | tf_op jit(solution)/shard_map/reduce_scatter | solution.py:668
  18.6 90.4 %copy-start.25 = (s32[16,1,128]{2,1,0:T(1,128)}, s32[16,1,128]{2,1,0:T(1,128)S(1)}, u32[]{:S(2)}) copy-start(s32[16,1,128]{2,1,0:T(1,128)S(1)} %broadcast_maximum_fusion.start_ref) | copy-start | bytes 24580
  132.7 244.3 %reduce-scatter.6.cloned.1.call-start = ((), (), s32[]{:S(2)}) async-start(), calls=%async_computation.6 | async-start | bytes 9437184 | tf_op jit(solution)/shard_map/reduce_scatter | solution.py:668
  211.9 252.0 %reduce-scatter.8.cloned.1.call-start = ((), (), s32[]{:S(2)}) async-start(), calls=%async_computation.7 | async-start | bytes 9437184 | tf_op jit(solution)/shard_map/reduce_scatter | solution.py:668
  215.5 23.9 %collective-permute-start = (bf16[240,2048]{1,0:T(8,128)(2,1)S(1)}, bf16[240,2048]{1,0:T(8,128)(2,1)S(1)}, u32[]{:S(2)}, u32[]{:S(2)}) collective-permute-start(bf16[240,2048]{1,0:T(8,128)(2,1)S(1)} %bitcast.128), channel_id=1, source_target_pairs={{0,8},{8,0},{16,24},{24,16},{1,9},{9,1},{17,25},{25,17},{2,10},{10... | collective-permute-start | bytes 2949128 | tf_op jit(solution)/shard_map/ppermute | solution.py:354
  215.6 24.4 %collective-permute-start.1 = (bf16[240,2048]{1,0:T(8,128)(2,1)S(1)}, bf16[240,2048]{1,0:T(8,128)(2,1)S(1)}, u32[]{:S(2)}, u32[]{:S(2)}) collective-permute-start(bf16[240,2048]{1,0:T(8,128)(2,1)S(1)} %bitcast.127), channel_id=1, source_target_pairs={{0,16},{8,24},{16,0},{24,8},{1,17},{9,25},{17,1},{25,9},{2,18},{10... | collective-permute-start | bytes 2949128 | tf_op jit(solution)/shard_map/ppermute | solution.py:354
  241.6 47.6 %collective-permute-start.4 = (bf16[120,2048]{1,0:T(8,128)(2,1)S(1)}, bf16[120,2048]{1,0:T(8,128)(2,1)}, u32[]{:S(2)}, u32[]{:S(2)}) collective-permute-start(bf16[120,2048]{1,0:T(8,128)(2,1)S(1)} %constant_dynamic-slice_fusion.9), channel_id=1, source_target_pairs={{0,16},{8,24},{16,0},{24,8},{1,17},{9,25},{17,1},{25,9},{2,18},{10... | collective-permute-start | bytes 1474568 | tf_op jit(solution)/shard_map/ppermute | solution.py:354
  241.6 48.9 %collective-permute-start.5 = (bf16[120,2048]{1,0:T(8,128)(2,1)}, bf16[120,2048]{1,0:T(8,128)(2,1)}, u32[]{:S(2)}, u32[]{:S(2)}) collective-permute-start(bf16[120,2048]{1,0:T(8,128)(2,1)} %constant_dynamic-slice_fusion.6), channel_id=1, source_target_pairs={{0,8},{8,0},{16,24},{24,16},{1,9},{9,1},{17,25},{25,17},{2,10},{10... | collective-permute-start | bytes 1474568 | tf_op jit(solution)/shard_map/ppermute | solution.py:354
  243.4 49.2 %collective-permute-start.2 = (bf16[352,2048]{1,0:T(8,128)(2,1)}, bf16[352,2048]{1,0:T(8,128)(2,1)}, u32[]{:S(2)}, u32[]{:S(2)}) collective-permute-start(bf16[352,2048]{1,0:T(8,128)(2,1)} %constant_dynamic-slice_fusion.13), channel_id=1, source_target_pairs={{0,8},{8,0},{16,24},{24,16},{1,9},{9,1},{17,25},{25,17},{2,10},{10... | collective-permute-start | bytes 4325384 | tf_op jit(solution)/shard_map/ppermute | solution.py:354
  243.7 52.0 %collective-permute-start.3 = (bf16[352,2048]{1,0:T(8,128)(2,1)}, bf16[352,2048]{1,0:T(8,128)(2,1)}, u32[]{:S(2)}, u32[]{:S(2)}) collective-permute-start(bf16[352,2048]{1,0:T(8,128)(2,1)} %constant_dynamic-slice_fusion.12), channel_id=1, source_target_pairs={{0,16},{8,24},{16,0},{24,8},{1,17},{9,25},{17,1},{25,9},{2,18},{10... | collective-permute-start | bytes 4325384 | tf_op jit(solution)/shard_map/ppermute | solution.py:354
  249.1 40.1 %copy-start.6 = (bf16[240,2048]{1,0:T(8,128)(2,1)S(1)}, bf16[240,2048]{1,0:T(8,128)(2,1)}, u32[]{:S(2)}) copy-start(bf16[240,2048]{1,0:T(8,128)(2,1)} %copy-done.5) | copy-start | bytes 2949124
  290.5 42.7 %copy-start.13 = (bf16[120,2048]{1,0:T(8,128)(2,1)}, bf16[120,2048]{1,0:T(8,128)(2,1)S(1)}, u32[]{:S(2)}) copy-start(bf16[120,2048]{1,0:T(8,128)(2,1)S(1)} %add_convert_fusion.7.refs_0_) | copy-start | bytes 1474564
  298.5 30.3 %collective-permute-start.6 = (bf16[176,2048]{1,0:T(8,128)(2,1)}, bf16[176,2048]{1,0:T(8,128)(2,1)}, u32[]{:S(2)}, u32[]{:S(2)}) collective-permute-start(bf16[176,2048]{1,0:T(8,128)(2,1)} %constant_dynamic-slice_fusion.5), channel_id=1, source_target_pairs={{0,16},{8,24},{16,0},{24,8},{1,17},{9,25},{17,1},{25,9},{2,18},{10... | collective-permute-start | bytes 2162696 | tf_op jit(solution)/shard_map/ppermute | solution.py:354
  298.5 32.5 %collective-permute-start.7 = (bf16[176,2048]{1,0:T(8,128)(2,1)}, bf16[176,2048]{1,0:T(8,128)(2,1)}, u32[]{:S(2)}, u32[]{:S(2)}) collective-permute-start(bf16[176,2048]{1,0:T(8,128)(2,1)} %constant_dynamic-slice_fusion.4), channel_id=1, source_target_pairs={{0,8},{8,0},{16,24},{24,16},{1,9},{9,1},{17,25},{25,17},{2,10},{10... | collective-permute-start | bytes 2162696 | tf_op jit(solution)/shard_map/ppermute | solution.py:354
  298.5 34.8 %collective-permute-start.8 = (bf16[120,2048]{1,0:T(8,128)(2,1)S(1)}, bf16[120,2048]{1,0:T(8,128)(2,1)}, u32[]{:S(2)}, u32[]{:S(2)}) collective-permute-start(bf16[120,2048]{1,0:T(8,128)(2,1)S(1)} %add_convert_fusion.7.refs_0_), channel_id=1, source_target_pairs={{0,16},{8,24},{16,0},{24,8},{1,17},{9,25},{17,1},{25,9},{2,18},{10... | collective-permute-start | bytes 1474568 | tf_op jit(solution)/shard_map/ppermute | solution.py:354
  300.5 32.7 %collective-permute-start.9 = (bf16[120,2048]{1,0:T(8,128)(2,1)}, bf16[120,2048]{1,0:T(8,128)(2,1)}, u32[]{:S(2)}, u32[]{:S(2)}) collective-permute-start(bf16[120,2048]{1,0:T(8,128)(2,1)} %add_convert_fusion.6.refs_4_), channel_id=1, source_target_pairs={{0,8},{8,0},{16,24},{24,16},{1,9},{9,1},{17,25},{25,17},{2,10},{10... | collective-permute-start | bytes 1474568 | tf_op jit(solution)/shard_map/ppermute | solution.py:354
  333.3 15.6 %collective-permute-start.10 = (bf16[120,2048]{1,0:T(8,128)(2,1)S(1)}, bf16[120,2048]{1,0:T(8,128)(2,1)S(1)}, u32[]{:S(2)}, u32[]{:S(2)}) collective-permute-start(bf16[120,2048]{1,0:T(8,128)(2,1)S(1)} %add_convert_fusion.7.refs_0_), channel_id=1, source_target_pairs={{0,8},{8,0},{16,24},{24,16},{1,9},{9,1},{17,25},{25,17},{2,10},{10... | collective-permute-start | bytes 1474568 | tf_op jit(solution)/shard_map/ppermute | solution.py:354
  333.4 21.1 %collective-permute-start.11 = (bf16[120,2048]{1,0:T(8,128)(2,1)}, bf16[120,2048]{1,0:T(8,128)(2,1)S(1)}, u32[]{:S(2)}, u32[]{:S(2)}) collective-permute-start(bf16[120,2048]{1,0:T(8,128)(2,1)} %collective-permute-done.8.refs_1_), channel_id=1, source_target_pairs={{0,8},{8,0},{16,24},{24,16},{1,9},{9,1},{17,25},{25,17},{2,10},{10... | collective-permute-start | bytes 1474568 | tf_op jit(solution)/shard_map/ppermute | solution.py:354
  335.4 19.1 %collective-permute-start.12 = (bf16[120,2048]{1,0:T(8,128)(2,1)}, bf16[120,2048]{1,0:T(8,128)(2,1)S(1)}, u32[]{:S(2)}, u32[]{:S(2)}) collective-permute-start(bf16[120,2048]{1,0:T(8,128)(2,1)} %add_convert_fusion.6.refs_4_), channel_id=1, source_target_pairs={{0,16},{8,24},{16,0},{24,8},{1,17},{9,25},{17,1},{25,9},{2,18},{10... | collective-permute-start | bytes 1474568 | tf_op jit(solution)/shard_map/ppermute | solution.py:354
  335.4 20.8 %collective-permute-start.13 = (bf16[120,2048]{1,0:T(8,128)(2,1)}, bf16[120,2048]{1,0:T(8,128)(2,1)}, u32[]{:S(2)}, u32[]{:S(2)}) collective-permute-start(bf16[120,2048]{1,0:T(8,128)(2,1)} %collective-permute-done.9.refs_5_), channel_id=1, source_target_pairs={{0,16},{8,24},{16,0},{24,8},{1,17},{9,25},{17,1},{25,9},{2,18},{10... | collective-permute-start | bytes 1474568 | tf_op jit(solution)/shard_map/ppermute | solution.py:354
  357.7 16.0 %collective-permute-start.15 = (bf16[512,768]{1,0:T(8,128)(2,1)S(1)}, bf16[512,768]{1,0:T(8,128)(2,1)S(1)}, u32[]{:S(2)}, u32[]{:S(2)}) collective-permute-start(bf16[512,768]{1,0:T(8,128)(2,1)S(1)} %get-tuple-element.288), channel_id=1, source_target_pairs={{0,16},{8,24},{16,0},{24,8},{1,17},{9,25},{17,1},{25,9},{2,18},{10... | collective-permute-start | bytes 2359304 | tf_op jit(solution)/shard_map/ppermute | solution.py:354
  358.1 16.1 %collective-permute-start.14 = (bf16[512,768]{1,0:T(8,128)(2,1)S(1)}, bf16[512,768]{1,0:T(8,128)(2,1)}, u32[]{:S(2)}, u32[]{:S(2)}) collective-permute-start(bf16[512,768]{1,0:T(8,128)(2,1)S(1)} %get-tuple-element.289), channel_id=1, source_target_pairs={{0,8},{8,0},{16,24},{24,16},{1,9},{9,1},{17,25},{25,17},{2,10},{10... | collective-permute-start | bytes 2359304 | tf_op jit(solution)/shard_map/ppermute | solution.py:354
  377.0 11.7 %collective-permute-start.16 = (f32[6,128]{1,0:T(8,128)S(1)}, f32[6,128]{1,0:T(8,128)S(1)}, u32[]{:S(2)}, u32[]{:S(2)}) collective-permute-start(f32[6,128]{1,0:T(8,128)S(1)} %bitcast.133), channel_id=1, source_target_pairs={{0,8},{8,0},{16,24},{24,16},{1,9},{9,1},{17,25},{25,17},{2,10},{10... | collective-permute-start | bytes 9224 | tf_op jit(solution)/shard_map/ppermute | solution.py:354
  377.8 12.1 %collective-permute-start.19 = (bf16[256,768]{1,0:T(8,128)(2,1)S(1)}, bf16[256,768]{1,0:T(8,128)(2,1)}, u32[]{:S(2)}, u32[]{:S(2)}) collective-permute-start(bf16[256,768]{1,0:T(8,128)(2,1)S(1)} %constant_dynamic-slice_fusion.2), channel_id=1, source_target_pairs={{0,16},{8,24},{16,0},{24,8},{1,17},{9,25},{17,1},{25,9},{2,18},{10... | collective-permute-start | bytes 1179656 | tf_op jit(solution)/shard_map/ppermute | solution.py:354
  379.1 12.3 %collective-permute-start.20 = (bf16[256,768]{1,0:T(8,128)(2,1)}, bf16[256,768]{1,0:T(8,128)(2,1)}, u32[]{:S(2)}, u32[]{:S(2)}) collective-permute-start(bf16[256,768]{1,0:T(8,128)(2,1)} %constant_dynamic-slice_fusion), channel_id=1, source_target_pairs={{0,8},{8,0},{16,24},{24,16},{1,9},{9,1},{17,25},{25,17},{2,10},{10... | collective-permute-start | bytes 1179656 | tf_op jit(solution)/shard_map/ppermute | solution.py:354
  380.6 21.8 %collective-permute-start.17 = (bf16[176,2048]{1,0:T(8,128)(2,1)}, bf16[176,2048]{1,0:T(8,128)(2,1)}, u32[]{:S(2)}, u32[]{:S(2)}) collective-permute-start(bf16[176,2048]{1,0:T(8,128)(2,1)} %add_convert_fusion.5.refs_0_), channel_id=1, source_target_pairs={{0,16},{8,24},{16,0},{24,8},{1,17},{9,25},{17,1},{25,9},{2,18},{10... | collective-permute-start | bytes 2162696 | tf_op jit(solution)/shard_map/ppermute | solution.py:354
  381.2 21.2 %collective-permute-start.18 = (bf16[176,2048]{1,0:T(8,128)(2,1)}, bf16[176,2048]{1,0:T(8,128)(2,1)}, u32[]{:S(2)}, u32[]{:S(2)}) collective-permute-start(bf16[176,2048]{1,0:T(8,128)(2,1)} %add_convert_fusion.4.refs_4_), channel_id=1, source_target_pairs={{0,8},{8,0},{16,24},{24,16},{1,9},{9,1},{17,25},{25,17},{2,10},{10... | collective-permute-start | bytes 2162696 | tf_op jit(solution)/shard_map/ppermute | solution.py:354
  391.0 66.6 %copy-start.14 = (bf16[256,768]{1,0:T(8,128)(2,1)}, bf16[256,768]{1,0:T(8,128)(2,1)S(1)}, u32[]{:S(2)}) copy-start(bf16[256,768]{1,0:T(8,128)(2,1)S(1)} %add_convert_fusion.9.refs_0_) | copy-start | bytes 1179652
  392.5 65.1 %copy-start.15 = (bf16[256,768]{1,0:T(8,128)(2,1)}, bf16[256,768]{1,0:T(8,128)(2,1)S(1)}, u32[]{:S(2)}) copy-start(bf16[256,768]{1,0:T(8,128)(2,1)S(1)} %add_convert_fusion.8.refs_4_) | copy-start | bytes 1179652
  402.4 12.8 %collective-permute-start.26 = (bf16[256,768]{1,0:T(8,128)(2,1)S(1)}, bf16[256,768]{1,0:T(8,128)(2,1)S(1)}, u32[]{:S(2)}, u32[]{:S(2)}) collective-permute-start(bf16[256,768]{1,0:T(8,128)(2,1)S(1)} %add_convert_fusion.9.refs_0_), channel_id=1, source_target_pairs={{0,16},{8,24},{16,0},{24,8},{1,17},{9,25},{17,1},{25,9},{2,18},{10... | collective-permute-start | bytes 1179656 | tf_op jit(solution)/shard_map/ppermute | solution.py:354
  403.1 11.4 %collective-permute-start.21 = (f32[6,128]{1,0:T(8,128)S(1)}, f32[6,128]{1,0:T(8,128)S(1)}, u32[]{:S(2)}, u32[]{:S(2)}) collective-permute-start(f32[6,128]{1,0:T(8,128)S(1)} %add.374), channel_id=1, source_target_pairs={{0,16},{8,24},{16,0},{24,8},{1,17},{9,25},{17,1},{25,9},{2,18},{10... | collective-permute-start | bytes 9224 | tf_op jit(solution)/shard_map/ppermute | solution.py:354
  404.4 39.7 %collective-permute-start.22 = (bf16[176,2048]{1,0:T(8,128)(2,1)}, bf16[176,2048]{1,0:T(8,128)(2,1)S(1)}, u32[]{:S(2)}, u32[]{:S(2)}) collective-permute-start(bf16[176,2048]{1,0:T(8,128)(2,1)} %add_convert_fusion.5.refs_0_), channel_id=1, source_target_pairs={{0,8},{8,0},{16,24},{24,16},{1,9},{9,1},{17,25},{25,17},{2,10},{10... | collective-permute-start | bytes 2162696 | tf_op jit(solution)/shard_map/ppermute | solution.py:354
  405.9 38.3 %collective-permute-start.23 = (bf16[176,2048]{1,0:T(8,128)(2,1)}, bf16[176,2048]{1,0:T(8,128)(2,1)S(1)}, u32[]{:S(2)}, u32[]{:S(2)}) collective-permute-start(bf16[176,2048]{1,0:T(8,128)(2,1)} %collective-permute-done.17.refs_1_), channel_id=1, source_target_pairs={{0,8},{8,0},{16,24},{24,16},{1,9},{9,1},{17,25},{25,17},{2,10},{10... | collective-permute-start | bytes 2162696 | tf_op jit(solution)/shard_map/ppermute | solution.py:354
  406.4 37.7 %collective-permute-start.24 = (bf16[176,2048]{1,0:T(8,128)(2,1)}, bf16[176,2048]{1,0:T(8,128)(2,1)S(1)}, u32[]{:S(2)}, u32[]{:S(2)}) collective-permute-start(bf16[176,2048]{1,0:T(8,128)(2,1)} %add_convert_fusion.4.refs_4_), channel_id=1, source_target_pairs={{0,16},{8,24},{16,0},{24,8},{1,17},{9,25},{17,1},{25,9},{2,18},{10... | collective-permute-start | bytes 2162696 | tf_op jit(solution)/shard_map/ppermute | solution.py:354
  414.5 29.7 %collective-permute-start.25 = (bf16[176,2048]{1,0:T(8,128)(2,1)}, bf16[176,2048]{1,0:T(8,128)(2,1)}, u32[]{:S(2)}, u32[]{:S(2)}) collective-permute-start(bf16[176,2048]{1,0:T(8,128)(2,1)} %collective-permute-done.18.refs_5_), channel_id=1, source_target_pairs={{0,16},{8,24},{16,0},{24,8},{1,17},{9,25},{17,1},{25,9},{2,18},{10... | collective-permute-start | bytes 2162696 | tf_op jit(solution)/shard_map/ppermute | solution.py:354
  416.0 28.2 %collective-permute-start.27 = (bf16[256,768]{1,0:T(8,128)(2,1)S(1)}, bf16[256,768]{1,0:T(8,128)(2,1)}, u32[]{:S(2)}, u32[]{:S(2)}) collective-permute-start(bf16[256,768]{1,0:T(8,128)(2,1)S(1)} %add_convert_fusion.8.refs_4_), channel_id=1, source_target_pairs={{0,8},{8,0},{16,24},{24,16},{1,9},{9,1},{17,25},{25,17},{2,10},{10... | collective-permute-start | bytes 1179656 | tf_op jit(solution)/shard_map/ppermute | solution.py:354
  444.2 13.4 %collective-permute-start.28 = (bf16[256,768]{1,0:T(8,128)(2,1)S(1)}, bf16[256,768]{1,0:T(8,128)(2,1)}, u32[]{:S(2)}, u32[]{:S(2)}) collective-permute-start(bf16[256,768]{1,0:T(8,128)(2,1)S(1)} %add_convert_fusion.9.refs_0_), channel_id=1, source_target_pairs={{0,8},{8,0},{16,24},{24,16},{1,9},{9,1},{17,25},{25,17},{2,10},{10... | collective-permute-start | bytes 1179656 | tf_op jit(solution)/shard_map/ppermute | solution.py:354
  446.2 11.4 %collective-permute-start.29 = (bf16[256,768]{1,0:T(8,128)(2,1)}, bf16[256,768]{1,0:T(8,128)(2,1)}, u32[]{:S(2)}, u32[]{:S(2)}) collective-permute-start(bf16[256,768]{1,0:T(8,128)(2,1)} %copy-done.23), channel_id=1, source_target_pairs={{0,8},{8,0},{16,24},{24,16},{1,9},{9,1},{17,25},{25,17},{2,10},{10... | collective-permute-start | bytes 1179656 | tf_op jit(solution)/shard_map/ppermute | solution.py:354
  446.3 11.4 %collective-permute-start.30 = (bf16[256,768]{1,0:T(8,128)(2,1)S(1)}, bf16[256,768]{1,0:T(8,128)(2,1)}, u32[]{:S(2)}, u32[]{:S(2)}) collective-permute-start(bf16[256,768]{1,0:T(8,128)(2,1)S(1)} %add_convert_fusion.8.refs_4_), channel_id=1, source_target_pairs={{0,16},{8,24},{16,0},{24,8},{1,17},{9,25},{17,1},{25,9},{2,18},{10... | collective-permute-start | bytes 1179656 | tf_op jit(solution)/shard_map/ppermute | solution.py:354
  447.5 10.8 %collective-permute-start.31 = (bf16[256,768]{1,0:T(8,128)(2,1)}, bf16[256,768]{1,0:T(8,128)(2,1)}, u32[]{:S(2)}, u32[]{:S(2)}) collective-permute-start(bf16[256,768]{1,0:T(8,128)(2,1)} %collective-permute-done.27.refs_5_), channel_id=1, source_target_pairs={{0,16},{8,24},{16,0},{24,8},{1,17},{9,25},{17,1},{25,9},{2,18},{10... | collective-permute-start | bytes 1179656 | tf_op jit(solution)/shard_map/ppermute | solution.py:354
  469.0 1.4 collective-permute-start.32
  471.2 4.0 collective-permute-start.33
  475.2 4.9 collective-permute-start.34
  480.1 4.0 collective-permute-start.35
  484.1 9.5 %collective-permute-start.36 = (f32[4,2048]{1,0:T(4,128)S(1)}, f32[4,2048]{1,0:T(4,128)S(1)}, u32[]{:S(2)}, u32[]{:S(2)}) collective-permute-start(f32[4,2048]{1,0:T(4,128)S(1)} %add.405), channel_id=1, source_target_pairs={{0,16},{8,24},{16,0},{24,8},{1,17},{9,25},{17,1},{25,9},{2,18},{10... | collective-permute-start | bytes 98312 | tf_op jit(solution)/shard_map/ppermute | solution.py:354
  (28 other events, 157.1 us)
Sparse Core Ops, SparseCore 0:
  14.1 84.7 all-gather.2
  100.5 80.5 all-gather.4
  183.3 88.0 reduce-scatter.3
  274.1 87.9 reduce-scatter.5
  377.1 86.7 reduce-scatter.7
where the time goes:
time: 512 us; the launch traced here: 503 us
  waiting for transfers between devices  149 us (29%)
  Pallas kernels  137 us (27%)
  matrix products  101 us (20%)
  other arithmetic  44.5 us (9%)
  starting transfers between devices  33.2 us (6%)
  local copies, waits for them, and re-layouts  22.4 us (4%)
  between operations  16.2 us (3%)
    all_gather x1, waiting for transfers between devices, local(): gathered = lax.all_gather(normed, 'mp', axis=0, tiled=True)  73.4 us
    ppermute x37, waiting for transfers between devices, swap(): return lax.ppermute(values, name, [(i, i ^ 1 << bit) for i in range(size)])  70.1 us
    dot_general x5, matrix products, token_sum(): lax.dot_general(left, right, (((0,), (0,)), ((), ())), preferred_element_...  44.9 us
    pallas_call x1, Pallas kernels, attend_back(): pl.pallas_call(attend_back_kernel, grid_spec=pltpu.PrefetchScalarGridSpec...  40.1 us
    dot_general x4, matrix products, turned_product(): lax.dot_general(left, right, (((1,), (1,)), ((), ())), preferred_element_...  39.8 us
    ppermute x37, starting transfers between devices, swap(): return lax.ppermute(values, name, [(i, i ^ 1 << bit) for i in range(size)])  32.4 us
    pallas_call x1, Pallas kernels, attend(): pl.pallas_call(attend_kernel, grid_spec=pltpu.PrefetchScalarGridSpec(num_...  29.2 us
    pallas_call x1, Pallas kernels, back_products(): pl.pallas_call(back_products_kernel, grid=(length // rows,), in_specs=[pl...  26.3 us
  transfers between devices with their start and end apart: 42, of which 17 were waited for; matrix products, arithmetic and copies ran while one was open for 30% of the time, Pallas kernels for 26%

commit v1 on v0

--- a/solution.py
+++ b/solution.py
@@ -680,17 +680,19 @@
     attn_sum = scattered(attn_partial)
 
     cotangent, attn_partial = lax.optimization_barrier((cotangent, attn_partial))
+    sum_down = DpSum(token_sum(hidden, cotangent), token_sum(attended, cotangent))
+    cotangent = fence(cotangent, sum_down)
+    sum_down.send()
     grad_hid = turned_product(cotangent, w_down).astype(BF16).astype(F32)
     grad_gate = (
         grad_hid * up * sigmoid_gate * (1.0 + gate * (1.0 - sigmoid_gate))
     ).astype(BF16)
     grad_up = (grad_hid * gate * sigmoid_gate).astype(BF16)
-    sum_down = DpSum(token_sum(hidden, cotangent), token_sum(attended, cotangent))
-    gathered_next = fence(gathered, sum_down)
+    sum_gate = token_sum(grad_gate, gathered)
+    sum_down.arrive()
+    sum_gate, grad_up = fence((sum_gate, grad_up), sum_down)
     sum_down.send()
-    sum_gate_up = DpSum(
-        token_sum(grad_gate, gathered_next), token_sum(grad_up, gathered_next), paired=True
-    )
+    sum_gate_up = DpSum(sum_gate, token_sum(grad_up, gathered), paired=True)
     sum_down.arrive()
     cotangent = fence(cotangent, sum_gate_up, sum_down)
     grad_att = turned_product(cotangent, w_out).astype(BF16)
@@ -704,17 +706,20 @@
     grad_proj, mlp_sum = fence((grad_proj, mlp_sum), sum_gate_up, sum_down)
     sum_gate_up.send()
     sum_down.send()
+    fresh = [held[len(held) // 2][0] for held in sum_down.held]
     normed_partial = back_products(grad_proj, w_qkv, grad_gate, grad_up, w_gate_up)
     sum_gate_up.arrive()
     sum_down.arrive()
-    grad_proj, normed_partial = fence((grad_proj, normed_partial), sum_gate_up, sum_down)
+    grad_proj, normed_partial, _ = fence((grad_proj, normed_partial, fresh), sum_gate_up)
     while sum_down.level < 2 * sum_down.count:
         sum_down.send()
         sum_down.arrive()
     sum_qkv = DpSum(fence(token_sum(gathered, grad_proj), sum_down))
     bias_sums = jnp.sum(grad_proj, axis=0, dtype=F32).reshape(-1, 128)
     sum_qkv.send()
+    sum_gate_up.send()
     sum_qkv.arrive()
+    sum_gate_up.arrive()
     normed_partial, attn_sum, bias_sums = fence(
         (normed_partial, attn_sum, bias_sums), sum_gate_up, sum_qkv
     )
@@ -739,21 +744,22 @@
     bias_sums, layer_out, stat_row = fence(
         (bias_sums, layer_out, stat_row), sum_gate_up, sum_qkv
     )
-    sum_gate_up.send()
     sum_qkv.send()
     bias_sums = sum_small(bias_sums, "dp", range(1, sum_qkv.count))
     down_sums = sum_down.result(write_rows)
-    sum_gate_up.arrive()
     sum_qkv.arrive()
-    down_sums, bias_sums = fence((down_sums, bias_sums), sum_gate_up, sum_qkv)
+    down_sums, bias_sums = fence((down_sums, bias_sums), sum_qkv)
     for item in (sum_gate_up, sum_qkv):
         while item.level < 2 * item.count:
             item.send()
             item.arrive()
     (grad_w_gate_up,) = sum_gate_up.result(write_stacked)
-    grad_normed, grad_w_gate_up = fence((grad_normed, grad_w_gate_up), sum_qkv)
+    grad_w_gate_up = fence(grad_w_gate_up, sum_qkv)
     (grad_w_qkv,) = sum_qkv.result(write_lanes)
     grad_w_down, grad_w_out = down_sums
+    grad_normed, grad_w_gate_up, grad_w_qkv = fence(
+        (grad_normed, grad_w_gate_up, grad_w_qkv)
+    )
     input_grad, small = tail(layer_in, grad_normed, cot_here, norm_gain, stat_row)
     small = sum_small(sum_small(small, "mp"), "dp")
     totals = small[2]

time: 512 us -> 516 us (level)
  starting transfers between devices: 33.2 us -> 39.1 us
    ppermute x37, waiting for transfers between devices: 70.1 us -> 62.4 us  [swap(): return lax.ppermute(values, name, [(i, i ^ 1 << bit) for i in range(size)])]
    reduce_scatter x3, waiting for transfers between devices: 5.55 us -> 11.6 us  [scattered(): return lax.psum_scatter(partial, 'mp', scatter_dimension=0, tiled=True)]
    ppermute x37, starting transfers between devices: 32.4 us -> 38.3 us  [swap(): return lax.ppermute(values, name, [(i, i ^ 1 << bit) for i in range(size)])]
  transfers between devices with their start and end apart: 42 -> 42, of which waited for: 17 -> 14; matrix products, arithmetic and copies ran while one was open for 30% -> 30% of each run, Pallas kernels for 26% -> 26%
where the time goes in v1:
time: 516 us; the launch traced here: 509 us
  waiting for transfers between devices  148 us (29%)
  Pallas kernels  140 us (27%)
  matrix products  106 us (21%)
  other arithmetic  40.9 us (8%)
  starting transfers between devices  39.1 us (8%)
  local copies, waits for them, and re-layouts  19 us (4%)
  between operations  16.2 us (3%)
    all_gather x1, waiting for transfers between devices, local(): gathered = lax.all_gather(normed, 'mp', axis=0, tiled=True)  73.5 us
    ppermute x37, waiting for transfers between devices, swap(): return lax.ppermute(values, name, [(i, i ^ 1 << bit) for i in range(size)])  62.4 us
    dot_general x5, matrix products, token_sum(): lax.dot_general(left, right, (((0,), (0,)), ((), ())), preferred_element_...  45.8 us
    dot_general x4, matrix products, turned_product(): lax.dot_general(left, right, (((1,), (1,)), ((), ())), preferred_element_...  44.3 us
    pallas_call x1, Pallas kernels, attend_back(): pl.pallas_call(attend_back_kernel, grid_spec=pltpu.PrefetchScalarGridSpec...  41.5 us
    ppermute x37, starting transfers between devices, swap(): return lax.ppermute(values, name, [(i, i ^ 1 << bit) for i in range(size)])  38.3 us
    pallas_call x1, Pallas kernels, attend(): pl.pallas_call(attend_kernel, grid_spec=pltpu.PrefetchScalarGridSpec(num_...  30.7 us
    pallas_call x1, Pallas kernels, back_products(): pl.pallas_call(back_products_kernel, grid=(length // rows,), in_specs=[pl...  26.3 us
  transfers between devices with their start and end apart: 42, of which 14 were waited for; matrix products, arithmetic and copies ran while one was open for 30% of the time, Pallas kernels for 26%

profile of v1, /device:TPU:0, one launch (start us, length us, event | category | flops | bytes accessed | tf_op | source)
XLA Modules:
  0.0 508.7 jit_solution(14863447633746829932)
XLA Ops:
  7.2 2.3 fusion.16
  11.2 2.7 fusion.12
  15.2 2.3 bitcast_select_fusion.c_ref
  19.6 5.8 %fusion.19 = (f32[2048,128]{1,0:T(8,128)}, f32[2048,128]{1,0:T(8,128)}, f32[2048,128]{1,0:T(8,128)}) fusion(f32[128]{0:T(128)S(1)} %compare_select_fusion.5, f32[2048]{0:T(1024)S(1)} %fusion.23, pred[128]{0:T(512)(128)(4,1)S(1)} %get-tuple-element.308, pred[128]{0:T(512)(128)(4,1)S(1)} %get-tuple-element.309), kind=kLoop, calls=%fused_computation.50 | loop fusion | flops 1048576 | bytes 3154688 | tf_op jit(solution)/shard_map/jit(_where)/select_n | solution.py:41
  25.4 73.5 %all-gather.3.cloned.1.call-done.x_ref = bf16[2048,2048]{1,0:T(8,128)(2,1)} async-done(((bf16[256,2048]{1,0:T(8,128)(2,1)}), bf16[2048,2048]{1,0:T(8,128)(2,1)}) %all-gather.3.cloned.1.call-update) | async-done | bytes 8388624 | tf_op jit(solution)/shard_map/all_gather | solution.py:641
  98.9 10.1 %fusion.6 = f32[2048,704]{1,0:T(8,128)S(1)} fusion(bf16[2048,2048]{1,0:T(8,128)(2,1)} %all-gather.3.cloned.1.call-done.x_ref, bf16[2,704,2048]{2,1,0:T(8,128)(2,1)} %bitcast.111), kind=kOutput, calls=%fused_computation.24 | convolution fusion | flops 5905580032 | bytes 17039360 | tf_op jit(solution)/shard_map/dot_general | solution.py:658
  109.0 13.1 %multiply_convert_fusion = (bf16[2048,704]{1,0:T(8,128)(2,1)S(1)}, f32[2048,704]{1,0:T(8,128)}) fusion(f32[2048,704]{1,0:T(8,128)S(1)} %fusion.6, bf16[2048,2048]{1,0:T(8,128)(2,1)S(1)} %copy-done.29, bf16[2,704,2048]{2,1,0:T(8,128)(2,1)} %bitcast.112), kind=kOutput, calls=%fused_computation.10 | convolution fusion | flops 5914230784 | bytes 25690112 | tf_op jit(solution)/shard_map/dot_general | solution.py:658
  123.8 8.9 %convolution_convert_fusion.1 = bf16[2048,2048]{1,0:T(8,128)(2,1)} fusion(bf16[2048,704]{1,0:T(8,128)(2,1)S(1)} %get-tuple-element.306, bf16[704,2048]{1,0:T(8,128)(2,1)S(1)} %copy-done), kind=kOutput, calls=%fused_computation.3 | convolution fusion | flops 5909774336 | bytes 14155776 | tf_op jit(solution)/shard_map/dot_general | solution.py:655
  133.2 13.2 %project.1 = (bf16[2048,256]{1,0:T(8,128)(2,1)}, bf16[2048,256]{1,0:T(8,128)(2,1)}, bf16[2048,256]{1,0:T(8,128)(2,1)}) custom-call(bf16[2048,2048]{1,0:T(8,128)(2,1)} %all-gather.3.cloned.1.call-done.x_ref, bf16[3,2048,256]{2,1,0:T(8,128)(2,1)} %bitcast.114, bf16[3,256]{1,0:T(4,128)(2,1)} %b_ref.1, f32[2048,128]{1,0:T(8,128)} %get-tuple-element.146.cos_ref, ...), custom_call_target="tpu_custom_call" | custom-call | flops 6442450944 | bytes 14680064 | tf_op jit(solution)/shard_map/project/pallas_call | solution.py:78
  146.5 30.7 %attend.1 = (bf16[2048,256]{1,0:T(8,128)(2,1)}, f32[16,1,512]{2,1,0:T(1,128)}) custom-call(s32[16]{0:T(128)} %and_select_fusion.first_ref, bf16[2048,256]{1,0:T(8,128)(2,1)} %get-tuple-element.149.q_ref, bf16[2048,256]{1,0:T(8,128)(2,1)} %get-tuple-element.150.k_ref, bf16[2048,256]{1,0:T(8,128)(2,1)} %get-tuple-element.151.v_ref, s32[16,1,128]{2,1,0:T(1,128)} %copy-done.26), custom_call_target="tpu_custom_call" | custom-call | flops 8589934592 | bytes 4194304 | tf_op jit(solution)/shard_map/attend/pallas_call | solution.py:181
  177.2 7.3 %convolution_convert_fusion = bf16[2048,2048]{1,0:T(8,128)(2,1)} fusion(bf16[2048,256]{1,0:T(8,128)(2,1)} %get-tuple-element.153.o_ref, bf16[256,2048]{1,0:T(8,128)(2,1)} %param.21), kind=kOutput, calls=%fused_computation.2 | convolution fusion | flops 2151677952 | bytes 10485760 | tf_op jit(solution)/shard_map/dot_general | solution.py:655
  184.5 7.7 %convolution_convert_fusion.8 = bf16[256,2048]{1,0:T(8,128)(2,1)} fusion(bf16[2048,256]{1,0:T(8,128)(2,1)} %get-tuple-element.153.o_ref, bf16[2048,2048]{1,0:T(8,128)(2,1)} %all-gather.5.cloned.1.call-done), kind=kOutput, calls=%fused_computation.31 | convolution fusion | flops 2148007936 | bytes 10485760 | tf_op jit(solution)/shard_map/dot_general | solution.py:663
  192.3 7.6 %convolution_convert_fusion.6 = bf16[704,2048]{1,0:T(8,128)(2,1)} fusion(bf16[2048,704]{1,0:T(8,128)(2,1)S(1)} %copy-done.31, bf16[2048,2048]{1,0:T(8,128)(2,1)S(1)} %copy-done.3), kind=kOutput, calls=%fused_computation.20 | convolution fusion | flops 5907021824 | bytes 14155776 | tf_op jit(solution)/shard_map/dot_general | solution.py:663
  200.1 2.2 constant_dynamic-slice_fusion.10
  202.7 2.1 collective-permute-start.1
  204.8 14.0 %fusion.4 = (bf16[2048,704]{1,0:T(8,128)(2,1)S(1)}, bf16[2048,704]{1,0:T(8,128)(2,1)S(1)}) fusion(f32[2048,704]{1,0:T(8,128)} %copy-done.32, f32[2048,704]{1,0:T(8,128)} %get-tuple-element.307, bf16[2048,2048]{1,0:T(8,128)(2,1)} %all-gather.5.cloned.1.call-done, bf16[704,2048]{1,0:T(8,128)(2,1)S(1)} %copy-done), kind=kOutput, calls=%fused_computation.8 | convolution fusion | flops 5927206912 | bytes 28573696 | tf_op jit(solution)/shard_map/dot_general | solution.py:658
  218.9 11.0 %convolution_convert_fusion.5 = bf16[704,2048]{1,0:T(8,128)(2,1)S(1)} fusion(bf16[2048,704]{1,0:T(8,128)(2,1)S(1)} %get-tuple-element.285.g_ref, bf16[2048,2048]{1,0:T(8,128)(2,1)} %all-gather.3.cloned.1.call-done.x_ref), kind=kOutput, calls=%fused_computation.19 | convolution fusion | flops 5907021824 | bytes 14155776 | tf_op jit(solution)/shard_map/dot_general | solution.py:663
  231.2 1.8 collective-permute-start.3
  233.0 8.9 %convolution_convert_fusion.4 = bf16[704,2048]{1,0:T(8,128)(2,1)S(1)} fusion(bf16[2048,704]{1,0:T(8,128)(2,1)S(1)} %get-tuple-element.159.u_ref, bf16[2048,2048]{1,0:T(8,128)(2,1)} %all-gather.3.cloned.1.call-done.x_ref), kind=kOutput, calls=%fused_computation.18 | convolution fusion | flops 5907021824 | bytes 14155776 | tf_op jit(solution)/shard_map/dot_general | solution.py:663
  249.7 7.1 %convolution_convert_fusion.7.do_ref = bf16[2048,256]{1,0:T(8,128)(2,1)} fusion(bf16[2048,2048]{1,0:T(8,128)(2,1)} %all-gather.5.cloned.1.call-done, bf16[256,2048]{1,0:T(8,128)(2,1)} %param.21), kind=kOutput, calls=%fused_computation.30 | convolution fusion | flops 2148007936 | bytes 10485760 | tf_op jit(solution)/shard_map/dot_general | solution.py:658
  256.8 41.5 %attend_back.1.p_ref = bf16[2048,768]{1,0:T(8,128)(2,1)} custom-call(s32[16]{0:T(128)} %and_select_fusion.first_ref, bf16[2048,256]{1,0:T(8,128)(2,1)} %get-tuple-element.149.q_ref, bf16[2048,256]{1,0:T(8,128)(2,1)} %get-tuple-element.150.k_ref, bf16[2048,256]{1,0:T(8,128)(2,1)} %get-tuple-element.151.v_ref, ...), custom_call_target="tpu_custom_call" | custom-call | flops 21474836480 | bytes 8388608 | tf_op jit(solution)/shard_map/attend_back/pallas_call | solution.py:312
  298.3 2.1 add_convert_fusion.1
  300.5 1.9 add_convert_fusion
  306.5 1.9 collective-permute-start.9
  308.5 26.3 %back_products.1 = bf16[2048,2048]{1,0:T(8,128)(2,1)} custom-call(bf16[2048,768]{1,0:T(8,128)(2,1)} %attend_back.1.p_ref, bf16[3,2048,256]{2,1,0:T(8,128)(2,1)} %bitcast.115, bf16[2048,704]{1,0:T(8,128)(2,1)} %copy-done.6, bf16[2048,704]{1,0:T(8,128)(2,1)} %copy-done.5, bf16[2,704,2048]{2,1,0:T(8,128)(2,1)} %bitcast.113), custom_call_target="tpu_custom_call" | custom-call | tf_op jit(solution)/shard_map/back_products/pallas_call | solution.py:597
  335.7 2.2 add_convert_fusion.5.refs_0_
  337.9 2.2 add_convert_fusion.4.refs_4_
  340.2 10.6 %convolution_convert_fusion.3 = bf16[2048,768]{1,0:T(8,128)(2,1)S(1)} fusion(bf16[2048,2048]{1,0:T(8,128)(2,1)} %all-gather.3.cloned.1.call-done.x_ref, bf16[2048,768]{1,0:T(8,128)(2,1)} %attend_back.1.p_ref), kind=kOutput, calls=%fused_computation.17 | convolution fusion | flops 6444023808 | bytes 14680064 | tf_op jit(solution)/shard_map/dot_general | solution.py:663
  354.4 2.0 collective-permute-start.16
  357.5 2.4 convert_reduce_fusion
  359.9 14.2 %collective-permute-done.17 = bf16[512,768]{1,0:T(8,128)(2,1)S(1)} collective-permute-done((bf16[512,768]{1,0:T(8,128)(2,1)}, bf16[512,768]{1,0:T(8,128)(2,1)S(1)}, u32[]{:S(2)}, u32[]{:S(2)}) %collective-permute-start.17) | collective-permute-done | bytes 786464 | tf_op jit(solution)/shard_map/ppermute | solution.py:354
  375.0 1.8 add_convert_fusion.2
  378.3 7.1 %collective-permute-done.12.refs_1_ = bf16[176,2048]{1,0:T(8,128)(2,1)} collective-permute-done((bf16[176,2048]{1,0:T(8,128)(2,1)S(1)}, bf16[176,2048]{1,0:T(8,128)(2,1)}, u32[]{:S(2)}, u32[]{:S(2)}) %collective-permute-start.12) | collective-permute-done | bytes 720928 | tf_op jit(solution)/shard_map/ppermute | solution.py:354
  387.6 2.0 collective-permute-start.18
  389.7 2.0 collective-permute-start.20
  393.7 3.0 fusion.13
  398.4 2.5 collective-permute-start.24
  401.5 3.3 select_maximum_fusion
  405.9 22.1 %collective-permute-done.24 = bf16[256,768]{1,0:T(8,128)(2,1)S(1)} collective-permute-done((bf16[256,768]{1,0:T(8,128)(2,1)}, bf16[256,768]{1,0:T(8,128)(2,1)S(1)}, u32[]{:S(2)}, u32[]{:S(2)}) %collective-permute-start.24) | collective-permute-done | bytes 393248 | tf_op jit(solution)/shard_map/ppermute | solution.py:354
  432.3 7.2 %place_blocks.4 = (f32[704,2048]{1,0:T(8,128)}, f32[256,2048]{1,0:T(8,128)}) custom-call(s32[8]{0:T(128)} %constant.128.clone.color_ref, s32[8]{0:T(128)} %stack.118.where_ref, bf16[120,2048]{1,0:T(8,128)(2,1)} %copy-done.13, bf16[120,2048]{1,0:T(8,128)(2,1)} %collective-permute-done.6.refs_1_, bf16[120,2048]{1,0:T(8,128)(2,1)} %collective-permute-done.8.refs_2_, ...), custom_call_target="tpu_custom_call" | custom-call | bytes 11796480 | tf_op jit(solution)/shard_map/place_blocks/pallas_call | solution.py:387
  445.9 8.7 %place_blocks.3 = f32[2,704,2048]{2,1,0:T(8,128)} custom-call(s32[8]{0:T(128)} %constant.128.clone.color_ref, s32[8]{0:T(128)} %stack.109.where_ref, bf16[176,2048]{1,0:T(8,128)(2,1)} %add_convert_fusion.5.refs_0_, bf16[176,2048]{1,0:T(8,128)(2,1)} %collective-permute-done.12.refs_1_, bf16[176,2048]{1,0:T(8,128)(2,1)} %collective-permute-done.19.refs_2_, ...), custom_call_target="tpu_custom_call" | custom-call | bytes 17301504 | tf_op jit(solution)/shard_map/place_blocks/pallas_call | solution.py:387
  456.8 6.8 %place_blocks.5 = f32[3,2048,256]{2,1,0:T(8,128)} custom-call(s32[8]{0:T(128)} %constant.128.clone.color_ref, s32[8]{0:T(128)} %stack.127.where_ref, bf16[256,768]{1,0:T(8,128)(2,1)} %copy-done.14, bf16[256,768]{1,0:T(8,128)(2,1)} %copy-done.18, bf16[256,768]{1,0:T(8,128)(2,1)} %copy-done.20, bf16[256,768]{1,0:T(8,128)(2,1)} %copy-done.21, ...), custom_call_target="tpu_custom_call" | custom-call | bytes 9437184 | tf_op jit(solution)/shard_map/place_blocks/pallas_call | solution.py:387
  463.6 11.6 %reduce-scatter.8.cloned.1.call-done.g_ref = bf16[256,2048]{1,0:T(8,128)(2,1)} async-done(((bf16[2048,2048]{1,0:T(8,128)(2,1)}), bf16[256,2048]{1,0:T(8,128)(2,1)}) %reduce-scatter.8.cloned.1.call-update) | async-done | bytes 1048592 | tf_op jit(solution)/shard_map/reduce_scatter | solution.py:668
  475.2 5.1 tail.1
  482.6 3.9 collective-permute-done.33
  486.9 4.5 collective-permute-done.34
  492.8 2.6 collective-permute-done.35
  497.4 1.9 collective-permute-done.36
  (192 shorter events, 56.6 us)
Async XLA Ops:
  7.2 116.6 %copy-start = (bf16[704,2048]{1,0:T(8,128)(2,1)S(1)}, bf16[704,2048]{1,0:T(8,128)(2,1)}, u32[]{:S(2)}) copy-start(bf16[704,2048]{1,0:T(8,128)(2,1)} %param.23) | copy-start | bytes 8650756
  7.2 91.7 %all-gather.3.cloned.1.call-start = ((), (), s32[]{:S(2)}) async-start(), calls=%async_computation.3 | async-start | bytes 9437184 | tf_op jit(solution)/shard_map/all_gather | solution.py:641
  13.9 170.6 %all-gather.5.cloned.1.call-start = ((), (), s32[]{:S(2)}) async-start(), calls=%async_computation.4 | async-start | bytes 9437184 | tf_op jit(solution)/shard_map/all_gather | solution.py:642
  17.5 286.8 %reduce-scatter.4.cloned.1.call-start = ((), (), s32[]{:S(2)}) async-start(), calls=%async_computation.5 | async-start | bytes 9437184 | tf_op jit(solution)/shard_map/reduce_scatter | solution.py:668
  18.6 90.5 %copy-start.26 = (s32[16,1,128]{2,1,0:T(1,128)}, s32[16,1,128]{2,1,0:T(1,128)S(1)}, u32[]{:S(2)}) copy-start(s32[16,1,128]{2,1,0:T(1,128)S(1)} %broadcast_maximum_fusion.start_ref) | copy-start | bytes 24580
  132.7 245.6 %reduce-scatter.6.cloned.1.call-start = ((), (), s32[]{:S(2)}) async-start(), calls=%async_computation.6 | async-start | bytes 9437184 | tf_op jit(solution)/shard_map/reduce_scatter | solution.py:668
  199.9 275.3 %reduce-scatter.8.cloned.1.call-start = ((), (), s32[]{:S(2)}) async-start(), calls=%async_computation.7 | async-start | bytes 9437184 | tf_op jit(solution)/shard_map/reduce_scatter | solution.py:668
  202.6 27.5 %collective-permute-start = (bf16[240,2048]{1,0:T(8,128)(2,1)S(1)}, bf16[240,2048]{1,0:T(8,128)(2,1)S(1)}, u32[]{:S(2)}, u32[]{:S(2)}) collective-permute-start(bf16[240,2048]{1,0:T(8,128)(2,1)S(1)} %bitcast.126), channel_id=1, source_target_pairs={{0,8},{8,0},{16,24},{24,16},{1,9},{9,1},{17,25},{25,17},{2,10},{10... | collective-permute-start | bytes 2949128 | tf_op jit(solution)/shard_map/ppermute | solution.py:354
  202.7 27.9 %collective-permute-start.1 = (bf16[240,2048]{1,0:T(8,128)(2,1)S(1)}, bf16[240,2048]{1,0:T(8,128)(2,1)S(1)}, u32[]{:S(2)}, u32[]{:S(2)}) collective-permute-start(bf16[240,2048]{1,0:T(8,128)(2,1)S(1)} %bitcast.125), channel_id=1, source_target_pairs={{0,16},{8,24},{16,0},{24,8},{1,17},{9,25},{17,1},{25,9},{2,18},{10... | collective-permute-start | bytes 2949128 | tf_op jit(solution)/shard_map/ppermute | solution.py:354
  231.0 13.5 %collective-permute-start.2 = (bf16[120,2048]{1,0:T(8,128)(2,1)S(1)}, bf16[120,2048]{1,0:T(8,128)(2,1)S(1)}, u32[]{:S(2)}, u32[]{:S(2)}) collective-permute-start(bf16[120,2048]{1,0:T(8,128)(2,1)S(1)} %constant_dynamic-slice_fusion.11), channel_id=1, source_target_pairs={{0,16},{8,24},{16,0},{24,8},{1,17},{9,25},{17,1},{25,9},{2,18},{10... | collective-permute-start | bytes 1474568 | tf_op jit(solution)/shard_map/ppermute | solution.py:354
  231.2 13.5 %collective-permute-start.3 = (bf16[120,2048]{1,0:T(8,128)(2,1)S(1)}, bf16[120,2048]{1,0:T(8,128)(2,1)S(1)}, u32[]{:S(2)}, u32[]{:S(2)}) collective-permute-start(bf16[120,2048]{1,0:T(8,128)(2,1)S(1)} %constant_dynamic-slice_fusion.8), channel_id=1, source_target_pairs={{0,8},{8,0},{16,24},{24,16},{1,9},{9,1},{17,25},{25,17},{2,10},{10... | collective-permute-start | bytes 1474568 | tf_op jit(solution)/shard_map/ppermute | solution.py:354
  244.6 60.8 %copy-start.13 = (bf16[120,2048]{1,0:T(8,128)(2,1)}, bf16[120,2048]{1,0:T(8,128)(2,1)S(1)}, u32[]{:S(2)}) copy-start(bf16[120,2048]{1,0:T(8,128)(2,1)S(1)} %add_convert_fusion.7.refs_0_) | copy-start | bytes 1474564
  245.6 58.7 %collective-permute-start.6 = (bf16[120,2048]{1,0:T(8,128)(2,1)S(1)}, bf16[120,2048]{1,0:T(8,128)(2,1)}, u32[]{:S(2)}, u32[]{:S(2)}) collective-permute-start(bf16[120,2048]{1,0:T(8,128)(2,1)S(1)} %add_convert_fusion.7.refs_0_), channel_id=1, source_target_pairs={{0,16},{8,24},{16,0},{24,8},{1,17},{9,25},{17,1},{25,9},{2,18},{10... | collective-permute-start | bytes 1474568 | tf_op jit(solution)/shard_map/ppermute | solution.py:354
  246.7 57.7 %collective-permute-start.7 = (bf16[120,2048]{1,0:T(8,128)(2,1)}, bf16[120,2048]{1,0:T(8,128)(2,1)}, u32[]{:S(2)}, u32[]{:S(2)}) collective-permute-start(bf16[120,2048]{1,0:T(8,128)(2,1)} %add_convert_fusion.6.refs_4_), channel_id=1, source_target_pairs={{0,8},{8,0},{16,24},{24,16},{1,9},{9,1},{17,25},{25,17},{2,10},{10... | collective-permute-start | bytes 1474568 | tf_op jit(solution)/shard_map/ppermute | solution.py:354
  247.7 50.6 %collective-permute-start.4 = (bf16[352,2048]{1,0:T(8,128)(2,1)}, bf16[352,2048]{1,0:T(8,128)(2,1)S(1)}, u32[]{:S(2)}, u32[]{:S(2)}) collective-permute-start(bf16[352,2048]{1,0:T(8,128)(2,1)} %constant_dynamic-slice_fusion.7), channel_id=1, source_target_pairs={{0,8},{8,0},{16,24},{24,16},{1,9},{9,1},{17,25},{25,17},{2,10},{10... | collective-permute-start | bytes 4325384 | tf_op jit(solution)/shard_map/ppermute | solution.py:354
  248.7 51.7 %collective-permute-start.5 = (bf16[352,2048]{1,0:T(8,128)(2,1)}, bf16[352,2048]{1,0:T(8,128)(2,1)}, u32[]{:S(2)}, u32[]{:S(2)}) collective-permute-start(bf16[352,2048]{1,0:T(8,128)(2,1)} %constant_dynamic-slice_fusion.6), channel_id=1, source_target_pairs={{0,16},{8,24},{16,0},{24,8},{1,17},{9,25},{17,1},{25,9},{2,18},{10... | collective-permute-start | bytes 4325384 | tf_op jit(solution)/shard_map/ppermute | solution.py:354
  304.3 30.4 %collective-permute-start.10 = (bf16[176,2048]{1,0:T(8,128)(2,1)}, bf16[176,2048]{1,0:T(8,128)(2,1)}, u32[]{:S(2)}, u32[]{:S(2)}) collective-permute-start(bf16[176,2048]{1,0:T(8,128)(2,1)} %constant_dynamic-slice_fusion.5), channel_id=1, source_target_pairs={{0,16},{8,24},{16,0},{24,8},{1,17},{9,25},{17,1},{25,9},{2,18},{10... | collective-permute-start | bytes 2162696 | tf_op jit(solution)/shard_map/ppermute | solution.py:354
  304.4 33.5 %collective-permute-start.11 = (bf16[176,2048]{1,0:T(8,128)(2,1)}, bf16[176,2048]{1,0:T(8,128)(2,1)}, u32[]{:S(2)}, u32[]{:S(2)}) collective-permute-start(bf16[176,2048]{1,0:T(8,128)(2,1)} %constant_dynamic-slice_fusion.4), channel_id=1, source_target_pairs={{0,8},{8,0},{16,24},{24,16},{1,9},{9,1},{17,25},{25,17},{2,10},{10... | collective-permute-start | bytes 2162696 | tf_op jit(solution)/shard_map/ppermute | solution.py:354
  305.4 34.8 %collective-permute-start.8 = (bf16[120,2048]{1,0:T(8,128)(2,1)S(1)}, bf16[120,2048]{1,0:T(8,128)(2,1)}, u32[]{:S(2)}, u32[]{:S(2)}) collective-permute-start(bf16[120,2048]{1,0:T(8,128)(2,1)S(1)} %add_convert_fusion.7.refs_0_), channel_id=1, source_target_pairs={{0,8},{8,0},{16,24},{24,16},{1,9},{9,1},{17,25},{25,17},{2,10},{10... | collective-permute-start | bytes 1474568 | tf_op jit(solution)/shard_map/ppermute | solution.py:354
  306.5 33.7 %collective-permute-start.9 = (bf16[120,2048]{1,0:T(8,128)(2,1)}, bf16[120,2048]{1,0:T(8,128)(2,1)}, u32[]{:S(2)}, u32[]{:S(2)}) collective-permute-start(bf16[120,2048]{1,0:T(8,128)(2,1)} %add_convert_fusion.6.refs_4_), channel_id=1, source_target_pairs={{0,16},{8,24},{16,0},{24,8},{1,17},{9,25},{17,1},{25,9},{2,18},{10... | collective-permute-start | bytes 1474568 | tf_op jit(solution)/shard_map/ppermute | solution.py:354
  308.4 42.3 %collective-permute-start.14 = (bf16[120,2048]{1,0:T(8,128)(2,1)}, bf16[120,2048]{1,0:T(8,128)(2,1)}, u32[]{:S(2)}, u32[]{:S(2)}) collective-permute-start(bf16[120,2048]{1,0:T(8,128)(2,1)} %collective-permute-done.6.refs_1_), channel_id=1, source_target_pairs={{0,8},{8,0},{16,24},{24,16},{1,9},{9,1},{17,25},{25,17},{2,10},{10... | collective-permute-start | bytes 1474568 | tf_op jit(solution)/shard_map/ppermute | solution.py:354
  334.7 16.0 %collective-permute-start.15 = (bf16[120,2048]{1,0:T(8,128)(2,1)}, bf16[120,2048]{1,0:T(8,128)(2,1)S(1)}, u32[]{:S(2)}, u32[]{:S(2)}) collective-permute-start(bf16[120,2048]{1,0:T(8,128)(2,1)} %collective-permute-done.7.refs_5_), channel_id=1, source_target_pairs={{0,16},{8,24},{16,0},{24,8},{1,17},{9,25},{17,1},{25,9},{2,18},{10... | collective-permute-start | bytes 1474568 | tf_op jit(solution)/shard_map/ppermute | solution.py:354
  353.4 20.6 %collective-permute-start.17 = (bf16[512,768]{1,0:T(8,128)(2,1)}, bf16[512,768]{1,0:T(8,128)(2,1)S(1)}, u32[]{:S(2)}, u32[]{:S(2)}) collective-permute-start(bf16[512,768]{1,0:T(8,128)(2,1)} %get-tuple-element.288), channel_id=1, source_target_pairs={{0,16},{8,24},{16,0},{24,8},{1,17},{9,25},{17,1},{25,9},{2,18},{10... | collective-permute-start | bytes 2359304 | tf_op jit(solution)/shard_map/ppermute | solution.py:354
  354.4 20.5 %collective-permute-start.16 = (bf16[512,768]{1,0:T(8,128)(2,1)S(1)}, bf16[512,768]{1,0:T(8,128)(2,1)}, u32[]{:S(2)}, u32[]{:S(2)}) collective-permute-start(bf16[512,768]{1,0:T(8,128)(2,1)S(1)} %get-tuple-element.289), channel_id=1, source_target_pairs={{0,8},{8,0},{16,24},{24,16},{1,9},{9,1},{17,25},{25,17},{2,10},{10... | collective-permute-start | bytes 2359304 | tf_op jit(solution)/shard_map/ppermute | solution.py:354
  356.5 28.9 %collective-permute-start.12 = (bf16[176,2048]{1,0:T(8,128)(2,1)S(1)}, bf16[176,2048]{1,0:T(8,128)(2,1)}, u32[]{:S(2)}, u32[]{:S(2)}) collective-permute-start(bf16[176,2048]{1,0:T(8,128)(2,1)S(1)} %copy-done.9), channel_id=1, source_target_pairs={{0,16},{8,24},{16,0},{24,8},{1,17},{9,25},{17,1},{25,9},{2,18},{10... | collective-permute-start | bytes 2162696 | tf_op jit(solution)/shard_map/ppermute | solution.py:354
  356.5 29.6 %collective-permute-start.13 = (bf16[176,2048]{1,0:T(8,128)(2,1)}, bf16[176,2048]{1,0:T(8,128)(2,1)}, u32[]{:S(2)}, u32[]{:S(2)}) collective-permute-start(bf16[176,2048]{1,0:T(8,128)(2,1)} %add_convert_fusion.4.refs_4_), channel_id=1, source_target_pairs={{0,8},{8,0},{16,24},{24,16},{1,9},{9,1},{17,25},{25,17},{2,10},{10... | collective-permute-start | bytes 2162696 | tf_op jit(solution)/shard_map/ppermute | solution.py:354
  386.2 12.3 %collective-permute-start.23 = (bf16[256,768]{1,0:T(8,128)(2,1)}, bf16[256,768]{1,0:T(8,128)(2,1)S(1)}, u32[]{:S(2)}, u32[]{:S(2)}) collective-permute-start(bf16[256,768]{1,0:T(8,128)(2,1)} %constant_dynamic-slice_fusion.2), channel_id=1, source_target_pairs={{0,16},{8,24},{16,0},{24,8},{1,17},{9,25},{17,1},{25,9},{2,18},{10... | collective-permute-start | bytes 1179656 | tf_op jit(solution)/shard_map/ppermute | solution.py:354
  387.6 5.2 %collective-permute-start.18 = (f32[6,128]{1,0:T(8,128)S(1)}, f32[6,128]{1,0:T(8,128)S(1)}, u32[]{:S(2)}, u32[]{:S(2)}) collective-permute-start(f32[6,128]{1,0:T(8,128)S(1)} %bitcast.131), channel_id=1, source_target_pairs={{0,8},{8,0},{16,24},{24,16},{1,9},{9,1},{17,25},{25,17},{2,10},{10... | collective-permute-start | bytes 9224 | tf_op jit(solution)/shard_map/ppermute | solution.py:354
  389.6 38.5 %collective-permute-start.19 = (bf16[176,2048]{1,0:T(8,128)(2,1)}, bf16[176,2048]{1,0:T(8,128)(2,1)}, u32[]{:S(2)}, u32[]{:S(2)}) collective-permute-start(bf16[176,2048]{1,0:T(8,128)(2,1)} %add_convert_fusion.5.refs_0_), channel_id=1, source_target_pairs={{0,8},{8,0},{16,24},{24,16},{1,9},{9,1},{17,25},{25,17},{2,10},{10... | collective-permute-start | bytes 2162696 | tf_op jit(solution)/shard_map/ppermute | solution.py:354
  389.7 38.5 %collective-permute-start.20 = (bf16[176,2048]{1,0:T(8,128)(2,1)}, bf16[176,2048]{1,0:T(8,128)(2,1)}, u32[]{:S(2)}, u32[]{:S(2)}) collective-permute-start(bf16[176,2048]{1,0:T(8,128)(2,1)} %collective-permute-done.12.refs_1_), channel_id=1, source_target_pairs={{0,8},{8,0},{16,24},{24,16},{1,9},{9,1},{17,25},{25,17},{2,10},{10... | collective-permute-start | bytes 2162696 | tf_op jit(solution)/shard_map/ppermute | solution.py:354
  391.7 36.5 %collective-permute-start.21 = (bf16[176,2048]{1,0:T(8,128)(2,1)}, bf16[176,2048]{1,0:T(8,128)(2,1)}, u32[]{:S(2)}, u32[]{:S(2)}) collective-permute-start(bf16[176,2048]{1,0:T(8,128)(2,1)} %add_convert_fusion.4.refs_4_), channel_id=1, source_target_pairs={{0,16},{8,24},{16,0},{24,8},{1,17},{9,25},{17,1},{25,9},{2,18},{10... | collective-permute-start | bytes 2162696 | tf_op jit(solution)/shard_map/ppermute | solution.py:354
  392.8 35.4 %collective-permute-start.22 = (bf16[176,2048]{1,0:T(8,128)(2,1)}, bf16[176,2048]{1,0:T(8,128)(2,1)}, u32[]{:S(2)}, u32[]{:S(2)}) collective-permute-start(bf16[176,2048]{1,0:T(8,128)(2,1)} %collective-permute-done.13.refs_5_), channel_id=1, source_target_pairs={{0,16},{8,24},{16,0},{24,8},{1,17},{9,25},{17,1},{25,9},{2,18},{10... | collective-permute-start | bytes 2162696 | tf_op jit(solution)/shard_map/ppermute | solution.py:354
  398.4 29.6 %collective-permute-start.24 = (bf16[256,768]{1,0:T(8,128)(2,1)}, bf16[256,768]{1,0:T(8,128)(2,1)S(1)}, u32[]{:S(2)}, u32[]{:S(2)}) collective-permute-start(bf16[256,768]{1,0:T(8,128)(2,1)} %constant_dynamic-slice_fusion), channel_id=1, source_target_pairs={{0,8},{8,0},{16,24},{24,16},{1,9},{9,1},{17,25},{25,17},{2,10},{10... | collective-permute-start | bytes 1179656 | tf_op jit(solution)/shard_map/ppermute | solution.py:354
  405.9 48.7 %copy-start.14 = (bf16[256,768]{1,0:T(8,128)(2,1)}, bf16[256,768]{1,0:T(8,128)(2,1)S(1)}, u32[]{:S(2)}) copy-start(bf16[256,768]{1,0:T(8,128)(2,1)S(1)} %add_convert_fusion.9.refs_0_) | copy-start | bytes 1179652
  428.1 26.5 %copy-start.15 = (bf16[256,768]{1,0:T(8,128)(2,1)}, bf16[256,768]{1,0:T(8,128)(2,1)S(1)}, u32[]{:S(2)}) copy-start(bf16[256,768]{1,0:T(8,128)(2,1)S(1)} %add_convert_fusion.8.refs_4_) | copy-start | bytes 1179652
  428.2 11.4 %collective-permute-start.26 = (bf16[256,768]{1,0:T(8,128)(2,1)S(1)}, bf16[256,768]{1,0:T(8,128)(2,1)S(1)}, u32[]{:S(2)}, u32[]{:S(2)}) collective-permute-start(bf16[256,768]{1,0:T(8,128)(2,1)S(1)} %add_convert_fusion.9.refs_0_), channel_id=1, source_target_pairs={{0,16},{8,24},{16,0},{24,8},{1,17},{9,25},{17,1},{25,9},{2,18},{10... | collective-permute-start | bytes 1179656 | tf_op jit(solution)/shard_map/ppermute | solution.py:354
  429.6 11.6 %collective-permute-start.27 = (bf16[256,768]{1,0:T(8,128)(2,1)S(1)}, bf16[256,768]{1,0:T(8,128)(2,1)S(1)}, u32[]{:S(2)}, u32[]{:S(2)}) collective-permute-start(bf16[256,768]{1,0:T(8,128)(2,1)S(1)} %add_convert_fusion.8.refs_4_), channel_id=1, source_target_pairs={{0,8},{8,0},{16,24},{24,16},{1,9},{9,1},{17,25},{25,17},{2,10},{10... | collective-permute-start | bytes 1179656 | tf_op jit(solution)/shard_map/ppermute | solution.py:354
  430.0 9.5 %collective-permute-start.25 = (f32[6,128]{1,0:T(8,128)S(1)}, f32[6,128]{1,0:T(8,128)S(1)}, u32[]{:S(2)}, u32[]{:S(2)}) collective-permute-start(f32[6,128]{1,0:T(8,128)S(1)} %add.374), channel_id=1, source_target_pairs={{0,16},{8,24},{16,0},{24,8},{1,17},{9,25},{17,1},{25,9},{2,18},{10... | collective-permute-start | bytes 9224 | tf_op jit(solution)/shard_map/ppermute | solution.py:354
  441.2 13.4 %collective-permute-start.28 = (bf16[256,768]{1,0:T(8,128)(2,1)S(1)}, bf16[256,768]{1,0:T(8,128)(2,1)S(1)}, u32[]{:S(2)}, u32[]{:S(2)}) collective-permute-start(bf16[256,768]{1,0:T(8,128)(2,1)S(1)} %add_convert_fusion.9.refs_0_), channel_id=1, source_target_pairs={{0,8},{8,0},{16,24},{24,16},{1,9},{9,1},{17,25},{25,17},{2,10},{10... | collective-permute-start | bytes 1179656 | tf_op jit(solution)/shard_map/ppermute | solution.py:354
  441.5 13.1 %collective-permute-start.29 = (bf16[256,768]{1,0:T(8,128)(2,1)S(1)}, bf16[256,768]{1,0:T(8,128)(2,1)S(1)}, u32[]{:S(2)}, u32[]{:S(2)}) collective-permute-start(bf16[256,768]{1,0:T(8,128)(2,1)S(1)} %collective-permute-done.26.refs_1_), channel_id=1, source_target_pairs={{0,8},{8,0},{16,24},{24,16},{1,9},{9,1},{17,25},{25,17},{2,10},{10... | collective-permute-start | bytes 1179656 | tf_op jit(solution)/shard_map/ppermute | solution.py:354
  443.3 11.4 %collective-permute-start.30 = (bf16[256,768]{1,0:T(8,128)(2,1)S(1)}, bf16[256,768]{1,0:T(8,128)(2,1)S(1)}, u32[]{:S(2)}, u32[]{:S(2)}) collective-permute-start(bf16[256,768]{1,0:T(8,128)(2,1)S(1)} %add_convert_fusion.8.refs_4_), channel_id=1, source_target_pairs={{0,16},{8,24},{16,0},{24,8},{1,17},{9,25},{17,1},{25,9},{2,18},{10... | collective-permute-start | bytes 1179656 | tf_op jit(solution)/shard_map/ppermute | solution.py:354
  444.0 11.3 %collective-permute-start.31 = (bf16[256,768]{1,0:T(8,128)(2,1)S(1)}, bf16[256,768]{1,0:T(8,128)(2,1)S(1)}, u32[]{:S(2)}, u32[]{:S(2)}) collective-permute-start(bf16[256,768]{1,0:T(8,128)(2,1)S(1)} %collective-permute-done.27.refs_5_), channel_id=1, source_target_pairs={{0,16},{8,24},{16,0},{24,8},{1,17},{9,25},{17,1},{25,9},{2,18},{10... | collective-permute-start | bytes 1179656 | tf_op jit(solution)/shard_map/ppermute | solution.py:354
  456.8 45.0 %copy-start.1 = (bf16[704,2048]{1,0:T(8,128)(2,1)S(1)}, bf16[704,2048]{1,0:T(8,128)(2,1)}, u32[]{:S(2)}) copy-start(bf16[704,2048]{1,0:T(8,128)(2,1)} %param.23) | copy-start | bytes 8650756
  480.3 1.4 collective-permute-start.32
  482.5 4.0 collective-permute-start.33
  486.5 4.9 collective-permute-start.34
  491.4 4.0 collective-permute-start.35
  495.4 4.0 collective-permute-start.36
  (27 other events, 195.3 us)
Sparse Core Ops, SparseCore 0:
  14.1 84.7 all-gather.2
  100.5 80.5 all-gather.4
  183.3 88.0 reduce-scatter.3
  274.1 88.0 reduce-scatter.5
  386.3 88.9 reduce-scatter.7

commit v2 on v1

--- a/solution.py
+++ b/solution.py
@@ -470,6 +470,9 @@
     def moving(self):
         return self.out if self.held is None else self.held
 
+    def fresh(self):
+        return [held[len(held) // 2][0] for held in self.held]
+
     def result(self, write):
         pieces, colors, where = [], [], []
         for color in range(2):
@@ -688,40 +691,42 @@
         grad_hid * up * sigmoid_gate * (1.0 + gate * (1.0 - sigmoid_gate))
     ).astype(BF16)
     grad_up = (grad_hid * gate * sigmoid_gate).astype(BF16)
+    grad_att = turned_product(cotangent, w_out).astype(BF16)
+    sum_down.arrive()
+    grad_gate, grad_up, grad_att = fence((grad_gate, grad_up, grad_att), sum_down)
+    sum_down.send()
     sum_gate = token_sum(grad_gate, gathered)
     sum_down.arrive()
     sum_gate, grad_up = fence((sum_gate, grad_up), sum_down)
     sum_down.send()
     sum_gate_up = DpSum(sum_gate, token_sum(grad_up, gathered), paired=True)
     sum_down.arrive()
-    cotangent = fence(cotangent, sum_gate_up, sum_down)
-    grad_att = turned_product(cotangent, w_out).astype(BF16)
+    grad_att = fence(grad_att, sum_gate_up, sum_down)
     sum_gate_up.send()
     sum_down.send()
+    fresh = sum_down.fresh()
     grad_proj = attend_back(
         first, queries, key_rows, value_rows, grad_att, attended, lse, start_blocks, tables
     )
     sum_gate_up.arrive()
     sum_down.arrive()
-    grad_proj, mlp_sum = fence((grad_proj, mlp_sum), sum_gate_up, sum_down)
+    grad_proj, mlp_sum, _ = fence((grad_proj, mlp_sum, fresh), sum_gate_up)
     sum_gate_up.send()
-    sum_down.send()
-    fresh = [held[len(held) // 2][0] for held in sum_down.held]
     normed_partial = back_products(grad_proj, w_qkv, grad_gate, grad_up, w_gate_up)
-    sum_gate_up.arrive()
-    sum_down.arrive()
-    grad_proj, normed_partial, _ = fence((grad_proj, normed_partial, fresh), sum_gate_up)
     while sum_down.level < 2 * sum_down.count:
         sum_down.send()
         sum_down.arrive()
-    sum_qkv = DpSum(fence(token_sum(gathered, grad_proj), sum_down))
+    sum_gate_up.arrive()
+    grad_proj, normed_partial = fence((grad_proj, normed_partial), sum_gate_up, sum_down)
+    sum_gate_up.send()
+    sum_qkv = token_sum(gathered, grad_proj)
+    sum_gate_up.arrive()
+    sum_qkv = DpSum(fence(sum_qkv, sum_gate_up))
     bias_sums = jnp.sum(grad_proj, axis=0, dtype=F32).reshape(-1, 128)
     sum_qkv.send()
-    sum_gate_up.send()
     sum_qkv.arrive()
-    sum_gate_up.arrive()
     normed_partial, attn_sum, bias_sums = fence(
-        (normed_partial, attn_sum, bias_sums), sum_gate_up, sum_qkv
+        (normed_partial, attn_sum, bias_sums), sum_qkv
     )
     grad_normed = scattered(normed_partial)
     sum_gate_up.send()
@@ -739,20 +744,21 @@
         ]
     )
     stat_row = jnp.pad(statistics, (0, model_width - 4)).reshape(1, model_width)
+    fresh = sum_gate_up.fresh()
     sum_gate_up.arrive()
     sum_qkv.arrive()
-    bias_sums, layer_out, stat_row = fence(
-        (bias_sums, layer_out, stat_row), sum_gate_up, sum_qkv
-    )
+    bias_sums, layer_out, stat_row, _ = fence((bias_sums, layer_out, stat_row, fresh), sum_qkv)
     sum_qkv.send()
     bias_sums = sum_small(bias_sums, "dp", range(1, sum_qkv.count))
     down_sums = sum_down.result(write_rows)
     sum_qkv.arrive()
-    down_sums, bias_sums = fence((down_sums, bias_sums), sum_qkv)
-    for item in (sum_gate_up, sum_qkv):
-        while item.level < 2 * item.count:
-            item.send()
-            item.arrive()
+    while sum_gate_up.level < 2 * sum_gate_up.count:
+        sum_gate_up.send()
+        sum_gate_up.arrive()
+    down_sums, bias_sums = fence((down_sums, bias_sums), sum_gate_up, sum_qkv)
+    while sum_qkv.level < 2 * sum_qkv.count:
+        sum_qkv.send()
+        sum_qkv.arrive()
     (grad_w_gate_up,) = sum_gate_up.result(write_stacked)
     grad_w_gate_up = fence(grad_w_gate_up, sum_qkv)
     (grad_w_qkv,) = sum_qkv.result(write_lanes)

time: 516 us -> 510 us (0.988)
  Pallas kernels: 140 us -> 132 us
  waiting for transfers between devices: 148 us -> 142 us
    ppermute x37, waiting for transfers between devices: 62.4 us -> 51.9 us  [swap(): return lax.ppermute(values, name, [(i, i ^ 1 << bit) for i in range(size)])]
  transfers between devices with their start and end apart: 42 -> 42, of which waited for: 14 -> 21; matrix products, arithmetic and copies ran while one was open for 30% -> 31% of each run, Pallas kernels for 26% -> 25%
where the time goes in v2:
time: 510 us; the launch traced here: 500 us
  waiting for transfers between devices  142 us (28%)
  Pallas kernels  132 us (26%)
  matrix products  105 us (21%)
  other arithmetic  45.3 us (9%)
  starting transfers between devices  41.1 us (8%)
  local copies, waits for them, and re-layouts  18.5 us (4%)
  between operations  16.2 us (3%)
    all_gather x1, waiting for transfers between devices, local(): gathered = lax.all_gather(normed, 'mp', axis=0, tiled=True)  73.5 us
    ppermute x37, waiting for transfers between devices, swap(): return lax.ppermute(values, name, [(i, i ^ 1 << bit) for i in range(size)])  51.9 us
    dot_general x5, matrix products, token_sum(): lax.dot_general(left, right, (((0,), (0,)), ((), ())), preferred_element_...  46 us
    dot_general x4, matrix products, turned_product(): lax.dot_general(left, right, (((1,), (1,)), ((), ())), preferred_element_...  43.2 us
    ppermute x37, starting transfers between devices, swap(): return lax.ppermute(values, name, [(i, i ^ 1 << bit) for i in range(size)])  40.3 us
    pallas_call x1, Pallas kernels, attend_back(): pl.pallas_call(attend_back_kernel, grid_spec=pltpu.PrefetchScalarGridSpec...  37.3 us
    pallas_call x1, Pallas kernels, attend(): pl.pallas_call(attend_kernel, grid_spec=pltpu.PrefetchScalarGridSpec(num_...  27 us
    pallas_call x1, Pallas kernels, back_products(): pl.pallas_call(back_products_kernel, grid=(length // rows,), in_specs=[pl...  26.2 us
  transfers between devices with their start and end apart: 42, of which 21 were waited for; matrix products, arithmetic and copies ran while one was open for 31% of the time, Pallas kernels for 25%

profile of v2, /device:TPU:0, one launch (start us, length us, event | category | flops | bytes accessed | tf_op | source)
XLA Modules:
  0.0 499.8 jit_solution(14669778131284878282)
XLA Ops:
  7.2 2.3 fusion.16
  9.6 1.6 fusion.9
  11.2 2.7 fusion.12
  15.2 2.3 bitcast_select_fusion.c_ref
  19.6 5.8 %fusion.19 = (f32[2048,128]{1,0:T(8,128)}, f32[2048,128]{1,0:T(8,128)}, f32[2048,128]{1,0:T(8,128)}) fusion(f32[128]{0:T(128)S(1)} %compare_select_fusion.5, f32[2048]{0:T(1024)S(1)} %fusion.23, pred[128]{0:T(512)(128)(4,1)S(1)} %get-tuple-element.314, pred[128]{0:T(512)(128)(4,1)S(1)} %get-tuple-element.315), kind=kLoop, calls=%fused_computation.50 | loop fusion | flops 1048576 | bytes 3154688 | tf_op jit(solution)/shard_map/jit(_where)/select_n | solution.py:41
  25.4 73.5 %all-gather.3.cloned.1.call-done.x_ref = bf16[2048,2048]{1,0:T(8,128)(2,1)} async-done(((bf16[256,2048]{1,0:T(8,128)(2,1)}), bf16[2048,2048]{1,0:T(8,128)(2,1)}) %all-gather.3.cloned.1.call-update) | async-done | bytes 8388624 | tf_op jit(solution)/shard_map/all_gather | solution.py:644
  98.9 10.1 %fusion.6 = f32[2048,704]{1,0:T(8,128)S(1)} fusion(bf16[2048,2048]{1,0:T(8,128)(2,1)} %all-gather.3.cloned.1.call-done.x_ref, bf16[2,704,2048]{2,1,0:T(8,128)(2,1)} %bitcast.113), kind=kOutput, calls=%fused_computation.24 | convolution fusion | flops 5905580032 | bytes 17039360 | tf_op jit(solution)/shard_map/dot_general | solution.py:661
  109.0 13.1 %multiply_convert_fusion = (bf16[2048,704]{1,0:T(8,128)(2,1)S(1)}, f32[2048,704]{1,0:T(8,128)}) fusion(f32[2048,704]{1,0:T(8,128)S(1)} %fusion.6, bf16[2048,2048]{1,0:T(8,128)(2,1)S(1)} %copy-done.29, bf16[2,704,2048]{2,1,0:T(8,128)(2,1)} %bitcast.114), kind=kOutput, calls=%fused_computation.10 | convolution fusion | flops 5914230784 | bytes 25690112 | tf_op jit(solution)/shard_map/dot_general | solution.py:661
  122.1 1.7 copy-done.30
  123.8 8.9 %convolution_convert_fusion.1 = bf16[2048,2048]{1,0:T(8,128)(2,1)} fusion(bf16[2048,704]{1,0:T(8,128)(2,1)S(1)} %get-tuple-element.312, bf16[704,2048]{1,0:T(8,128)(2,1)S(1)} %copy-done), kind=kOutput, calls=%fused_computation.3 | convolution fusion | flops 5909774336 | bytes 14155776 | tf_op jit(solution)/shard_map/dot_general | solution.py:658
  133.2 13.2 %project.1 = (bf16[2048,256]{1,0:T(8,128)(2,1)}, bf16[2048,256]{1,0:T(8,128)(2,1)}, bf16[2048,256]{1,0:T(8,128)(2,1)}) custom-call(bf16[2048,2048]{1,0:T(8,128)(2,1)} %all-gather.3.cloned.1.call-done.x_ref, bf16[3,2048,256]{2,1,0:T(8,128)(2,1)} %bitcast.116, bf16[3,256]{1,0:T(4,128)(2,1)} %b_ref.1, f32[2048,128]{1,0:T(8,128)} %get-tuple-element.149.cos_ref, ...), custom_call_target="tpu_custom_call" | custom-call | flops 6442450944 | bytes 14680064 | tf_op jit(solution)/shard_map/project/pallas_call | solution.py:78
  146.5 27.0 %attend.1 = (bf16[2048,256]{1,0:T(8,128)(2,1)}, f32[16,1,512]{2,1,0:T(1,128)}) custom-call(s32[16]{0:T(128)} %and_select_fusion.first_ref, bf16[2048,256]{1,0:T(8,128)(2,1)} %get-tuple-element.152.q_ref, bf16[2048,256]{1,0:T(8,128)(2,1)} %get-tuple-element.153.k_ref, bf16[2048,256]{1,0:T(8,128)(2,1)} %get-tuple-element.154.v_ref, s32[16,1,128]{2,1,0:T(1,128)} %copy-done.26), custom_call_target="tpu_custom_call" | custom-call | flops 8589934592 | bytes 4194304 | tf_op jit(solution)/shard_map/attend/pallas_call | solution.py:181
  173.5 7.3 %convolution_convert_fusion = bf16[2048,2048]{1,0:T(8,128)(2,1)} fusion(bf16[2048,256]{1,0:T(8,128)(2,1)} %get-tuple-element.156.o_ref, bf16[256,2048]{1,0:T(8,128)(2,1)} %param.21), kind=kOutput, calls=%fused_computation.2 | convolution fusion | flops 2151677952 | bytes 10485760 | tf_op jit(solution)/shard_map/dot_general | solution.py:658
  181.0 7.2 %convolution_convert_fusion.8 = bf16[256,2048]{1,0:T(8,128)(2,1)} fusion(bf16[2048,256]{1,0:T(8,128)(2,1)} %get-tuple-element.156.o_ref, bf16[2048,2048]{1,0:T(8,128)(2,1)} %all-gather.5.cloned.1.call-done), kind=kOutput, calls=%fused_computation.31 | convolution fusion | flops 2148007936 | bytes 10485760 | tf_op jit(solution)/shard_map/dot_general | solution.py:666
  188.2 7.6 %convolution_convert_fusion.6 = bf16[704,2048]{1,0:T(8,128)(2,1)} fusion(bf16[2048,704]{1,0:T(8,128)(2,1)S(1)} %copy-done.31, bf16[2048,2048]{1,0:T(8,128)(2,1)S(1)} %copy-done.3), kind=kOutput, calls=%fused_computation.20 | convolution fusion | flops 5907021824 | bytes 14155776 | tf_op jit(solution)/shard_map/dot_general | solution.py:666
  196.1 2.2 constant_dynamic-slice_fusion.10
  201.2 4.4 collective-permute-start
  205.6 15.3 %fusion.4 = (bf16[2048,704]{1,0:T(8,128)(2,1)}, bf16[2048,704]{1,0:T(8,128)(2,1)S(1)}) fusion(f32[2048,704]{1,0:T(8,128)} %copy-done.32, f32[2048,704]{1,0:T(8,128)} %get-tuple-element.313, bf16[2048,2048]{1,0:T(8,128)(2,1)} %all-gather.5.cloned.1.call-done, bf16[704,2048]{1,0:T(8,128)(2,1)S(1)} %copy-done), kind=kOutput, calls=%fused_computation.8 | convolution fusion | flops 5927206912 | bytes 28573696 | tf_op jit(solution)/shard_map/dot_general | solution.py:661
  222.1 4.7 convolution_convert_fusion.7.do_ref
  233.2 9.8 %convolution_convert_fusion.5 = bf16[704,2048]{1,0:T(8,128)(2,1)} fusion(bf16[2048,704]{1,0:T(8,128)(2,1)S(1)} %get-tuple-element.162.g_ref, bf16[2048,2048]{1,0:T(8,128)(2,1)} %all-gather.3.cloned.1.call-done.x_ref), kind=kOutput, calls=%fused_computation.19 | convolution fusion | flops 5907021824 | bytes 14155776 | tf_op jit(solution)/shard_map/dot_general | solution.py:666
  248.3 9.8 %convolution_convert_fusion.4 = bf16[704,2048]{1,0:T(8,128)(2,1)S(1)} fusion(bf16[2048,704]{1,0:T(8,128)(2,1)} %get-tuple-element.167.u_ref, bf16[2048,2048]{1,0:T(8,128)(2,1)} %all-gather.3.cloned.1.call-done.x_ref), kind=kOutput, calls=%fused_computation.18 | convolution fusion | flops 5907021824 | bytes 14155776 | tf_op jit(solution)/shard_map/dot_general | solution.py:666
  264.4 37.3 %attend_back.1.p_ref = bf16[2048,768]{1,0:T(8,128)(2,1)} custom-call(s32[16]{0:T(128)} %and_select_fusion.first_ref, bf16[2048,256]{1,0:T(8,128)(2,1)} %get-tuple-element.152.q_ref, bf16[2048,256]{1,0:T(8,128)(2,1)} %get-tuple-element.153.k_ref, bf16[2048,256]{1,0:T(8,128)(2,1)} %get-tuple-element.154.v_ref, ...), custom_call_target="tpu_custom_call" | custom-call | flops 21474836480 | bytes 8388608 | tf_op jit(solution)/shard_map/attend_back/pallas_call | solution.py:312
  302.3 2.8 add_convert_fusion.1
  305.1 1.9 add_convert_fusion
  309.3 2.1 collective-permute-start.11
  311.5 1.9 collective-permute-start.13
  313.4 26.2 %back_products.1 = bf16[2048,2048]{1,0:T(8,128)(2,1)} custom-call(bf16[2048,768]{1,0:T(8,128)(2,1)} %attend_back.1.p_ref, bf16[3,2048,256]{2,1,0:T(8,128)(2,1)} %bitcast.117, bf16[2048,704]{1,0:T(8,128)(2,1)} %copy-done.5, bf16[2048,704]{1,0:T(8,128)(2,1)} %get-tuple-element.167.u_ref, bf16[2,704,2048]{2,1,0:T(8,128)(2,1)} %bitcast.115), custom_call_target="tpu_custom_call" | custom-call | tf_op jit(solution)/shard_map/back_products/pallas_call | solution.py:600
  339.7 2.2 add_convert_fusion.5.refs_0_
  343.4 2.0 collective-permute-start.15
  345.4 11.6 %convolution_convert_fusion.3 = bf16[2048,768]{1,0:T(8,128)(2,1)} fusion(bf16[2048,2048]{1,0:T(8,128)(2,1)} %all-gather.3.cloned.1.call-done.x_ref, bf16[2048,768]{1,0:T(8,128)(2,1)} %attend_back.1.p_ref), kind=kOutput, calls=%fused_computation.17 | convolution fusion | flops 6444023808 | bytes 14680064 | tf_op jit(solution)/shard_map/dot_general | solution.py:666
  362.7 2.4 convert_reduce_fusion
  365.1 9.9 %collective-permute-done.17 = bf16[512,768]{1,0:T(8,128)(2,1)S(1)} collective-permute-done((bf16[512,768]{1,0:T(8,128)(2,1)S(1)}, bf16[512,768]{1,0:T(8,128)(2,1)S(1)}, u32[]{:S(2)}, u32[]{:S(2)}) %collective-permute-start.17) | collective-permute-done | bytes 786464 | tf_op jit(solution)/shard_map/ppermute | solution.py:354
  376.1 2.0 add_convert_fusion.2
  384.1 3.0 fusion.13
  387.8 3.3 select_maximum_fusion
  391.0 7.4 %collective-permute-done.18 = f32[6,128]{1,0:T(8,128)S(1)} collective-permute-done((f32[6,128]{1,0:T(8,128)S(1)}, f32[6,128]{1,0:T(8,128)S(1)}, u32[]{:S(2)}, u32[]{:S(2)}) %collective-permute-start.18) | collective-permute-done | bytes 3104 | tf_op jit(solution)/shard_map/ppermute | solution.py:354
  399.4 5.3 %collective-permute-done.21 = bf16[256,768]{1,0:T(8,128)(2,1)S(1)} collective-permute-done((bf16[256,768]{1,0:T(8,128)(2,1)S(1)}, bf16[256,768]{1,0:T(8,128)(2,1)S(1)}, u32[]{:S(2)}, u32[]{:S(2)}) %collective-permute-start.21) | collective-permute-done | bytes 393248 | tf_op jit(solution)/shard_map/ppermute | solution.py:354
  408.6 1.6 collective-permute-start.27
  411.5 7.2 %place_blocks.3 = (f32[704,2048]{1,0:T(8,128)}, f32[256,2048]{1,0:T(8,128)}) custom-call(s32[8]{0:T(128)} %constant.128.clone.color_ref, s32[8]{0:T(128)} %stack.109.where_ref, bf16[120,2048]{1,0:T(8,128)(2,1)} %copy-done.10, bf16[120,2048]{1,0:T(8,128)(2,1)} %copy-done.16, bf16[120,2048]{1,0:T(8,128)(2,1)} %collective-permute-done.6.refs_2_, ...), custom_call_target="tpu_custom_call" | custom-call | bytes 11796480 | tf_op jit(solution)/shard_map/place_blocks/pallas_call | solution.py:387
  418.8 8.3 %collective-permute-done.23 = f32[6,128]{1,0:T(8,128)S(1)} collective-permute-done((f32[6,128]{1,0:T(8,128)S(1)}, f32[6,128]{1,0:T(8,128)S(1)}, u32[]{:S(2)}, u32[]{:S(2)}) %collective-permute-start.23) | collective-permute-done | bytes 3104 | tf_op jit(solution)/shard_map/ppermute | solution.py:354
  432.6 8.7 %place_blocks.4 = f32[2,704,2048]{2,1,0:T(8,128)} custom-call(s32[8]{0:T(128)} %constant.128.clone.color_ref, s32[8]{0:T(128)} %stack.118.where_ref, bf16[176,2048]{1,0:T(8,128)(2,1)} %add_convert_fusion.5.refs_0_, bf16[176,2048]{1,0:T(8,128)(2,1)} %copy-done.13, bf16[176,2048]{1,0:T(8,128)(2,1)} %copy-done.14, ...), custom_call_target="tpu_custom_call" | custom-call | bytes 17301504 | tf_op jit(solution)/shard_map/place_blocks/pallas_call | solution.py:387
  443.6 6.8 %place_blocks.5 = f32[3,2048,256]{2,1,0:T(8,128)} custom-call(s32[8]{0:T(128)} %constant.128.clone.color_ref, s32[8]{0:T(128)} %stack.127.where_ref, bf16[256,768]{1,0:T(8,128)(2,1)} %copy-done.11, bf16[256,768]{1,0:T(8,128)(2,1)} %copy-done.19, bf16[256,768]{1,0:T(8,128)(2,1)} %copy-done.21, bf16[256,768]{1,0:T(8,128)(2,1)} %copy-done.22, ...), custom_call_target="tpu_custom_call" | custom-call | bytes 9437184 | tf_op jit(solution)/shard_map/place_blocks/pallas_call | solution.py:387
  450.3 16.0 %reduce-scatter.8.cloned.1.call-done.g_ref = bf16[256,2048]{1,0:T(8,128)(2,1)} async-done(((bf16[2048,2048]{1,0:T(8,128)(2,1)}), bf16[256,2048]{1,0:T(8,128)(2,1)}) %reduce-scatter.8.cloned.1.call-update) | async-done | bytes 1048592 | tf_op jit(solution)/shard_map/reduce_scatter | solution.py:671
  466.3 5.1 %tail.1 = (f32[256,1,2048]{2,1,0:T(1,128)}, f32[4,2048]{1,0:T(4,128)}) custom-call(bf16[256,2048]{1,0:T(8,128)(2,1)} %bitcast.108, bf16[256,2048]{1,0:T(8,128)(2,1)} %reduce-scatter.8.cloned.1.call-done.g_ref, bf16[256,2048]{1,0:T(8,128)(2,1)} %bitcast_select_fusion.c_ref, f32[1,2048]{1,0:T(1,128)} %bitcast.128, f32[1,2048]{1,0:T(1,128)} %bitcast.129), custom_call_target="tpu_custom_call" | custom-call | tf_op jit(solution)/shard_map/tail/pallas_call | solution.py:564
  473.7 3.9 collective-permute-done.33
  478.1 4.4 collective-permute-done.34
  484.1 2.4 collective-permute-done.35
  488.6 1.8 collective-permute-done.36
  (197 shorter events, 65.5 us)
Async XLA Ops:
  7.2 116.6 %copy-start = (bf16[704,2048]{1,0:T(8,128)(2,1)S(1)}, bf16[704,2048]{1,0:T(8,128)(2,1)}, u32[]{:S(2)}) copy-start(bf16[704,2048]{1,0:T(8,128)(2,1)} %param.23) | copy-start | bytes 8650756
  7.2 91.7 %all-gather.3.cloned.1.call-start = ((), (), s32[]{:S(2)}) async-start(), calls=%async_computation.3 | async-start | bytes 9437184 | tf_op jit(solution)/shard_map/all_gather | solution.py:644
  13.9 167.1 %all-gather.5.cloned.1.call-start = ((), (), s32[]{:S(2)}) async-start(), calls=%async_computation.4 | async-start | bytes 9437184 | tf_op jit(solution)/shard_map/all_gather | solution.py:645
  17.5 291.4 %reduce-scatter.4.cloned.1.call-start = ((), (), s32[]{:S(2)}) async-start(), calls=%async_computation.5 | async-start | bytes 9437184 | tf_op jit(solution)/shard_map/reduce_scatter | solution.py:671
  18.6 90.4 %copy-start.26 = (s32[16,1,128]{2,1,0:T(1,128)}, s32[16,1,128]{2,1,0:T(1,128)S(1)}, u32[]{:S(2)}) copy-start(s32[16,1,128]{2,1,0:T(1,128)S(1)} %broadcast_maximum_fusion.start_ref) | copy-start | bytes 24580
  132.7 246.2 %reduce-scatter.6.cloned.1.call-start = ((), (), s32[]{:S(2)}) async-start(), calls=%async_computation.6 | async-start | bytes 9437184 | tf_op jit(solution)/shard_map/reduce_scatter | solution.py:671
  195.8 270.5 %reduce-scatter.8.cloned.1.call-start = ((), (), s32[]{:S(2)}) async-start(), calls=%async_computation.7 | async-start | bytes 9437184 | tf_op jit(solution)/shard_map/reduce_scatter | solution.py:671
  200.1 22.0 %slice-start = ((s8[8388608]{0:T(1024)(128)(4,1)}), s8[4194304]{0:T(1024)(128)(4,1)S(1)}, s32[]{:S(2)}) async-start(s8[8388608]{0:T(1024)(128)(4,1)} %bitcast.109), calls=%async_computation.8 | async-start | bytes 8388608
  201.2 26.8 %collective-permute-start = (bf16[240,2048]{1,0:T(8,128)(2,1)}, bf16[240,2048]{1,0:T(8,128)(2,1)}, u32[]{:S(2)}, u32[]{:S(2)}) collective-permute-start(bf16[240,2048]{1,0:T(8,128)(2,1)} %bitcast.13), channel_id=1, source_target_pairs={{0,8},{8,0},{16,24},{24,16},{1,9},{9,1},{17,25},{25,17},{2,10},{10... | collective-permute-start | bytes 2949128 | tf_op jit(solution)/shard_map/ppermute | solution.py:354
  205.6 24.1 %collective-permute-start.1 = (bf16[240,2048]{1,0:T(8,128)(2,1)}, bf16[240,2048]{1,0:T(8,128)(2,1)}, u32[]{:S(2)}, u32[]{:S(2)}) collective-permute-start(bf16[240,2048]{1,0:T(8,128)(2,1)} %bitcast.16), channel_id=1, source_target_pairs={{0,16},{8,24},{16,0},{24,8},{1,17},{9,25},{17,1},{25,9},{2,18},{10... | collective-permute-start | bytes 2949128 | tf_op jit(solution)/shard_map/ppermute | solution.py:354
  231.3 12.9 %collective-permute-start.2 = (bf16[120,2048]{1,0:T(8,128)(2,1)S(1)}, bf16[120,2048]{1,0:T(8,128)(2,1)S(1)}, u32[]{:S(2)}, u32[]{:S(2)}) collective-permute-start(bf16[120,2048]{1,0:T(8,128)(2,1)S(1)} %constant_dynamic-slice_fusion.11), channel_id=1, source_target_pairs={{0,16},{8,24},{16,0},{24,8},{1,17},{9,25},{17,1},{25,9},{2,18},{10... | collective-permute-start | bytes 1474568 | tf_op jit(solution)/shard_map/ppermute | solution.py:354
  232.3 12.5 %collective-permute-start.3 = (bf16[120,2048]{1,0:T(8,128)(2,1)S(1)}, bf16[120,2048]{1,0:T(8,128)(2,1)S(1)}, u32[]{:S(2)}, u32[]{:S(2)}) collective-permute-start(bf16[120,2048]{1,0:T(8,128)(2,1)S(1)} %constant_dynamic-slice_fusion.8), channel_id=1, source_target_pairs={{0,8},{8,0},{16,24},{24,16},{1,9},{9,1},{17,25},{25,17},{2,10},{10... | collective-permute-start | bytes 1474568 | tf_op jit(solution)/shard_map/ppermute | solution.py:354
  245.7 14.6 %collective-permute-start.4 = (bf16[120,2048]{1,0:T(8,128)(2,1)S(1)}, bf16[120,2048]{1,0:T(8,128)(2,1)S(1)}, u32[]{:S(2)}, u32[]{:S(2)}) collective-permute-start(bf16[120,2048]{1,0:T(8,128)(2,1)S(1)} %add_convert_fusion.7.refs_0_), channel_id=1, source_target_pairs={{0,16},{8,24},{16,0},{24,8},{1,17},{9,25},{17,1},{25,9},{2,18},{10... | collective-permute-start | bytes 1474568 | tf_op jit(solution)/shard_map/ppermute | solution.py:354
  246.8 13.5 %collective-permute-start.5 = (bf16[120,2048]{1,0:T(8,128)(2,1)}, bf16[120,2048]{1,0:T(8,128)(2,1)S(1)}, u32[]{:S(2)}, u32[]{:S(2)}) collective-permute-start(bf16[120,2048]{1,0:T(8,128)(2,1)} %add_convert_fusion.6.refs_4_), channel_id=1, source_target_pairs={{0,8},{8,0},{16,24},{24,16},{1,9},{9,1},{17,25},{25,17},{2,10},{10... | collective-permute-start | bytes 1474568 | tf_op jit(solution)/shard_map/ppermute | solution.py:354
  260.3 48.6 %collective-permute-start.6 = (bf16[120,2048]{1,0:T(8,128)(2,1)S(1)}, bf16[120,2048]{1,0:T(8,128)(2,1)}, u32[]{:S(2)}, u32[]{:S(2)}) collective-permute-start(bf16[120,2048]{1,0:T(8,128)(2,1)S(1)} %add_convert_fusion.7.refs_0_), channel_id=1, source_target_pairs={{0,8},{8,0},{16,24},{24,16},{1,9},{9,1},{17,25},{25,17},{2,10},{10... | collective-permute-start | bytes 1474568 | tf_op jit(solution)/shard_map/ppermute | solution.py:354
  261.0 47.9 %collective-permute-start.7 = (bf16[120,2048]{1,0:T(8,128)(2,1)}, bf16[120,2048]{1,0:T(8,128)(2,1)}, u32[]{:S(2)}, u32[]{:S(2)}) collective-permute-start(bf16[120,2048]{1,0:T(8,128)(2,1)} %add_convert_fusion.6.refs_4_), channel_id=1, source_target_pairs={{0,16},{8,24},{16,0},{24,8},{1,17},{9,25},{17,1},{25,9},{2,18},{10... | collective-permute-start | bytes 1474568 | tf_op jit(solution)/shard_map/ppermute | solution.py:354
  261.9 40.4 %collective-permute-start.8 = (bf16[352,2048]{1,0:T(8,128)(2,1)}, bf16[352,2048]{1,0:T(8,128)(2,1)}, u32[]{:S(2)}, u32[]{:S(2)}) collective-permute-start(bf16[352,2048]{1,0:T(8,128)(2,1)} %constant_dynamic-slice_fusion.7), channel_id=1, source_target_pairs={{0,8},{8,0},{16,24},{24,16},{1,9},{9,1},{17,25},{25,17},{2,10},{10... | collective-permute-start | bytes 4325384 | tf_op jit(solution)/shard_map/ppermute | solution.py:354
  262.9 42.2 %collective-permute-start.9 = (bf16[352,2048]{1,0:T(8,128)(2,1)S(1)}, bf16[352,2048]{1,0:T(8,128)(2,1)}, u32[]{:S(2)}, u32[]{:S(2)}) collective-permute-start(bf16[352,2048]{1,0:T(8,128)(2,1)S(1)} %constant_dynamic-slice_fusion.6), channel_id=1, source_target_pairs={{0,16},{8,24},{16,0},{24,8},{1,17},{9,25},{17,1},{25,9},{2,18},{10... | collective-permute-start | bytes 4325384 | tf_op jit(solution)/shard_map/ppermute | solution.py:354
  308.9 30.7 %collective-permute-start.10 = (bf16[176,2048]{1,0:T(8,128)(2,1)}, bf16[176,2048]{1,0:T(8,128)(2,1)}, u32[]{:S(2)}, u32[]{:S(2)}) collective-permute-start(bf16[176,2048]{1,0:T(8,128)(2,1)} %constant_dynamic-slice_fusion.5), channel_id=1, source_target_pairs={{0,16},{8,24},{16,0},{24,8},{1,17},{9,25},{17,1},{25,9},{2,18},{10... | collective-permute-start | bytes 2162696 | tf_op jit(solution)/shard_map/ppermute | solution.py:354
  309.3 32.5 %collective-permute-start.11 = (bf16[176,2048]{1,0:T(8,128)(2,1)}, bf16[176,2048]{1,0:T(8,128)(2,1)}, u32[]{:S(2)}, u32[]{:S(2)}) collective-permute-start(bf16[176,2048]{1,0:T(8,128)(2,1)} %constant_dynamic-slice_fusion.4), channel_id=1, source_target_pairs={{0,8},{8,0},{16,24},{24,16},{1,9},{9,1},{17,25},{25,17},{2,10},{10... | collective-permute-start | bytes 2162696 | tf_op jit(solution)/shard_map/ppermute | solution.py:354
  311.4 31.8 %collective-permute-start.12 = (bf16[120,2048]{1,0:T(8,128)(2,1)}, bf16[120,2048]{1,0:T(8,128)(2,1)S(1)}, u32[]{:S(2)}, u32[]{:S(2)}) collective-permute-start(bf16[120,2048]{1,0:T(8,128)(2,1)} %copy-done.16), channel_id=1, source_target_pairs={{0,8},{8,0},{16,24},{24,16},{1,9},{9,1},{17,25},{25,17},{2,10},{10... | collective-permute-start | bytes 1474568 | tf_op jit(solution)/shard_map/ppermute | solution.py:354
  311.5 31.8 %collective-permute-start.13 = (bf16[120,2048]{1,0:T(8,128)(2,1)}, bf16[120,2048]{1,0:T(8,128)(2,1)}, u32[]{:S(2)}, u32[]{:S(2)}) collective-permute-start(bf16[120,2048]{1,0:T(8,128)(2,1)} %copy-done.17), channel_id=1, source_target_pairs={{0,16},{8,24},{16,0},{24,8},{1,17},{9,25},{17,1},{25,9},{2,18},{10... | collective-permute-start | bytes 1474568 | tf_op jit(solution)/shard_map/ppermute | solution.py:354
  343.3 14.4 %collective-permute-start.14 = (bf16[176,2048]{1,0:T(8,128)(2,1)}, bf16[176,2048]{1,0:T(8,128)(2,1)S(1)}, u32[]{:S(2)}, u32[]{:S(2)}) collective-permute-start(bf16[176,2048]{1,0:T(8,128)(2,1)} %add_convert_fusion.5.refs_0_), channel_id=1, source_target_pairs={{0,16},{8,24},{16,0},{24,8},{1,17},{9,25},{17,1},{25,9},{2,18},{10... | collective-permute-start | bytes 2162696 | tf_op jit(solution)/shard_map/ppermute | solution.py:354
  343.4 15.2 %collective-permute-start.15 = (bf16[176,2048]{1,0:T(8,128)(2,1)S(1)}, bf16[176,2048]{1,0:T(8,128)(2,1)}, u32[]{:S(2)}, u32[]{:S(2)}) collective-permute-start(bf16[176,2048]{1,0:T(8,128)(2,1)S(1)} %add_convert_fusion.4.refs_4_), channel_id=1, source_target_pairs={{0,8},{8,0},{16,24},{24,16},{1,9},{9,1},{17,25},{25,17},{2,10},{10... | collective-permute-start | bytes 2162696 | tf_op jit(solution)/shard_map/ppermute | solution.py:354
  360.2 14.8 %collective-permute-start.17 = (bf16[512,768]{1,0:T(8,128)(2,1)S(1)}, bf16[512,768]{1,0:T(8,128)(2,1)S(1)}, u32[]{:S(2)}, u32[]{:S(2)}) collective-permute-start(bf16[512,768]{1,0:T(8,128)(2,1)S(1)} %get-tuple-element.294), channel_id=1, source_target_pairs={{0,16},{8,24},{16,0},{24,8},{1,17},{9,25},{17,1},{25,9},{2,18},{10... | collective-permute-start | bytes 2359304 | tf_op jit(solution)/shard_map/ppermute | solution.py:354
  361.6 14.5 %collective-permute-start.16 = (bf16[512,768]{1,0:T(8,128)(2,1)S(1)}, bf16[512,768]{1,0:T(8,128)(2,1)}, u32[]{:S(2)}, u32[]{:S(2)}) collective-permute-start(bf16[512,768]{1,0:T(8,128)(2,1)S(1)} %get-tuple-element.295), channel_id=1, source_target_pairs={{0,8},{8,0},{16,24},{24,16},{1,9},{9,1},{17,25},{25,17},{2,10},{10... | collective-permute-start | bytes 2359304 | tf_op jit(solution)/shard_map/ppermute | solution.py:354
  379.0 27.9 %collective-permute-start.19 = (bf16[176,2048]{1,0:T(8,128)(2,1)}, bf16[176,2048]{1,0:T(8,128)(2,1)S(1)}, u32[]{:S(2)}, u32[]{:S(2)}) collective-permute-start(bf16[176,2048]{1,0:T(8,128)(2,1)} %add_convert_fusion.5.refs_0_), channel_id=1, source_target_pairs={{0,8},{8,0},{16,24},{24,16},{1,9},{9,1},{17,25},{25,17},{2,10},{10... | collective-permute-start | bytes 2162696 | tf_op jit(solution)/shard_map/ppermute | solution.py:354
  380.1 26.9 %collective-permute-start.20 = (bf16[176,2048]{1,0:T(8,128)(2,1)}, bf16[176,2048]{1,0:T(8,128)(2,1)S(1)}, u32[]{:S(2)}, u32[]{:S(2)}) collective-permute-start(bf16[176,2048]{1,0:T(8,128)(2,1)} %copy-done.6), channel_id=1, source_target_pairs={{0,16},{8,24},{16,0},{24,8},{1,17},{9,25},{17,1},{25,9},{2,18},{10... | collective-permute-start | bytes 2162696 | tf_op jit(solution)/shard_map/ppermute | solution.py:354
  381.4 17.0 %collective-permute-start.18 = (f32[6,128]{1,0:T(8,128)S(1)}, f32[6,128]{1,0:T(8,128)S(1)}, u32[]{:S(2)}, u32[]{:S(2)}) collective-permute-start(f32[6,128]{1,0:T(8,128)S(1)} %bitcast.131), channel_id=1, source_target_pairs={{0,8},{8,0},{16,24},{24,16},{1,9},{9,1},{17,25},{25,17},{2,10},{10... | collective-permute-start | bytes 9224 | tf_op jit(solution)/shard_map/ppermute | solution.py:354
  381.8 22.8 %collective-permute-start.21 = (bf16[256,768]{1,0:T(8,128)(2,1)S(1)}, bf16[256,768]{1,0:T(8,128)(2,1)S(1)}, u32[]{:S(2)}, u32[]{:S(2)}) collective-permute-start(bf16[256,768]{1,0:T(8,128)(2,1)S(1)} %constant_dynamic-slice_fusion.2), channel_id=1, source_target_pairs={{0,16},{8,24},{16,0},{24,8},{1,17},{9,25},{17,1},{25,9},{2,18},{10... | collective-permute-start | bytes 1179656 | tf_op jit(solution)/shard_map/ppermute | solution.py:354
  383.1 23.7 %collective-permute-start.22 = (bf16[256,768]{1,0:T(8,128)(2,1)}, bf16[256,768]{1,0:T(8,128)(2,1)S(1)}, u32[]{:S(2)}, u32[]{:S(2)}) collective-permute-start(bf16[256,768]{1,0:T(8,128)(2,1)} %constant_dynamic-slice_fusion), channel_id=1, source_target_pairs={{0,8},{8,0},{16,24},{24,16},{1,9},{9,1},{17,25},{25,17},{2,10},{10... | collective-permute-start | bytes 1179656 | tf_op jit(solution)/shard_map/ppermute | solution.py:354
  398.4 28.7 %collective-permute-start.24 = (bf16[176,2048]{1,0:T(8,128)(2,1)}, bf16[176,2048]{1,0:T(8,128)(2,1)}, u32[]{:S(2)}, u32[]{:S(2)}) collective-permute-start(bf16[176,2048]{1,0:T(8,128)(2,1)} %copy-done.13), channel_id=1, source_target_pairs={{0,8},{8,0},{16,24},{24,16},{1,9},{9,1},{17,25},{25,17},{2,10},{10... | collective-permute-start | bytes 2162696 | tf_op jit(solution)/shard_map/ppermute | solution.py:354
  404.7 22.4 %collective-permute-start.25 = (bf16[176,2048]{1,0:T(8,128)(2,1)}, bf16[176,2048]{1,0:T(8,128)(2,1)}, u32[]{:S(2)}, u32[]{:S(2)}) collective-permute-start(bf16[176,2048]{1,0:T(8,128)(2,1)} %collective-permute-done.15.refs_5_), channel_id=1, source_target_pairs={{0,16},{8,24},{16,0},{24,8},{1,17},{9,25},{17,1},{25,9},{2,18},{10... | collective-permute-start | bytes 2162696 | tf_op jit(solution)/shard_map/ppermute | solution.py:354
  406.2 35.1 %copy-start.11 = (bf16[256,768]{1,0:T(8,128)(2,1)}, bf16[256,768]{1,0:T(8,128)(2,1)S(1)}, u32[]{:S(2)}) copy-start(bf16[256,768]{1,0:T(8,128)(2,1)S(1)} %add_convert_fusion.9.refs_0_) | copy-start | bytes 1179652
  406.9 34.4 %copy-start.12 = (bf16[256,768]{1,0:T(8,128)(2,1)}, bf16[256,768]{1,0:T(8,128)(2,1)S(1)}, u32[]{:S(2)}) copy-start(bf16[256,768]{1,0:T(8,128)(2,1)S(1)} %add_convert_fusion.8.refs_4_) | copy-start | bytes 1179652
  407.9 19.2 %collective-permute-start.26 = (bf16[256,768]{1,0:T(8,128)(2,1)S(1)}, bf16[256,768]{1,0:T(8,128)(2,1)S(1)}, u32[]{:S(2)}, u32[]{:S(2)}) collective-permute-start(bf16[256,768]{1,0:T(8,128)(2,1)S(1)} %add_convert_fusion.9.refs_0_), channel_id=1, source_target_pairs={{0,16},{8,24},{16,0},{24,8},{1,17},{9,25},{17,1},{25,9},{2,18},{10... | collective-permute-start | bytes 1179656 | tf_op jit(solution)/shard_map/ppermute | solution.py:354
  408.6 19.3 %collective-permute-start.27 = (bf16[256,768]{1,0:T(8,128)(2,1)S(1)}, bf16[256,768]{1,0:T(8,128)(2,1)S(1)}, u32[]{:S(2)}, u32[]{:S(2)}) collective-permute-start(bf16[256,768]{1,0:T(8,128)(2,1)S(1)} %add_convert_fusion.8.refs_4_), channel_id=1, source_target_pairs={{0,8},{8,0},{16,24},{24,16},{1,9},{9,1},{17,25},{25,17},{2,10},{10... | collective-permute-start | bytes 1179656 | tf_op jit(solution)/shard_map/ppermute | solution.py:354
  410.2 16.8 %collective-permute-start.23 = (f32[6,128]{1,0:T(8,128)S(1)}, f32[6,128]{1,0:T(8,128)S(1)}, u32[]{:S(2)}, u32[]{:S(2)}) collective-permute-start(f32[6,128]{1,0:T(8,128)S(1)} %add.374), channel_id=1, source_target_pairs={{0,16},{8,24},{16,0},{24,8},{1,17},{9,25},{17,1},{25,9},{2,18},{10... | collective-permute-start | bytes 9224 | tf_op jit(solution)/shard_map/ppermute | solution.py:354
  427.9 13.5 %collective-permute-start.28 = (bf16[256,768]{1,0:T(8,128)(2,1)S(1)}, bf16[256,768]{1,0:T(8,128)(2,1)S(1)}, u32[]{:S(2)}, u32[]{:S(2)}) collective-permute-start(bf16[256,768]{1,0:T(8,128)(2,1)S(1)} %add_convert_fusion.9.refs_0_), channel_id=1, source_target_pairs={{0,8},{8,0},{16,24},{24,16},{1,9},{9,1},{17,25},{25,17},{2,10},{10... | collective-permute-start | bytes 1179656 | tf_op jit(solution)/shard_map/ppermute | solution.py:354
  429.2 12.2 %collective-permute-start.29 = (bf16[256,768]{1,0:T(8,128)(2,1)S(1)}, bf16[256,768]{1,0:T(8,128)(2,1)S(1)}, u32[]{:S(2)}, u32[]{:S(2)}) collective-permute-start(bf16[256,768]{1,0:T(8,128)(2,1)S(1)} %collective-permute-done.26.refs_1_), channel_id=1, source_target_pairs={{0,8},{8,0},{16,24},{24,16},{1,9},{9,1},{17,25},{25,17},{2,10},{10... | collective-permute-start | bytes 1179656 | tf_op jit(solution)/shard_map/ppermute | solution.py:354
  429.9 11.5 %collective-permute-start.30 = (bf16[256,768]{1,0:T(8,128)(2,1)S(1)}, bf16[256,768]{1,0:T(8,128)(2,1)S(1)}, u32[]{:S(2)}, u32[]{:S(2)}) collective-permute-start(bf16[256,768]{1,0:T(8,128)(2,1)S(1)} %add_convert_fusion.8.refs_4_), channel_id=1, source_target_pairs={{0,16},{8,24},{16,0},{24,8},{1,17},{9,25},{17,1},{25,9},{2,18},{10... | collective-permute-start | bytes 1179656 | tf_op jit(solution)/shard_map/ppermute | solution.py:354
  431.2 10.7 %collective-permute-start.31 = (bf16[256,768]{1,0:T(8,128)(2,1)S(1)}, bf16[256,768]{1,0:T(8,128)(2,1)S(1)}, u32[]{:S(2)}, u32[]{:S(2)}) collective-permute-start(bf16[256,768]{1,0:T(8,128)(2,1)S(1)} %collective-permute-done.27.refs_5_), channel_id=1, source_target_pairs={{0,16},{8,24},{16,0},{24,8},{1,17},{9,25},{17,1},{25,9},{2,18},{10... | collective-permute-start | bytes 1179656 | tf_op jit(solution)/shard_map/ppermute | solution.py:354
  443.6 49.3 %copy-start.1 = (bf16[704,2048]{1,0:T(8,128)(2,1)S(1)}, bf16[704,2048]{1,0:T(8,128)(2,1)}, u32[]{:S(2)}) copy-start(bf16[704,2048]{1,0:T(8,128)(2,1)} %param.23) | copy-start | bytes 8650756
  471.4 1.4 collective-permute-start.32
  473.6 4.0 collective-permute-start.33
  477.6 4.9 collective-permute-start.34
  482.5 4.0 collective-permute-start.35
  486.5 4.0 collective-permute-start.36
  (29 other events, 202.5 us)
Sparse Core Ops, SparseCore 0:
  14.1 84.7 all-gather.2
  100.5 80.5 all-gather.4
  183.3 88.0 reduce-scatter.3
  274.1 88.1 reduce-scatter.5
  379.1 87.1 reduce-scatter.7

commit v3 on v2

--- a/solution.py
+++ b/solution.py
@@ -723,12 +723,13 @@
     sum_gate_up.arrive()
     sum_qkv = DpSum(fence(sum_qkv, sum_gate_up))
     bias_sums = jnp.sum(grad_proj, axis=0, dtype=F32).reshape(-1, 128)
+    normed_partial, attn_sum, bias_sums, _ = fence(
+        (normed_partial, attn_sum, bias_sums, sum_qkv.out)
+    )
+    grad_normed = scattered(normed_partial)
     sum_qkv.send()
     sum_qkv.arrive()
-    normed_partial, attn_sum, bias_sums = fence(
-        (normed_partial, attn_sum, bias_sums), sum_qkv
-    )
-    grad_normed = scattered(normed_partial)
+    fence((), sum_gate_up, sum_qkv)
     sum_gate_up.send()
     sum_qkv.send()
     bias_sums = sum_small(bias_sums, "dp", [0])

time: 510 us -> 506 us (level)
  starting transfers between devices: 41.1 us -> 48.4 us
    reduce_scatter x3, waiting for transfers between devices: 16 us -> 2.19 us  [scattered(): return lax.psum_scatter(partial, 'mp', scatter_dimension=0, tiled=True)]
    ppermute x37, waiting for transfers between devices: 51.9 us -> 61 us  [swap(): return lax.ppermute(values, name, [(i, i ^ 1 << bit) for i in range(size)])]
    ppermute x37, starting transfers between devices: 40.3 us -> 47.5 us  [swap(): return lax.ppermute(values, name, [(i, i ^ 1 << bit) for i in range(size)])]
  transfers between devices with their start and end apart: 42 -> 42, of which waited for: 21 -> 20; matrix products, arithmetic and copies ran while one was open for 31% -> 31% of each run, Pallas kernels for 25% -> 24%
where the time goes in v3:
time: 506 us; the launch traced here: 497 us
  waiting for transfers between devices  139 us (27%)
  Pallas kernels  127 us (25%)
  matrix products  105 us (21%)
  starting transfers between devices  48.4 us (10%)
  other arithmetic  43.9 us (9%)
  local copies, waits for them, and re-layouts  17 us (3%)
  between operations  16.2 us (3%)
    all_gather x1, waiting for transfers between devices, local(): gathered = lax.all_gather(normed, 'mp', axis=0, tiled=True)  73.5 us
    ppermute x37, waiting for transfers between devices, swap(): return lax.ppermute(values, name, [(i, i ^ 1 << bit) for i in range(size)])  61 us
    ppermute x37, starting transfers between devices, swap(): return lax.ppermute(values, name, [(i, i ^ 1 << bit) for i in range(size)])  47.5 us
    dot_general x5, matrix products, token_sum(): lax.dot_general(left, right, (((0,), (0,)), ((), ())), preferred_element_...  46.1 us
    dot_general x4, matrix products, turned_product(): lax.dot_general(left, right, (((1,), (1,)), ((), ())), preferred_element_...  43.2 us
    pallas_call x1, Pallas kernels, attend_back(): pl.pallas_call(attend_back_kernel, grid_spec=pltpu.PrefetchScalarGridSpec...  34.9 us
    pallas_call x1, Pallas kernels, back_products(): pl.pallas_call(back_products_kernel, grid=(length // rows,), in_specs=[pl...  26.2 us
    pallas_call x1, Pallas kernels, attend(): pl.pallas_call(attend_kernel, grid_spec=pltpu.PrefetchScalarGridSpec(num_...  24.6 us
  transfers between devices with their start and end apart: 42, of which 20 were waited for; matrix products, arithmetic and copies ran while one was open for 31% of the time, Pallas kernels for 24%

profile of v3, /device:TPU:0, one launch (start us, length us, event | category | flops | bytes accessed | tf_op | source)
XLA Modules:
  0.0 497.1 jit_solution(7810310078774475910)
XLA Ops:
  7.2 2.3 fusion.16
  11.2 2.7 fusion.12
  15.2 2.3 bitcast_select_fusion.c_ref
  19.6 5.8 %fusion.19 = (f32[2048,128]{1,0:T(8,128)}, f32[2048,128]{1,0:T(8,128)}, f32[2048,128]{1,0:T(8,128)}) fusion(f32[128]{0:T(128)S(1)} %compare_select_fusion.5, f32[2048]{0:T(1024)S(1)} %fusion.23, pred[128]{0:T(512)(128)(4,1)S(1)} %get-tuple-element.330, pred[128]{0:T(512)(128)(4,1)S(1)} %get-tuple-element.331), kind=kLoop, calls=%fused_computation.50 | loop fusion | flops 1048576 | bytes 3154688 | tf_op jit(solution)/shard_map/jit(_where)/select_n | solution.py:41
  25.4 73.5 %all-gather.3.cloned.1.call-done.x_ref = bf16[2048,2048]{1,0:T(8,128)(2,1)} async-done(((bf16[256,2048]{1,0:T(8,128)(2,1)}), bf16[2048,2048]{1,0:T(8,128)(2,1)}) %all-gather.3.cloned.1.call-update) | async-done | bytes 8388624 | tf_op jit(solution)/shard_map/all_gather | solution.py:644
  98.9 10.1 %fusion.6 = f32[2048,704]{1,0:T(8,128)S(1)} fusion(bf16[2048,2048]{1,0:T(8,128)(2,1)} %all-gather.3.cloned.1.call-done.x_ref, bf16[2,704,2048]{2,1,0:T(8,128)(2,1)} %bitcast.113), kind=kOutput, calls=%fused_computation.24 | convolution fusion | flops 5905580032 | bytes 17039360 | tf_op jit(solution)/shard_map/dot_general | solution.py:661
  109.0 13.1 %multiply_convert_fusion = (bf16[2048,704]{1,0:T(8,128)(2,1)S(1)}, f32[2048,704]{1,0:T(8,128)}) fusion(f32[2048,704]{1,0:T(8,128)S(1)} %fusion.6, bf16[2048,2048]{1,0:T(8,128)(2,1)S(1)} %copy-done.33, bf16[2,704,2048]{2,1,0:T(8,128)(2,1)} %bitcast.114), kind=kOutput, calls=%fused_computation.10 | convolution fusion | flops 5914230784 | bytes 25690112 | tf_op jit(solution)/shard_map/dot_general | solution.py:661
  123.8 8.9 %convolution_convert_fusion.1 = bf16[2048,2048]{1,0:T(8,128)(2,1)} fusion(bf16[2048,704]{1,0:T(8,128)(2,1)S(1)} %get-tuple-element.328, bf16[704,2048]{1,0:T(8,128)(2,1)S(1)} %copy-done), kind=kOutput, calls=%fused_computation.3 | convolution fusion | flops 5909774336 | bytes 14155776 | tf_op jit(solution)/shard_map/dot_general | solution.py:658
  133.2 13.3 %project.1 = (bf16[2048,256]{1,0:T(8,128)(2,1)}, bf16[2048,256]{1,0:T(8,128)(2,1)}, bf16[2048,256]{1,0:T(8,128)(2,1)}) custom-call(bf16[2048,2048]{1,0:T(8,128)(2,1)} %all-gather.3.cloned.1.call-done.x_ref, bf16[3,2048,256]{2,1,0:T(8,128)(2,1)} %bitcast.116, bf16[3,256]{1,0:T(4,128)(2,1)} %b_ref.1, f32[2048,128]{1,0:T(8,128)} %get-tuple-element.157.cos_ref, ...), custom_call_target="tpu_custom_call" | custom-call | flops 6442450944 | bytes 14680064 | tf_op jit(solution)/shard_map/project/pallas_call | solution.py:78
  146.5 24.6 %attend.1 = (bf16[2048,256]{1,0:T(8,128)(2,1)}, f32[16,1,512]{2,1,0:T(1,128)}) custom-call(s32[16]{0:T(128)} %and_select_fusion.first_ref, bf16[2048,256]{1,0:T(8,128)(2,1)} %get-tuple-element.160.q_ref, bf16[2048,256]{1,0:T(8,128)(2,1)} %get-tuple-element.161.k_ref, bf16[2048,256]{1,0:T(8,128)(2,1)} %get-tuple-element.162.v_ref, s32[16,1,128]{2,1,0:T(1,128)} %copy-done.30), custom_call_target="tpu_custom_call" | custom-call | flops 8589934592 | bytes 4194304 | tf_op jit(solution)/shard_map/attend/pallas_call | solution.py:181
  171.1 7.3 %convolution_convert_fusion = bf16[2048,2048]{1,0:T(8,128)(2,1)} fusion(bf16[2048,256]{1,0:T(8,128)(2,1)} %get-tuple-element.164.o_ref, bf16[256,2048]{1,0:T(8,128)(2,1)} %param.21), kind=kOutput, calls=%fused_computation.2 | convolution fusion | flops 2151677952 | bytes 10485760 | tf_op jit(solution)/shard_map/dot_general | solution.py:658
  178.4 2.6 all-gather.5.cloned.1.call-done
  181.0 7.2 %convolution_convert_fusion.8 = bf16[256,2048]{1,0:T(8,128)(2,1)} fusion(bf16[2048,256]{1,0:T(8,128)(2,1)} %get-tuple-element.164.o_ref, bf16[2048,2048]{1,0:T(8,128)(2,1)} %all-gather.5.cloned.1.call-done), kind=kOutput, calls=%fused_computation.31 | convolution fusion | flops 2148007936 | bytes 10485760 | tf_op jit(solution)/shard_map/dot_general | solution.py:666
  188.2 7.6 %convolution_convert_fusion.6 = bf16[704,2048]{1,0:T(8,128)(2,1)} fusion(bf16[2048,704]{1,0:T(8,128)(2,1)S(1)} %copy-done.35, bf16[2048,2048]{1,0:T(8,128)(2,1)S(1)} %copy-done.3), kind=kOutput, calls=%fused_computation.20 | convolution fusion | flops 5907021824 | bytes 14155776 | tf_op jit(solution)/shard_map/dot_general | solution.py:666
  196.1 2.2 constant_dynamic-slice_fusion.10
  201.2 3.8 collective-permute-start
  205.1 15.3 %fusion.4 = (bf16[2048,704]{1,0:T(8,128)(2,1)}, bf16[2048,704]{1,0:T(8,128)(2,1)S(1)}) fusion(f32[2048,704]{1,0:T(8,128)} %copy-done.36, f32[2048,704]{1,0:T(8,128)} %get-tuple-element.329, bf16[2048,2048]{1,0:T(8,128)(2,1)} %all-gather.5.cloned.1.call-done, bf16[704,2048]{1,0:T(8,128)(2,1)S(1)} %copy-done), kind=kOutput, calls=%fused_computation.8 | convolution fusion | flops 5927206912 | bytes 28573696 | tf_op jit(solution)/shard_map/dot_general | solution.py:661
  221.6 4.7 convolution_convert_fusion.7.do_ref
  232.9 9.8 %convolution_convert_fusion.5 = bf16[704,2048]{1,0:T(8,128)(2,1)} fusion(bf16[2048,704]{1,0:T(8,128)(2,1)S(1)} %get-tuple-element.170.g_ref, bf16[2048,2048]{1,0:T(8,128)(2,1)} %all-gather.3.cloned.1.call-done.x_ref), kind=kOutput, calls=%fused_computation.19 | convolution fusion | flops 5907021824 | bytes 14155776 | tf_op jit(solution)/shard_map/dot_general | solution.py:666
  247.8 9.9 %convolution_convert_fusion.4 = bf16[704,2048]{1,0:T(8,128)(2,1)S(1)} fusion(bf16[2048,704]{1,0:T(8,128)(2,1)} %get-tuple-element.175.u_ref, bf16[2048,2048]{1,0:T(8,128)(2,1)} %all-gather.3.cloned.1.call-done.x_ref), kind=kOutput, calls=%fused_computation.18 | convolution fusion | flops 5907021824 | bytes 14155776 | tf_op jit(solution)/shard_map/dot_general | solution.py:666
  263.9 34.9 %attend_back.1.p_ref = bf16[2048,768]{1,0:T(8,128)(2,1)} custom-call(s32[16]{0:T(128)} %and_select_fusion.first_ref, bf16[2048,256]{1,0:T(8,128)(2,1)} %get-tuple-element.160.q_ref, bf16[2048,256]{1,0:T(8,128)(2,1)} %get-tuple-element.161.k_ref, bf16[2048,256]{1,0:T(8,128)(2,1)} %get-tuple-element.162.v_ref, ...), custom_call_target="tpu_custom_call" | custom-call | flops 21474836480 | bytes 8388608 | tf_op jit(solution)/shard_map/attend_back/pallas_call | solution.py:312
  298.9 3.0 collective-permute-done.8
  301.8 2.4 add_convert_fusion.1
  308.1 2.2 collective-permute-start.10
  310.4 1.9 collective-permute-start.12
  312.4 26.2 %back_products.1 = bf16[2048,2048]{1,0:T(8,128)(2,1)} custom-call(bf16[2048,768]{1,0:T(8,128)(2,1)} %attend_back.1.p_ref, bf16[3,2048,256]{2,1,0:T(8,128)(2,1)} %bitcast.117, bf16[2048,704]{1,0:T(8,128)(2,1)} %copy-done.5, bf16[2048,704]{1,0:T(8,128)(2,1)} %get-tuple-element.175.u_ref, bf16[2,704,2048]{2,1,0:T(8,128)(2,1)} %bitcast.115), custom_call_target="tpu_custom_call" | custom-call | tf_op jit(solution)/shard_map/back_products/pallas_call | solution.py:600
  338.7 2.2 add_convert_fusion.5.refs_0_
  342.3 2.0 collective-permute-start.14
  344.4 11.6 %convolution_convert_fusion.3 = bf16[2048,768]{1,0:T(8,128)(2,1)} fusion(bf16[2048,2048]{1,0:T(8,128)(2,1)} %all-gather.3.cloned.1.call-done.x_ref, bf16[2048,768]{1,0:T(8,128)(2,1)} %attend_back.1.p_ref), kind=kOutput, calls=%fused_computation.17 | convolution fusion | flops 6444023808 | bytes 14680064 | tf_op jit(solution)/shard_map/dot_general | solution.py:666
  356.1 2.6 convert_reduce_fusion
  359.9 2.2 reduce-scatter.6.cloned.1.call-done
  365.7 14.3 %collective-permute-done.18 = bf16[512,768]{1,0:T(8,128)(2,1)S(1)} collective-permute-done((bf16[512,768]{1,0:T(8,128)(2,1)}, bf16[512,768]{1,0:T(8,128)(2,1)S(1)}, u32[]{:S(2)}, u32[]{:S(2)}) %collective-permute-start.18) | collective-permute-done | bytes 786464 | tf_op jit(solution)/shard_map/ppermute | solution.py:354
  381.3 2.3 add_convert_fusion.2
  390.0 3.3 select_maximum_fusion
  397.1 15.5 %collective-permute-done.22 = bf16[256,768]{1,0:T(8,128)(2,1)S(1)} collective-permute-done((bf16[256,768]{1,0:T(8,128)(2,1)S(1)}, bf16[256,768]{1,0:T(8,128)(2,1)S(1)}, u32[]{:S(2)}, u32[]{:S(2)}) %collective-permute-start.22) | collective-permute-done | bytes 393248 | tf_op jit(solution)/shard_map/ppermute | solution.py:354
  417.4 7.2 %place_blocks.3 = (f32[704,2048]{1,0:T(8,128)}, f32[256,2048]{1,0:T(8,128)}) custom-call(s32[8]{0:T(128)} %constant.128.clone.color_ref, s32[8]{0:T(128)} %stack.109.where_ref, bf16[120,2048]{1,0:T(8,128)(2,1)} %copy-done.12, bf16[120,2048]{1,0:T(8,128)(2,1)} %copy-done.20, bf16[120,2048]{1,0:T(8,128)(2,1)} %collective-permute-done.6.refs_2_, ...), custom_call_target="tpu_custom_call" | custom-call | bytes 11796480 | tf_op jit(solution)/shard_map/place_blocks/pallas_call | solution.py:387
  424.7 6.8 %collective-permute-done.23 = f32[6,128]{1,0:T(8,128)S(1)} collective-permute-done((f32[6,128]{1,0:T(8,128)S(1)}, f32[6,128]{1,0:T(8,128)S(1)}, u32[]{:S(2)}, u32[]{:S(2)}) %collective-permute-start.23) | collective-permute-done | bytes 3104 | tf_op jit(solution)/shard_map/ppermute | solution.py:354
  431.5 2.3 collective-permute-done.27.refs_5_
  438.4 8.7 %place_blocks.4 = f32[2,704,2048]{2,1,0:T(8,128)} custom-call(s32[8]{0:T(128)} %constant.128.clone.color_ref, s32[8]{0:T(128)} %stack.118.where_ref, bf16[176,2048]{1,0:T(8,128)(2,1)} %add_convert_fusion.5.refs_0_, bf16[176,2048]{1,0:T(8,128)(2,1)} %collective-permute-done.14.refs_1_, bf16[176,2048]{1,0:T(8,128)(2,1)} %copy-done.18, ...), custom_call_target="tpu_custom_call" | custom-call | bytes 17301504 | tf_op jit(solution)/shard_map/place_blocks/pallas_call | solution.py:387
  447.1 2.7 collective-permute-done.29.refs_3_
  451.9 6.8 %place_blocks.5 = f32[3,2048,256]{2,1,0:T(8,128)} custom-call(s32[8]{0:T(128)} %constant.128.clone.color_ref, s32[8]{0:T(128)} %stack.127.where_ref, bf16[256,768]{1,0:T(8,128)(2,1)} %copy-done.13, bf16[256,768]{1,0:T(8,128)(2,1)} %copy-done.23, bf16[256,768]{1,0:T(8,128)(2,1)} %copy-done.25, bf16[256,768]{1,0:T(8,128)(2,1)} %copy-done.26, ...), custom_call_target="tpu_custom_call" | custom-call | bytes 9437184 | tf_op jit(solution)/shard_map/place_blocks/pallas_call | solution.py:387
  458.7 5.1 %tail.1 = (f32[256,1,2048]{2,1,0:T(1,128)}, f32[4,2048]{1,0:T(4,128)}) custom-call(bf16[256,2048]{1,0:T(8,128)(2,1)} %bitcast.108, bf16[256,2048]{1,0:T(8,128)(2,1)} %reduce-scatter.8.cloned.1.call-done.g_ref, bf16[256,2048]{1,0:T(8,128)(2,1)} %bitcast_select_fusion.c_ref, f32[1,2048]{1,0:T(1,128)} %bitcast.128, f32[1,2048]{1,0:T(1,128)} %bitcast.129), custom_call_target="tpu_custom_call" | custom-call | tf_op jit(solution)/shard_map/tail/pallas_call | solution.py:564
  465.9 7.0 %collective-permute-start.33 = (f32[4,2048]{1,0:T(4,128)S(1)}, f32[4,2048]{1,0:T(4,128)S(1)}, u32[]{:S(2)}, u32[]{:S(2)}) collective-permute-start(f32[4,2048]{1,0:T(4,128)S(1)} %add.414), channel_id=1, source_target_pairs={{0,2},{1,3},{2,0},{3,1},{4,6},{5,7},{6,4},{7,5},{8,10},{9,11},{10,... | collective-permute-start | bytes 98312 | tf_op jit(solution)/shard_map/ppermute | solution.py:354
  472.9 1.9 collective-permute-done.33
  474.8 2.6 collective-permute-start.34
  477.4 2.3 collective-permute-done.34
  481.1 2.6 collective-permute-done.35
  485.0 2.7 collective-permute-done.36
  (205 shorter events, 68.6 us)
Async XLA Ops:
  7.2 116.6 %copy-start = (bf16[704,2048]{1,0:T(8,128)(2,1)S(1)}, bf16[704,2048]{1,0:T(8,128)(2,1)}, u32[]{:S(2)}) copy-start(bf16[704,2048]{1,0:T(8,128)(2,1)} %param.23) | copy-start | bytes 8650756
  7.2 91.7 %all-gather.3.cloned.1.call-start = ((), (), s32[]{:S(2)}) async-start(), calls=%async_computation.3 | async-start | bytes 9437184 | tf_op jit(solution)/shard_map/all_gather | solution.py:644
  13.9 167.1 %all-gather.5.cloned.1.call-start = ((), (), s32[]{:S(2)}) async-start(), calls=%async_computation.4 | async-start | bytes 9437184 | tf_op jit(solution)/shard_map/all_gather | solution.py:645
  17.5 290.6 %reduce-scatter.4.cloned.1.call-start = ((), (), s32[]{:S(2)}) async-start(), calls=%async_computation.5 | async-start | bytes 9437184 | tf_op jit(solution)/shard_map/reduce_scatter | solution.py:671
  18.6 90.4 %copy-start.30 = (s32[16,1,128]{2,1,0:T(1,128)}, s32[16,1,128]{2,1,0:T(1,128)S(1)}, u32[]{:S(2)}) copy-start(s32[16,1,128]{2,1,0:T(1,128)S(1)} %broadcast_maximum_fusion.start_ref) | copy-start | bytes 24580
  132.7 229.4 %reduce-scatter.6.cloned.1.call-start = ((), (), s32[]{:S(2)}) async-start(), calls=%async_computation.6 | async-start | bytes 9437184 | tf_op jit(solution)/shard_map/reduce_scatter | solution.py:671
  195.8 262.8 %reduce-scatter.8.cloned.1.call-start = ((), (), s32[]{:S(2)}) async-start(), calls=%async_computation.7 | async-start | bytes 9437184 | tf_op jit(solution)/shard_map/reduce_scatter | solution.py:671
  201.2 26.3 %collective-permute-start = (bf16[240,2048]{1,0:T(8,128)(2,1)}, bf16[240,2048]{1,0:T(8,128)(2,1)}, u32[]{:S(2)}, u32[]{:S(2)}) collective-permute-start(bf16[240,2048]{1,0:T(8,128)(2,1)} %bitcast.13), channel_id=1, source_target_pairs={{0,8},{8,0},{16,24},{24,16},{1,9},{9,1},{17,25},{25,17},{2,10},{10... | collective-permute-start | bytes 2949128 | tf_op jit(solution)/shard_map/ppermute | solution.py:354
  205.0 24.1 %collective-permute-start.1 = (bf16[240,2048]{1,0:T(8,128)(2,1)}, bf16[240,2048]{1,0:T(8,128)(2,1)}, u32[]{:S(2)}, u32[]{:S(2)}) collective-permute-start(bf16[240,2048]{1,0:T(8,128)(2,1)} %bitcast.16), channel_id=1, source_target_pairs={{0,16},{8,24},{16,0},{24,8},{1,17},{9,25},{17,1},{25,9},{2,18},{10... | collective-permute-start | bytes 2949128 | tf_op jit(solution)/shard_map/ppermute | solution.py:354
  230.8 12.9 %collective-permute-start.2 = (bf16[120,2048]{1,0:T(8,128)(2,1)S(1)}, bf16[120,2048]{1,0:T(8,128)(2,1)S(1)}, u32[]{:S(2)}, u32[]{:S(2)}) collective-permute-start(bf16[120,2048]{1,0:T(8,128)(2,1)S(1)} %constant_dynamic-slice_fusion.11), channel_id=1, source_target_pairs={{0,16},{8,24},{16,0},{24,8},{1,17},{9,25},{17,1},{25,9},{2,18},{10... | collective-permute-start | bytes 1474568 | tf_op jit(solution)/shard_map/ppermute | solution.py:354
  232.6 12.2 %collective-permute-start.3 = (bf16[120,2048]{1,0:T(8,128)(2,1)S(1)}, bf16[120,2048]{1,0:T(8,128)(2,1)S(1)}, u32[]{:S(2)}, u32[]{:S(2)}) collective-permute-start(bf16[120,2048]{1,0:T(8,128)(2,1)S(1)} %constant_dynamic-slice_fusion.8), channel_id=1, source_target_pairs={{0,8},{8,0},{16,24},{24,16},{1,9},{9,1},{17,25},{25,17},{2,10},{10... | collective-permute-start | bytes 1474568 | tf_op jit(solution)/shard_map/ppermute | solution.py:354
  245.8 14.0 %collective-permute-start.4 = (bf16[120,2048]{1,0:T(8,128)(2,1)S(1)}, bf16[120,2048]{1,0:T(8,128)(2,1)S(1)}, u32[]{:S(2)}, u32[]{:S(2)}) collective-permute-start(bf16[120,2048]{1,0:T(8,128)(2,1)S(1)} %add_convert_fusion.7.refs_0_), channel_id=1, source_target_pairs={{0,16},{8,24},{16,0},{24,8},{1,17},{9,25},{17,1},{25,9},{2,18},{10... | collective-permute-start | bytes 1474568 | tf_op jit(solution)/shard_map/ppermute | solution.py:354
  246.3 13.5 %collective-permute-start.5 = (bf16[120,2048]{1,0:T(8,128)(2,1)}, bf16[120,2048]{1,0:T(8,128)(2,1)S(1)}, u32[]{:S(2)}, u32[]{:S(2)}) collective-permute-start(bf16[120,2048]{1,0:T(8,128)(2,1)} %add_convert_fusion.6.refs_4_), channel_id=1, source_target_pairs={{0,8},{8,0},{16,24},{24,16},{1,9},{9,1},{17,25},{25,17},{2,10},{10... | collective-permute-start | bytes 1474568 | tf_op jit(solution)/shard_map/ppermute | solution.py:354
  259.8 48.3 %collective-permute-start.6 = (bf16[120,2048]{1,0:T(8,128)(2,1)S(1)}, bf16[120,2048]{1,0:T(8,128)(2,1)}, u32[]{:S(2)}, u32[]{:S(2)}) collective-permute-start(bf16[120,2048]{1,0:T(8,128)(2,1)S(1)} %add_convert_fusion.7.refs_0_), channel_id=1, source_target_pairs={{0,8},{8,0},{16,24},{24,16},{1,9},{9,1},{17,25},{25,17},{2,10},{10... | collective-permute-start | bytes 1474568 | tf_op jit(solution)/shard_map/ppermute | solution.py:354
  260.5 47.6 %collective-permute-start.7 = (bf16[120,2048]{1,0:T(8,128)(2,1)}, bf16[120,2048]{1,0:T(8,128)(2,1)}, u32[]{:S(2)}, u32[]{:S(2)}) collective-permute-start(bf16[120,2048]{1,0:T(8,128)(2,1)} %add_convert_fusion.6.refs_4_), channel_id=1, source_target_pairs={{0,16},{8,24},{16,0},{24,8},{1,17},{9,25},{17,1},{25,9},{2,18},{10... | collective-permute-start | bytes 1474568 | tf_op jit(solution)/shard_map/ppermute | solution.py:354
  261.9 39.9 %collective-permute-start.8 = (bf16[352,2048]{1,0:T(8,128)(2,1)}, bf16[352,2048]{1,0:T(8,128)(2,1)}, u32[]{:S(2)}, u32[]{:S(2)}) collective-permute-start(bf16[352,2048]{1,0:T(8,128)(2,1)} %constant_dynamic-slice_fusion.7), channel_id=1, source_target_pairs={{0,8},{8,0},{16,24},{24,16},{1,9},{9,1},{17,25},{25,17},{2,10},{10... | collective-permute-start | bytes 4325384 | tf_op jit(solution)/shard_map/ppermute | solution.py:354
  262.5 41.8 %collective-permute-start.9 = (bf16[352,2048]{1,0:T(8,128)(2,1)S(1)}, bf16[352,2048]{1,0:T(8,128)(2,1)}, u32[]{:S(2)}, u32[]{:S(2)}) collective-permute-start(bf16[352,2048]{1,0:T(8,128)(2,1)S(1)} %constant_dynamic-slice_fusion.6), channel_id=1, source_target_pairs={{0,16},{8,24},{16,0},{24,8},{1,17},{9,25},{17,1},{25,9},{2,18},{10... | collective-permute-start | bytes 4325384 | tf_op jit(solution)/shard_map/ppermute | solution.py:354
  308.1 30.6 %collective-permute-start.10 = (bf16[176,2048]{1,0:T(8,128)(2,1)}, bf16[176,2048]{1,0:T(8,128)(2,1)}, u32[]{:S(2)}, u32[]{:S(2)}) collective-permute-start(bf16[176,2048]{1,0:T(8,128)(2,1)} %constant_dynamic-slice_fusion.5), channel_id=1, source_target_pairs={{0,16},{8,24},{16,0},{24,8},{1,17},{9,25},{17,1},{25,9},{2,18},{10... | collective-permute-start | bytes 2162696 | tf_op jit(solution)/shard_map/ppermute | solution.py:354
  310.3 30.6 %collective-permute-start.11 = (bf16[176,2048]{1,0:T(8,128)(2,1)}, bf16[176,2048]{1,0:T(8,128)(2,1)}, u32[]{:S(2)}, u32[]{:S(2)}) collective-permute-start(bf16[176,2048]{1,0:T(8,128)(2,1)} %constant_dynamic-slice_fusion.4), channel_id=1, source_target_pairs={{0,8},{8,0},{16,24},{24,16},{1,9},{9,1},{17,25},{25,17},{2,10},{10... | collective-permute-start | bytes 2162696 | tf_op jit(solution)/shard_map/ppermute | solution.py:354
  310.4 31.9 %collective-permute-start.12 = (bf16[120,2048]{1,0:T(8,128)(2,1)}, bf16[120,2048]{1,0:T(8,128)(2,1)S(1)}, u32[]{:S(2)}, u32[]{:S(2)}) collective-permute-start(bf16[120,2048]{1,0:T(8,128)(2,1)} %copy-done.20), channel_id=1, source_target_pairs={{0,8},{8,0},{16,24},{24,16},{1,9},{9,1},{17,25},{25,17},{2,10},{10... | collective-permute-start | bytes 1474568 | tf_op jit(solution)/shard_map/ppermute | solution.py:354
  312.4 29.9 %collective-permute-start.13 = (bf16[120,2048]{1,0:T(8,128)(2,1)}, bf16[120,2048]{1,0:T(8,128)(2,1)}, u32[]{:S(2)}, u32[]{:S(2)}) collective-permute-start(bf16[120,2048]{1,0:T(8,128)(2,1)} %copy-done.21), channel_id=1, source_target_pairs={{0,16},{8,24},{16,0},{24,8},{1,17},{9,25},{17,1},{25,9},{2,18},{10... | collective-permute-start | bytes 1474568 | tf_op jit(solution)/shard_map/ppermute | solution.py:354
  342.3 16.4 %collective-permute-start.14 = (bf16[176,2048]{1,0:T(8,128)(2,1)}, bf16[176,2048]{1,0:T(8,128)(2,1)}, u32[]{:S(2)}, u32[]{:S(2)}) collective-permute-start(bf16[176,2048]{1,0:T(8,128)(2,1)} %add_convert_fusion.5.refs_0_), channel_id=1, source_target_pairs={{0,16},{8,24},{16,0},{24,8},{1,17},{9,25},{17,1},{25,9},{2,18},{10... | collective-permute-start | bytes 2162696 | tf_op jit(solution)/shard_map/ppermute | solution.py:354
  344.3 14.3 %collective-permute-start.15 = (bf16[176,2048]{1,0:T(8,128)(2,1)S(1)}, bf16[176,2048]{1,0:T(8,128)(2,1)}, u32[]{:S(2)}, u32[]{:S(2)}) collective-permute-start(bf16[176,2048]{1,0:T(8,128)(2,1)S(1)} %add_convert_fusion.4.refs_4_), channel_id=1, source_target_pairs={{0,8},{8,0},{16,24},{24,16},{1,9},{9,1},{17,25},{25,17},{2,10},{10... | collective-permute-start | bytes 2162696 | tf_op jit(solution)/shard_map/ppermute | solution.py:354
  362.1 17.8 %collective-permute-start.18 = (bf16[512,768]{1,0:T(8,128)(2,1)}, bf16[512,768]{1,0:T(8,128)(2,1)S(1)}, u32[]{:S(2)}, u32[]{:S(2)}) collective-permute-start(bf16[512,768]{1,0:T(8,128)(2,1)} %get-tuple-element.310), channel_id=1, source_target_pairs={{0,16},{8,24},{16,0},{24,8},{1,17},{9,25},{17,1},{25,9},{2,18},{10... | collective-permute-start | bytes 2359304 | tf_op jit(solution)/shard_map/ppermute | solution.py:354
  363.6 17.8 %collective-permute-start.17 = (bf16[512,768]{1,0:T(8,128)(2,1)S(1)}, bf16[512,768]{1,0:T(8,128)(2,1)}, u32[]{:S(2)}, u32[]{:S(2)}) collective-permute-start(bf16[512,768]{1,0:T(8,128)(2,1)S(1)} %get-tuple-element.311), channel_id=1, source_target_pairs={{0,8},{8,0},{16,24},{24,16},{1,9},{9,1},{17,25},{25,17},{2,10},{10... | collective-permute-start | bytes 2359304 | tf_op jit(solution)/shard_map/ppermute | solution.py:354
  365.2 21.8 %copy-start.16 = (bf16[256,2048]{1,0:T(8,128)(2,1)S(1)}, bf16[256,2048]{1,0:T(8,128)(2,1)}, u32[]{:S(2)}) copy-start(bf16[256,2048]{1,0:T(8,128)(2,1)} %reduce-scatter.6.cloned.1.call-done) | copy-start | bytes 3145732
  365.2 28.1 %collective-permute-start.16 = (f32[6,128]{1,0:T(8,128)S(1)}, f32[6,128]{1,0:T(8,128)S(1)}, u32[]{:S(2)}, u32[]{:S(2)}) collective-permute-start(f32[6,128]{1,0:T(8,128)S(1)} %bitcast.131), channel_id=1, source_target_pairs={{0,8},{8,0},{16,24},{24,16},{1,9},{9,1},{17,25},{25,17},{2,10},{10... | collective-permute-start | bytes 9224 | tf_op jit(solution)/shard_map/ppermute | solution.py:354
  383.7 12.1 %collective-permute-start.21 = (bf16[256,768]{1,0:T(8,128)(2,1)S(1)}, bf16[256,768]{1,0:T(8,128)(2,1)S(1)}, u32[]{:S(2)}, u32[]{:S(2)}) collective-permute-start(bf16[256,768]{1,0:T(8,128)(2,1)S(1)} %constant_dynamic-slice_fusion.1), channel_id=1, source_target_pairs={{0,16},{8,24},{16,0},{24,8},{1,17},{9,25},{17,1},{25,9},{2,18},{10... | collective-permute-start | bytes 1179656 | tf_op jit(solution)/shard_map/ppermute | solution.py:354
  385.0 27.8 %collective-permute-start.19 = (bf16[176,2048]{1,0:T(8,128)(2,1)}, bf16[176,2048]{1,0:T(8,128)(2,1)S(1)}, u32[]{:S(2)}, u32[]{:S(2)}) collective-permute-start(bf16[176,2048]{1,0:T(8,128)(2,1)} %add_convert_fusion.5.refs_0_), channel_id=1, source_target_pairs={{0,8},{8,0},{16,24},{24,16},{1,9},{9,1},{17,25},{25,17},{2,10},{10... | collective-permute-start | bytes 2162696 | tf_op jit(solution)/shard_map/ppermute | solution.py:354
  386.1 26.7 %collective-permute-start.20 = (bf16[176,2048]{1,0:T(8,128)(2,1)S(1)}, bf16[176,2048]{1,0:T(8,128)(2,1)S(1)}, u32[]{:S(2)}, u32[]{:S(2)}) collective-permute-start(bf16[176,2048]{1,0:T(8,128)(2,1)S(1)} %copy-done.8), channel_id=1, source_target_pairs={{0,16},{8,24},{16,0},{24,8},{1,17},{9,25},{17,1},{25,9},{2,18},{10... | collective-permute-start | bytes 2162696 | tf_op jit(solution)/shard_map/ppermute | solution.py:354
  388.5 24.2 %collective-permute-start.22 = (bf16[256,768]{1,0:T(8,128)(2,1)S(1)}, bf16[256,768]{1,0:T(8,128)(2,1)S(1)}, u32[]{:S(2)}, u32[]{:S(2)}) collective-permute-start(bf16[256,768]{1,0:T(8,128)(2,1)S(1)} %constant_dynamic-slice_fusion), channel_id=1, source_target_pairs={{0,8},{8,0},{16,24},{24,16},{1,9},{9,1},{17,25},{25,17},{2,10},{10... | collective-permute-start | bytes 1179656 | tf_op jit(solution)/shard_map/ppermute | solution.py:354
  393.2 38.2 %collective-permute-start.24 = (bf16[176,2048]{1,0:T(8,128)(2,1)}, bf16[176,2048]{1,0:T(8,128)(2,1)}, u32[]{:S(2)}, u32[]{:S(2)}) collective-permute-start(bf16[176,2048]{1,0:T(8,128)(2,1)} %collective-permute-done.14.refs_1_), channel_id=1, source_target_pairs={{0,8},{8,0},{16,24},{24,16},{1,9},{9,1},{17,25},{25,17},{2,10},{10... | collective-permute-start | bytes 2162696 | tf_op jit(solution)/shard_map/ppermute | solution.py:354
  395.8 35.7 %collective-permute-start.25 = (bf16[176,2048]{1,0:T(8,128)(2,1)}, bf16[176,2048]{1,0:T(8,128)(2,1)}, u32[]{:S(2)}, u32[]{:S(2)}) collective-permute-start(bf16[176,2048]{1,0:T(8,128)(2,1)} %collective-permute-done.15.refs_5_), channel_id=1, source_target_pairs={{0,16},{8,24},{16,0},{24,8},{1,17},{9,25},{17,1},{25,9},{2,18},{10... | collective-permute-start | bytes 2162696 | tf_op jit(solution)/shard_map/ppermute | solution.py:354
  397.1 50.0 %copy-start.13 = (bf16[256,768]{1,0:T(8,128)(2,1)}, bf16[256,768]{1,0:T(8,128)(2,1)S(1)}, u32[]{:S(2)}) copy-start(bf16[256,768]{1,0:T(8,128)(2,1)S(1)} %add_convert_fusion.9.refs_0_) | copy-start | bytes 1179652
  412.8 34.3 %copy-start.14 = (bf16[256,768]{1,0:T(8,128)(2,1)}, bf16[256,768]{1,0:T(8,128)(2,1)S(1)}, u32[]{:S(2)}) copy-start(bf16[256,768]{1,0:T(8,128)(2,1)S(1)} %add_convert_fusion.8.refs_4_) | copy-start | bytes 1179652
  413.7 17.7 %collective-permute-start.26 = (bf16[256,768]{1,0:T(8,128)(2,1)S(1)}, bf16[256,768]{1,0:T(8,128)(2,1)S(1)}, u32[]{:S(2)}, u32[]{:S(2)}) collective-permute-start(bf16[256,768]{1,0:T(8,128)(2,1)S(1)} %add_convert_fusion.9.refs_0_), channel_id=1, source_target_pairs={{0,16},{8,24},{16,0},{24,8},{1,17},{9,25},{17,1},{25,9},{2,18},{10... | collective-permute-start | bytes 1179656 | tf_op jit(solution)/shard_map/ppermute | solution.py:354
  414.5 19.2 %collective-permute-start.27 = (bf16[256,768]{1,0:T(8,128)(2,1)S(1)}, bf16[256,768]{1,0:T(8,128)(2,1)S(1)}, u32[]{:S(2)}, u32[]{:S(2)}) collective-permute-start(bf16[256,768]{1,0:T(8,128)(2,1)S(1)} %add_convert_fusion.8.refs_4_), channel_id=1, source_target_pairs={{0,8},{8,0},{16,24},{24,16},{1,9},{9,1},{17,25},{25,17},{2,10},{10... | collective-permute-start | bytes 1179656 | tf_op jit(solution)/shard_map/ppermute | solution.py:354
  415.6 15.8 %collective-permute-start.23 = (f32[6,128]{1,0:T(8,128)S(1)}, f32[6,128]{1,0:T(8,128)S(1)}, u32[]{:S(2)}, u32[]{:S(2)}) collective-permute-start(f32[6,128]{1,0:T(8,128)S(1)} %add.368), channel_id=1, source_target_pairs={{0,16},{8,24},{16,0},{24,8},{1,17},{9,25},{17,1},{25,9},{2,18},{10... | collective-permute-start | bytes 9224 | tf_op jit(solution)/shard_map/ppermute | solution.py:354
  433.7 13.4 %collective-permute-start.28 = (bf16[256,768]{1,0:T(8,128)(2,1)S(1)}, bf16[256,768]{1,0:T(8,128)(2,1)S(1)}, u32[]{:S(2)}, u32[]{:S(2)}) collective-permute-start(bf16[256,768]{1,0:T(8,128)(2,1)S(1)} %add_convert_fusion.9.refs_0_), channel_id=1, source_target_pairs={{0,8},{8,0},{16,24},{24,16},{1,9},{9,1},{17,25},{25,17},{2,10},{10... | collective-permute-start | bytes 1179656 | tf_op jit(solution)/shard_map/ppermute | solution.py:354
  434.7 15.1 %collective-permute-start.29 = (bf16[256,768]{1,0:T(8,128)(2,1)S(1)}, bf16[256,768]{1,0:T(8,128)(2,1)S(1)}, u32[]{:S(2)}, u32[]{:S(2)}) collective-permute-start(bf16[256,768]{1,0:T(8,128)(2,1)S(1)} %collective-permute-done.26.refs_1_), channel_id=1, source_target_pairs={{0,8},{8,0},{16,24},{24,16},{1,9},{9,1},{17,25},{25,17},{2,10},{10... | collective-permute-start | bytes 1179656 | tf_op jit(solution)/shard_map/ppermute | solution.py:354
  435.8 14.1 %collective-permute-start.30 = (bf16[256,768]{1,0:T(8,128)(2,1)S(1)}, bf16[256,768]{1,0:T(8,128)(2,1)S(1)}, u32[]{:S(2)}, u32[]{:S(2)}) collective-permute-start(bf16[256,768]{1,0:T(8,128)(2,1)S(1)} %add_convert_fusion.8.refs_4_), channel_id=1, source_target_pairs={{0,16},{8,24},{16,0},{24,8},{1,17},{9,25},{17,1},{25,9},{2,18},{10... | collective-permute-start | bytes 1179656 | tf_op jit(solution)/shard_map/ppermute | solution.py:354
  435.9 14.6 %collective-permute-start.31 = (bf16[256,768]{1,0:T(8,128)(2,1)S(1)}, bf16[256,768]{1,0:T(8,128)(2,1)S(1)}, u32[]{:S(2)}, u32[]{:S(2)}) collective-permute-start(bf16[256,768]{1,0:T(8,128)(2,1)S(1)} %collective-permute-done.27.refs_5_), channel_id=1, source_target_pairs={{0,16},{8,24},{16,0},{24,8},{1,17},{9,25},{17,1},{25,9},{2,18},{10... | collective-permute-start | bytes 1179656 | tf_op jit(solution)/shard_map/ppermute | solution.py:354
  451.9 38.2 %copy-start.1 = (bf16[704,2048]{1,0:T(8,128)(2,1)S(1)}, bf16[704,2048]{1,0:T(8,128)(2,1)}, u32[]{:S(2)}) copy-start(bf16[704,2048]{1,0:T(8,128)(2,1)} %param.23) | copy-start | bytes 8650756
  463.7 1.4 collective-permute-start.32
  465.9 8.9 %collective-permute-start.33 = (f32[4,2048]{1,0:T(4,128)S(1)}, f32[4,2048]{1,0:T(4,128)S(1)}, u32[]{:S(2)}, u32[]{:S(2)}) collective-permute-start(f32[4,2048]{1,0:T(4,128)S(1)} %add.414), channel_id=1, source_target_pairs={{0,2},{1,3},{2,0},{3,1},{4,6},{5,7},{6,4},{7,5},{8,10},{9,11},{10,... | collective-permute-start | bytes 98312 | tf_op jit(solution)/shard_map/ppermute | solution.py:354
  474.8 4.9 collective-permute-start.34
  479.7 4.0 collective-permute-start.35
  483.7 4.0 collective-permute-start.36
  (33 other events, 286.8 us)
Sparse Core Ops, SparseCore 0:
  14.1 84.7 all-gather.2
  100.5 80.5 all-gather.4
  183.3 88.0 reduce-scatter.3
  274.1 88.0 reduce-scatter.5
  364.3 88.0 reduce-scatter.7

commit v4 on v2

--- a/solution.py
+++ b/solution.py
@@ -531,6 +531,28 @@
     return values
 
 
+def norm_kernel(x_ref, gain_ref, shift_ref, out_ref):
+    residual = x_ref[...].astype(F32)
+    centered = residual - jnp.mean(residual, -1, keepdims=True)
+    inv_std = lax.rsqrt(jnp.mean(centered * centered, -1, keepdims=True) + EPSILON)
+    out_ref[...] = (centered * inv_std * gain_ref[...] + shift_ref[...]).astype(BF16)
+
+
+def norm(layer_in, norm_gain, norm_shift):
+    length, width = layer_in.shape
+    rows = min(64, length)
+    row_spec = pl.BlockSpec((rows, width), lambda i: (i, 0))
+    one_spec = pl.BlockSpec((1, width), lambda i: (0, 0))
+    return pl.pallas_call(
+        norm_kernel,
+        grid=(length // rows,),
+        in_specs=[row_spec, one_spec, one_spec],
+        out_specs=row_spec,
+        out_shape=jax.ShapeDtypeStruct((length, width), BF16),
+        name="norm",
+    )(layer_in, norm_gain.reshape(1, width), norm_shift.reshape(1, width))
+
+
 def tail_kernel(x_ref, g_ref, c_ref, gain_ref, stat_ref, grad_ref, sums_ref):
     @pl.when(pl.program_id(0) == 0)
     def _():
@@ -636,10 +658,7 @@
     valid_here = (position_here < valid_counts[0]).astype(F32)
 
     residual = layer_in.astype(F32)
-    centered = residual - jnp.mean(residual, -1, keepdims=True)
-    inv_std = lax.rsqrt(jnp.mean(centered * centered, -1, keepdims=True) + EPSILON)
-    normalized = centered * inv_std
-    normed = (normalized * norm_gain + norm_shift).astype(BF16)
+    normed = norm(layer_in, norm_gain, norm_shift)
     cot_here = jnp.where(valid_here[:, None] > 0, out_grad[:, 0], jnp.zeros((), BF16))
     gathered = lax.all_gather(normed, "mp", axis=0, tiled=True)
     cotangent = lax.all_gather(cot_here, "mp", axis=0, tiled=True)
@@ -712,26 +731,24 @@
     sum_down.arrive()
     grad_proj, mlp_sum, _ = fence((grad_proj, mlp_sum, fresh), sum_gate_up)
     sum_gate_up.send()
-    normed_partial = back_products(grad_proj, w_qkv, grad_gate, grad_up, w_gate_up)
+    sum_qkv = token_sum(gathered, grad_proj)
     while sum_down.level < 2 * sum_down.count:
         sum_down.send()
         sum_down.arrive()
     sum_gate_up.arrive()
-    grad_proj, normed_partial = fence((grad_proj, normed_partial), sum_gate_up, sum_down)
+    sum_qkv = DpSum(sum_qkv)
+    grad_proj = fence(grad_proj, sum_gate_up, sum_down, sum_qkv)
+    sum_qkv.send()
     sum_gate_up.send()
-    sum_qkv = token_sum(gathered, grad_proj)
+    normed_partial = back_products(grad_proj, w_qkv, grad_gate, grad_up, w_gate_up)
+    bias_sums = jnp.sum(grad_proj, axis=0, dtype=F32).reshape(-1, 128)
     sum_gate_up.arrive()
-    sum_qkv = DpSum(fence(sum_qkv, sum_gate_up))
-    bias_sums = jnp.sum(grad_proj, axis=0, dtype=F32).reshape(-1, 128)
-    sum_qkv.send()
+    sum_qkv.got = fence(sum_qkv.got, sum_gate_up)
     sum_qkv.arrive()
-    normed_partial, attn_sum, bias_sums = fence(
-        (normed_partial, attn_sum, bias_sums), sum_qkv
-    )
+    normed_partial, attn_sum = fence((normed_partial, attn_sum), sum_qkv)
     grad_normed = scattered(normed_partial)
     sum_gate_up.send()
     sum_qkv.send()
-    bias_sums = sum_small(bias_sums, "dp", [0])
     mlp_part = mlp_sum.astype(F32)
     attn_part = attn_sum.astype(F32)
     layer_out = (residual + attn_part + mlp_part).astype(BF16)
@@ -748,8 +765,8 @@
     sum_gate_up.arrive()
     sum_qkv.arrive()
     bias_sums, layer_out, stat_row, _ = fence((bias_sums, layer_out, stat_row, fresh), sum_qkv)
+    bias_sums = sum_small(bias_sums, "dp", [0])
     sum_qkv.send()
-    bias_sums = sum_small(bias_sums, "dp", range(1, sum_qkv.count))
     down_sums = sum_down.result(write_rows)
     sum_qkv.arrive()
     while sum_gate_up.level < 2 * sum_gate_up.count:
@@ -760,7 +777,8 @@
         sum_qkv.send()
         sum_qkv.arrive()
     (grad_w_gate_up,) = sum_gate_up.result(write_stacked)
-    grad_w_gate_up = fence(grad_w_gate_up, sum_qkv)
+    bias_sums = sum_small(bias_sums, "dp", range(1, sum_qkv.count))
+    grad_w_gate_up, bias_sums = fence((grad_w_gate_up, bias_sums), sum_qkv)
     (grad_w_qkv,) = sum_qkv.result(write_lanes)
     grad_w_down, grad_w_out = down_sums
     grad_normed, grad_w_gate_up, grad_w_qkv = fence(

time: 510 us -> 506 us (level)
  other arithmetic: 45.3 us -> 34.8 us
  waiting for transfers between devices: 142 us -> 150 us
    ppermute x37, waiting for transfers between devices: 51.9 us -> 61.2 us  [swap(): return lax.ppermute(values, name, [(i, i ^ 1 << bit) for i in range(size)])]
  transfers between devices with their start and end apart: 42 -> 42, of which waited for: 21 -> 19; matrix products, arithmetic and copies ran while one was open for 31% -> 30% of each run, Pallas kernels for 25% -> 25%
where the time goes in v4:
time: 506 us; the launch traced here: 498 us
  waiting for transfers between devices  150 us (30%)
  Pallas kernels  131 us (26%)
  matrix products  104 us (21%)
  starting transfers between devices  41.4 us (8%)
  other arithmetic  34.8 us (7%)
  local copies, waits for them, and re-layouts  21 us (4%)
  between operations  16.1 us (3%)
    all_gather x1, waiting for transfers between devices, local(): gathered = lax.all_gather(normed, 'mp', axis=0, tiled=True)  73.5 us
    ppermute x37, waiting for transfers between devices, swap(): return lax.ppermute(values, name, [(i, i ^ 1 << bit) for i in range(size)])  61.2 us
    dot_general x5, matrix products, token_sum(): lax.dot_general(left, right, (((0,), (0,)), ((), ())), preferred_element_...  44.8 us
    dot_general x4, matrix products, turned_product(): lax.dot_general(left, right, (((1,), (1,)), ((), ())), preferred_element_...  43.3 us
    ppermute x37, starting transfers between devices, swap(): return lax.ppermute(values, name, [(i, i ^ 1 << bit) for i in range(size)])  40.6 us
    pallas_call x1, Pallas kernels, attend_back(): pl.pallas_call(attend_back_kernel, grid_spec=pltpu.PrefetchScalarGridSpec...  34.9 us
    pallas_call x1, Pallas kernels, back_products(): pl.pallas_call(back_products_kernel, grid=(length // rows,), in_specs=[pl...  26.5 us
    pallas_call x1, Pallas kernels, attend(): pl.pallas_call(attend_kernel, grid_spec=pltpu.PrefetchScalarGridSpec(num_...  24.7 us
  transfers between devices with their start and end apart: 42, of which 19 were waited for; matrix products, arithmetic and copies ran while one was open for 30% of the time, Pallas kernels for 25%

profile of v4, /device:TPU:0, one launch (start us, length us, event | category | flops | bytes accessed | tf_op | source)
XLA Modules:
  0.0 498.4 jit_solution(11608461672498015058)
XLA Ops:
  7.2 4.1 norm.1
  12.6 2.3 bitcast_select_fusion.c_ref
  17.0 5.7 %fusion.13 = (f32[2048,128]{1,0:T(8,128)}, f32[2048,128]{1,0:T(8,128)}, f32[2048,128]{1,0:T(8,128)}) fusion(f32[128]{0:T(128)S(1)} %compare_select_fusion.5, f32[2048]{0:T(1024)S(1)} %fusion.17, pred[128]{0:T(512)(128)(4,1)S(1)} %get-tuple-element.317, pred[128]{0:T(512)(128)(4,1)S(1)} %get-tuple-element.318), kind=kLoop, calls=%fused_computation.42 | loop fusion | flops 1048576 | bytes 3154688 | tf_op jit(solution)/shard_map/jit(_where)/select_n | solution.py:41
  22.7 73.5 %all-gather.3.cloned.1.call-done.x_ref = bf16[2048,2048]{1,0:T(8,128)(2,1)} async-done(((bf16[256,2048]{1,0:T(8,128)(2,1)}), bf16[2048,2048]{1,0:T(8,128)(2,1)}) %all-gather.3.cloned.1.call-update) | async-done | bytes 8388624 | tf_op jit(solution)/shard_map/all_gather | solution.py:663
  96.3 10.1 %fusion.6 = f32[2048,704]{1,0:T(8,128)S(1)} fusion(bf16[2048,2048]{1,0:T(8,128)(2,1)} %all-gather.3.cloned.1.call-done.x_ref, bf16[2,704,2048]{2,1,0:T(8,128)(2,1)} %bitcast.112), kind=kOutput, calls=%fused_computation.20 | convolution fusion | flops 5905580032 | bytes 17039360 | tf_op jit(solution)/shard_map/dot_general | solution.py:680
  106.4 13.1 %multiply_convert_fusion = (bf16[2048,704]{1,0:T(8,128)(2,1)S(1)}, f32[2048,704]{1,0:T(8,128)}) fusion(f32[2048,704]{1,0:T(8,128)S(1)} %fusion.6, bf16[2048,2048]{1,0:T(8,128)(2,1)S(1)} %copy-done.31, bf16[2,704,2048]{2,1,0:T(8,128)(2,1)} %bitcast.113), kind=kOutput, calls=%fused_computation.10 | convolution fusion | flops 5914230784 | bytes 25690112 | tf_op jit(solution)/shard_map/dot_general | solution.py:680
  119.5 1.7 copy-done.32
  121.2 8.8 %convolution_convert_fusion.1 = bf16[2048,2048]{1,0:T(8,128)(2,1)} fusion(bf16[2048,704]{1,0:T(8,128)(2,1)S(1)} %get-tuple-element.315, bf16[704,2048]{1,0:T(8,128)(2,1)S(1)} %copy-done), kind=kOutput, calls=%fused_computation.3 | convolution fusion | flops 5909774336 | bytes 14155776 | tf_op jit(solution)/shard_map/dot_general | solution.py:677
  130.5 13.2 %project.1 = (bf16[2048,256]{1,0:T(8,128)(2,1)}, bf16[2048,256]{1,0:T(8,128)(2,1)}, bf16[2048,256]{1,0:T(8,128)(2,1)}) custom-call(bf16[2048,2048]{1,0:T(8,128)(2,1)} %all-gather.3.cloned.1.call-done.x_ref, bf16[3,2048,256]{2,1,0:T(8,128)(2,1)} %bitcast.115, bf16[3,256]{1,0:T(4,128)(2,1)} %b_ref.1, f32[2048,128]{1,0:T(8,128)} %get-tuple-element.151.cos_ref, ...), custom_call_target="tpu_custom_call" | custom-call | flops 6442450944 | bytes 14680064 | tf_op jit(solution)/shard_map/project/pallas_call | solution.py:78
  143.8 24.7 %attend.1 = (bf16[2048,256]{1,0:T(8,128)(2,1)}, f32[16,1,512]{2,1,0:T(1,128)}) custom-call(s32[16]{0:T(128)} %and_select_fusion.first_ref, bf16[2048,256]{1,0:T(8,128)(2,1)} %get-tuple-element.154.q_ref, bf16[2048,256]{1,0:T(8,128)(2,1)} %get-tuple-element.155.k_ref, bf16[2048,256]{1,0:T(8,128)(2,1)} %get-tuple-element.156.v_ref, s32[16,1,128]{2,1,0:T(1,128)} %copy-done.29), custom_call_target="tpu_custom_call" | custom-call | flops 8589934592 | bytes 4194304 | tf_op jit(solution)/shard_map/attend/pallas_call | solution.py:181
  168.5 7.3 %convolution_convert_fusion = bf16[2048,2048]{1,0:T(8,128)(2,1)} fusion(bf16[2048,256]{1,0:T(8,128)(2,1)} %get-tuple-element.158.o_ref, bf16[256,2048]{1,0:T(8,128)(2,1)} %param.21), kind=kOutput, calls=%fused_computation.2 | convolution fusion | flops 2151677952 | bytes 10485760 | tf_op jit(solution)/shard_map/dot_general | solution.py:677
  175.8 2.6 all-gather.5.cloned.1.call-done
  178.4 7.2 %convolution_convert_fusion.8 = bf16[256,2048]{1,0:T(8,128)(2,1)} fusion(bf16[2048,256]{1,0:T(8,128)(2,1)} %get-tuple-element.158.o_ref, bf16[2048,2048]{1,0:T(8,128)(2,1)} %all-gather.5.cloned.1.call-done), kind=kOutput, calls=%fused_computation.29 | convolution fusion | flops 2148007936 | bytes 10485760 | tf_op jit(solution)/shard_map/dot_general | solution.py:685
  185.6 7.6 %convolution_convert_fusion.6 = bf16[704,2048]{1,0:T(8,128)(2,1)} fusion(bf16[2048,704]{1,0:T(8,128)(2,1)S(1)} %copy-done.33, bf16[2048,2048]{1,0:T(8,128)(2,1)S(1)} %copy-done.2), kind=kOutput, calls=%fused_computation.16 | convolution fusion | flops 5907021824 | bytes 14155776 | tf_op jit(solution)/shard_map/dot_general | solution.py:685
  193.5 2.2 constant_dynamic-slice_fusion.10
  198.6 4.2 collective-permute-start
  202.8 1.6 collective-permute-start.1
  204.3 15.2 %fusion.4 = (bf16[2048,704]{1,0:T(8,128)(2,1)}, bf16[2048,704]{1,0:T(8,128)(2,1)S(1)}) fusion(f32[2048,704]{1,0:T(8,128)} %copy-done.34, f32[2048,704]{1,0:T(8,128)} %get-tuple-element.316, bf16[2048,2048]{1,0:T(8,128)(2,1)} %all-gather.5.cloned.1.call-done, bf16[704,2048]{1,0:T(8,128)(2,1)S(1)} %copy-done), kind=kOutput, calls=%fused_computation.8 | convolution fusion | flops 5927206912 | bytes 28573696 | tf_op jit(solution)/shard_map/dot_general | solution.py:680
  220.8 4.8 convolution_convert_fusion.7.do_ref
  225.8 1.6 fusion.12
  227.4 1.6 fusion.11
  230.3 1.6 collective-permute-start.3
  231.9 9.9 %convolution_convert_fusion.5 = bf16[704,2048]{1,0:T(8,128)(2,1)} fusion(bf16[2048,704]{1,0:T(8,128)(2,1)S(1)} %get-tuple-element.164.g_ref, bf16[2048,2048]{1,0:T(8,128)(2,1)} %all-gather.3.cloned.1.call-done.x_ref), kind=kOutput, calls=%fused_computation.15 | convolution fusion | flops 5907021824 | bytes 14155776 | tf_op jit(solution)/shard_map/dot_general | solution.py:685
  245.5 9.8 %convolution_convert_fusion.4 = bf16[704,2048]{1,0:T(8,128)(2,1)S(1)} fusion(bf16[2048,704]{1,0:T(8,128)(2,1)} %get-tuple-element.169.u_ref, bf16[2048,2048]{1,0:T(8,128)(2,1)} %all-gather.3.cloned.1.call-done.x_ref), kind=kOutput, calls=%fused_computation.14 | convolution fusion | flops 5907021824 | bytes 14155776 | tf_op jit(solution)/shard_map/dot_general | solution.py:685
  263.5 34.9 %attend_back.1.p_ref = bf16[2048,768]{1,0:T(8,128)(2,1)} custom-call(s32[16]{0:T(128)} %and_select_fusion.first_ref, bf16[2048,256]{1,0:T(8,128)(2,1)} %get-tuple-element.154.q_ref, bf16[2048,256]{1,0:T(8,128)(2,1)} %get-tuple-element.155.k_ref, bf16[2048,256]{1,0:T(8,128)(2,1)} %get-tuple-element.156.v_ref, ...), custom_call_target="tpu_custom_call" | custom-call | flops 21474836480 | bytes 8388608 | tf_op jit(solution)/shard_map/attend_back/pallas_call | solution.py:312
  298.4 12.5 %collective-permute-done.8 = bf16[352,2048]{1,0:T(8,128)(2,1)S(1)} collective-permute-done((bf16[352,2048]{1,0:T(8,128)(2,1)}, bf16[352,2048]{1,0:T(8,128)(2,1)S(1)}, u32[]{:S(2)}, u32[]{:S(2)}) %collective-permute-start.8) | collective-permute-done | bytes 1441824 | tf_op jit(solution)/shard_map/ppermute | solution.py:354
  313.3 2.4 add_convert_fusion.1
  315.8 1.9 add_convert_fusion
  321.5 10.3 %convolution_convert_fusion.3 = bf16[2048,768]{1,0:T(8,128)(2,1)S(1)} fusion(bf16[2048,2048]{1,0:T(8,128)(2,1)} %all-gather.3.cloned.1.call-done.x_ref, bf16[2048,768]{1,0:T(8,128)(2,1)} %attend_back.1.p_ref), kind=kOutput, calls=%fused_computation.13 | convolution fusion | flops 6444023808 | bytes 14680064 | tf_op jit(solution)/shard_map/dot_general | solution.py:685
  333.2 4.9 collective-permute-done.10
  343.6 26.5 %back_products.1 = bf16[2048,2048]{1,0:T(8,128)(2,1)} custom-call(bf16[2048,768]{1,0:T(8,128)(2,1)} %attend_back.1.p_ref, bf16[3,2048,256]{2,1,0:T(8,128)(2,1)} %bitcast.116, bf16[2048,704]{1,0:T(8,128)(2,1)} %copy-done.5, bf16[2048,704]{1,0:T(8,128)(2,1)} %get-tuple-element.169.u_ref, bf16[2,704,2048]{2,1,0:T(8,128)(2,1)} %bitcast.114), custom_call_target="tpu_custom_call" | custom-call | tf_op jit(solution)/shard_map/back_products/pallas_call | solution.py:622
  370.1 2.1 collective-permute-done.16.refs_1_
  374.0 2.2 add_convert_fusion.2
  377.1 2.6 convert_reduce_fusion
  386.9 3.3 select_maximum_fusion
  393.2 15.3 %collective-permute-done.18.refs_2_ = bf16[176,2048]{1,0:T(8,128)(2,1)S(1)} collective-permute-done((bf16[176,2048]{1,0:T(8,128)(2,1)}, bf16[176,2048]{1,0:T(8,128)(2,1)S(1)}, u32[]{:S(2)}, u32[]{:S(2)}) %collective-permute-start.18) | collective-permute-done | bytes 720928 | tf_op jit(solution)/shard_map/ppermute | solution.py:354
  413.0 7.2 %place_blocks.3 = (f32[704,2048]{1,0:T(8,128)}, f32[256,2048]{1,0:T(8,128)}) custom-call(s32[8]{0:T(128)} %constant.122.clone.color_ref, s32[8]{0:T(128)} %stack.109.where_ref, bf16[120,2048]{1,0:T(8,128)(2,1)} %copy-done.11, bf16[120,2048]{1,0:T(8,128)(2,1)} %copy-done.21, bf16[120,2048]{1,0:T(8,128)(2,1)} %collective-permute-done.6.refs_2_, ...), custom_call_target="tpu_custom_call" | custom-call | bytes 11796480 | tf_op jit(solution)/shard_map/place_blocks/pallas_call | solution.py:387
  420.2 9.4 %collective-permute-done.22 = f32[6,128]{1,0:T(8,128)S(1)} collective-permute-done((f32[6,128]{1,0:T(8,128)S(1)}, f32[6,128]{1,0:T(8,128)S(1)}, u32[]{:S(2)}, u32[]{:S(2)}) %collective-permute-start.22) | collective-permute-done | bytes 3104 | tf_op jit(solution)/shard_map/ppermute | solution.py:354
  430.0 1.7 collective-permute-start.29
  435.0 8.7 %place_blocks.4 = f32[2,704,2048]{2,1,0:T(8,128)} custom-call(s32[8]{0:T(128)} %constant.122.clone.color_ref, s32[8]{0:T(128)} %stack.118.where_ref, bf16[176,2048]{1,0:T(8,128)(2,1)} %add_convert_fusion.5.refs_0_, bf16[176,2048]{1,0:T(8,128)(2,1)} %copy-done.18, bf16[176,2048]{1,0:T(8,128)(2,1)} %copy-done.19, ...), custom_call_target="tpu_custom_call" | custom-call | bytes 17301504 | tf_op jit(solution)/shard_map/place_blocks/pallas_call | solution.py:387
  446.0 6.8 %place_blocks.5 = f32[3,2048,256]{2,1,0:T(8,128)} custom-call(s32[8]{0:T(128)} %constant.122.clone.color_ref, s32[8]{0:T(128)} %stack.127.where_ref, bf16[256,768]{1,0:T(8,128)(2,1)} %copy-done.12, bf16[256,768]{1,0:T(8,128)(2,1)} %copy-done.22, bf16[256,768]{1,0:T(8,128)(2,1)} %copy-done.24, bf16[256,768]{1,0:T(8,128)(2,1)} %copy-done.25, ...), custom_call_target="tpu_custom_call" | custom-call | bytes 9437184 | tf_op jit(solution)/shard_map/place_blocks/pallas_call | solution.py:387
  452.9 12.0 %reduce-scatter.8.cloned.1.call-done.g_ref = bf16[256,2048]{1,0:T(8,128)(2,1)} async-done(((bf16[2048,2048]{1,0:T(8,128)(2,1)}), bf16[256,2048]{1,0:T(8,128)(2,1)}) %reduce-scatter.8.cloned.1.call-update) | async-done | bytes 1048592 | tf_op jit(solution)/shard_map/reduce_scatter | solution.py:690
  464.9 5.1 %tail.1 = (f32[256,1,2048]{2,1,0:T(1,128)}, f32[4,2048]{1,0:T(4,128)}) custom-call(bf16[256,2048]{1,0:T(8,128)(2,1)} %bitcast.110, bf16[256,2048]{1,0:T(8,128)(2,1)} %reduce-scatter.8.cloned.1.call-done.g_ref, bf16[256,2048]{1,0:T(8,128)(2,1)} %bitcast_select_fusion.c_ref, f32[1,2048]{1,0:T(1,128)} %bitcast.128, f32[1,2048]{1,0:T(1,128)} %bitcast.129), custom_call_target="tpu_custom_call" | custom-call | tf_op jit(solution)/shard_map/tail/pallas_call | solution.py:586
  472.2 3.9 collective-permute-done.33
  476.6 4.4 collective-permute-done.34
  481.0 1.5 collective-permute-start.35
  482.6 2.4 collective-permute-done.35
  487.2 1.9 collective-permute-done.36
  (197 shorter events, 63.6 us)
Async XLA Ops:
  7.2 114.0 %copy-start = (bf16[704,2048]{1,0:T(8,128)(2,1)S(1)}, bf16[704,2048]{1,0:T(8,128)(2,1)}, u32[]{:S(2)}) copy-start(bf16[704,2048]{1,0:T(8,128)(2,1)} %param.23) | copy-start | bytes 8650756
  7.2 89.1 %all-gather.3.cloned.1.call-start = ((), (), s32[]{:S(2)}) async-start(), calls=%async_computation.3 | async-start | bytes 9437184 | tf_op jit(solution)/shard_map/all_gather | solution.py:663
  11.3 167.1 %all-gather.5.cloned.1.call-start = ((), (), s32[]{:S(2)}) async-start(), calls=%async_computation.4 | async-start | bytes 9437184 | tf_op jit(solution)/shard_map/all_gather | solution.py:664
  14.9 304.7 %reduce-scatter.4.cloned.1.call-start = ((), (), s32[]{:S(2)}) async-start(), calls=%async_computation.5 | async-start | bytes 9437184 | tf_op jit(solution)/shard_map/reduce_scatter | solution.py:690
  16.0 90.4 %copy-start.29 = (s32[16,1,128]{2,1,0:T(1,128)}, s32[16,1,128]{2,1,0:T(1,128)S(1)}, u32[]{:S(2)}) copy-start(s32[16,1,128]{2,1,0:T(1,128)S(1)} %broadcast_maximum_fusion.start_ref) | copy-start | bytes 24580
  130.0 247.0 %reduce-scatter.6.cloned.1.call-start = ((), (), s32[]{:S(2)}) async-start(), calls=%async_computation.6 | async-start | bytes 9437184 | tf_op jit(solution)/shard_map/reduce_scatter | solution.py:690
  193.2 271.6 %reduce-scatter.8.cloned.1.call-start = ((), (), s32[]{:S(2)}) async-start(), calls=%async_computation.7 | async-start | bytes 9437184 | tf_op jit(solution)/shard_map/reduce_scatter | solution.py:690
  198.6 27.2 %collective-permute-start = (bf16[240,2048]{1,0:T(8,128)(2,1)}, bf16[240,2048]{1,0:T(8,128)(2,1)}, u32[]{:S(2)}, u32[]{:S(2)}) collective-permute-start(bf16[240,2048]{1,0:T(8,128)(2,1)} %bitcast.15), channel_id=1, source_target_pairs={{0,8},{8,0},{16,24},{24,16},{1,9},{9,1},{17,25},{25,17},{2,10},{10... | collective-permute-start | bytes 2949128 | tf_op jit(solution)/shard_map/ppermute | solution.py:354
  202.8 24.6 %collective-permute-start.1 = (bf16[240,2048]{1,0:T(8,128)(2,1)}, bf16[240,2048]{1,0:T(8,128)(2,1)}, u32[]{:S(2)}, u32[]{:S(2)}) collective-permute-start(bf16[240,2048]{1,0:T(8,128)(2,1)} %bitcast.18), channel_id=1, source_target_pairs={{0,16},{8,24},{16,0},{24,8},{1,17},{9,25},{17,1},{25,9},{2,18},{10... | collective-permute-start | bytes 2949128 | tf_op jit(solution)/shard_map/ppermute | solution.py:354
  229.1 12.9 %collective-permute-start.2 = (bf16[120,2048]{1,0:T(8,128)(2,1)S(1)}, bf16[120,2048]{1,0:T(8,128)(2,1)S(1)}, u32[]{:S(2)}, u32[]{:S(2)}) collective-permute-start(bf16[120,2048]{1,0:T(8,128)(2,1)S(1)} %constant_dynamic-slice_fusion.11), channel_id=1, source_target_pairs={{0,16},{8,24},{16,0},{24,8},{1,17},{9,25},{17,1},{25,9},{2,18},{10... | collective-permute-start | bytes 1474568 | tf_op jit(solution)/shard_map/ppermute | solution.py:354
  230.3 12.2 %collective-permute-start.3 = (bf16[120,2048]{1,0:T(8,128)(2,1)S(1)}, bf16[120,2048]{1,0:T(8,128)(2,1)S(1)}, u32[]{:S(2)}, u32[]{:S(2)}) collective-permute-start(bf16[120,2048]{1,0:T(8,128)(2,1)S(1)} %constant_dynamic-slice_fusion.8), channel_id=1, source_target_pairs={{0,8},{8,0},{16,24},{24,16},{1,9},{9,1},{17,25},{25,17},{2,10},{10... | collective-permute-start | bytes 1474568 | tf_op jit(solution)/shard_map/ppermute | solution.py:354
  243.5 14.0 %collective-permute-start.4 = (bf16[120,2048]{1,0:T(8,128)(2,1)S(1)}, bf16[120,2048]{1,0:T(8,128)(2,1)S(1)}, u32[]{:S(2)}, u32[]{:S(2)}) collective-permute-start(bf16[120,2048]{1,0:T(8,128)(2,1)S(1)} %add_convert_fusion.7.refs_0_), channel_id=1, source_target_pairs={{0,16},{8,24},{16,0},{24,8},{1,17},{9,25},{17,1},{25,9},{2,18},{10... | collective-permute-start | bytes 1474568 | tf_op jit(solution)/shard_map/ppermute | solution.py:354
  244.6 13.7 %collective-permute-start.5 = (bf16[120,2048]{1,0:T(8,128)(2,1)}, bf16[120,2048]{1,0:T(8,128)(2,1)}, u32[]{:S(2)}, u32[]{:S(2)}) collective-permute-start(bf16[120,2048]{1,0:T(8,128)(2,1)} %add_convert_fusion.6.refs_4_), channel_id=1, source_target_pairs={{0,8},{8,0},{16,24},{24,16},{1,9},{9,1},{17,25},{25,17},{2,10},{10... | collective-permute-start | bytes 1474568 | tf_op jit(solution)/shard_map/ppermute | solution.py:354
  258.3 61.3 %collective-permute-start.6 = (bf16[120,2048]{1,0:T(8,128)(2,1)S(1)}, bf16[120,2048]{1,0:T(8,128)(2,1)}, u32[]{:S(2)}, u32[]{:S(2)}) collective-permute-start(bf16[120,2048]{1,0:T(8,128)(2,1)S(1)} %add_convert_fusion.7.refs_0_), channel_id=1, source_target_pairs={{0,8},{8,0},{16,24},{24,16},{1,9},{9,1},{17,25},{25,17},{2,10},{10... | collective-permute-start | bytes 1474568 | tf_op jit(solution)/shard_map/ppermute | solution.py:354
  259.4 60.2 %collective-permute-start.7 = (bf16[120,2048]{1,0:T(8,128)(2,1)}, bf16[120,2048]{1,0:T(8,128)(2,1)}, u32[]{:S(2)}, u32[]{:S(2)}) collective-permute-start(bf16[120,2048]{1,0:T(8,128)(2,1)} %add_convert_fusion.6.refs_4_), channel_id=1, source_target_pairs={{0,16},{8,24},{16,0},{24,8},{1,17},{9,25},{17,1},{25,9},{2,18},{10... | collective-permute-start | bytes 1474568 | tf_op jit(solution)/shard_map/ppermute | solution.py:354
  260.4 79.1 %collective-permute-start.12 = (bf16[120,2048]{1,0:T(8,128)(2,1)}, bf16[120,2048]{1,0:T(8,128)(2,1)}, u32[]{:S(2)}, u32[]{:S(2)}) collective-permute-start(bf16[120,2048]{1,0:T(8,128)(2,1)} %copy-done.21), channel_id=1, source_target_pairs={{0,8},{8,0},{16,24},{24,16},{1,9},{9,1},{17,25},{25,17},{2,10},{10... | collective-permute-start | bytes 1474568 | tf_op jit(solution)/shard_map/ppermute | solution.py:354
  261.8 49.1 %collective-permute-start.8 = (bf16[352,2048]{1,0:T(8,128)(2,1)}, bf16[352,2048]{1,0:T(8,128)(2,1)S(1)}, u32[]{:S(2)}, u32[]{:S(2)}) collective-permute-start(bf16[352,2048]{1,0:T(8,128)(2,1)} %constant_dynamic-slice_fusion.7), channel_id=1, source_target_pairs={{0,8},{8,0},{16,24},{24,16},{1,9},{9,1},{17,25},{25,17},{2,10},{10... | collective-permute-start | bytes 4325384 | tf_op jit(solution)/shard_map/ppermute | solution.py:354
  262.4 53.4 %collective-permute-start.9 = (bf16[352,2048]{1,0:T(8,128)(2,1)S(1)}, bf16[352,2048]{1,0:T(8,128)(2,1)}, u32[]{:S(2)}, u32[]{:S(2)}) collective-permute-start(bf16[352,2048]{1,0:T(8,128)(2,1)S(1)} %constant_dynamic-slice_fusion.6), channel_id=1, source_target_pairs={{0,16},{8,24},{16,0},{24,8},{1,17},{9,25},{17,1},{25,9},{2,18},{10... | collective-permute-start | bytes 4325384 | tf_op jit(solution)/shard_map/ppermute | solution.py:354
  312.0 27.5 %collective-permute-start.13 = (bf16[120,2048]{1,0:T(8,128)(2,1)}, bf16[120,2048]{1,0:T(8,128)(2,1)}, u32[]{:S(2)}, u32[]{:S(2)}) collective-permute-start(bf16[120,2048]{1,0:T(8,128)(2,1)} %collective-permute-done.5.refs_5_), channel_id=1, source_target_pairs={{0,16},{8,24},{16,0},{24,8},{1,17},{9,25},{17,1},{25,9},{2,18},{10... | collective-permute-start | bytes 1474568 | tf_op jit(solution)/shard_map/ppermute | solution.py:354
  319.6 18.5 %collective-permute-start.10 = (bf16[176,2048]{1,0:T(8,128)(2,1)}, bf16[176,2048]{1,0:T(8,128)(2,1)S(1)}, u32[]{:S(2)}, u32[]{:S(2)}) collective-permute-start(bf16[176,2048]{1,0:T(8,128)(2,1)} %constant_dynamic-slice_fusion.5), channel_id=1, source_target_pairs={{0,16},{8,24},{16,0},{24,8},{1,17},{9,25},{17,1},{25,9},{2,18},{10... | collective-permute-start | bytes 2162696 | tf_op jit(solution)/shard_map/ppermute | solution.py:354
  320.3 18.9 %collective-permute-start.11 = (bf16[176,2048]{1,0:T(8,128)(2,1)}, bf16[176,2048]{1,0:T(8,128)(2,1)S(1)}, u32[]{:S(2)}, u32[]{:S(2)}) collective-permute-start(bf16[176,2048]{1,0:T(8,128)(2,1)} %constant_dynamic-slice_fusion.4), channel_id=1, source_target_pairs={{0,8},{8,0},{16,24},{24,16},{1,9},{9,1},{17,25},{25,17},{2,10},{10... | collective-permute-start | bytes 2162696 | tf_op jit(solution)/shard_map/ppermute | solution.py:354
  339.5 30.7 %copy-start.7 = (bf16[176,2048]{1,0:T(8,128)(2,1)}, bf16[176,2048]{1,0:T(8,128)(2,1)S(1)}, u32[]{:S(2)}) copy-start(bf16[176,2048]{1,0:T(8,128)(2,1)S(1)} %add_convert_fusion.4.refs_4_) | copy-start | bytes 2162692
  339.5 32.7 %collective-permute-start.14 = (bf16[512,768]{1,0:T(8,128)(2,1)}, bf16[512,768]{1,0:T(8,128)(2,1)S(1)}, u32[]{:S(2)}, u32[]{:S(2)}) collective-permute-start(bf16[512,768]{1,0:T(8,128)(2,1)} %get-tuple-element.190), channel_id=1, source_target_pairs={{0,8},{8,0},{16,24},{24,16},{1,9},{9,1},{17,25},{25,17},{2,10},{10... | collective-permute-start | bytes 2359304 | tf_op jit(solution)/shard_map/ppermute | solution.py:354
  340.8 33.2 %collective-permute-start.15 = (bf16[512,768]{1,0:T(8,128)(2,1)}, bf16[512,768]{1,0:T(8,128)(2,1)}, u32[]{:S(2)}, u32[]{:S(2)}) collective-permute-start(bf16[512,768]{1,0:T(8,128)(2,1)} %get-tuple-element.191), channel_id=1, source_target_pairs={{0,16},{8,24},{16,0},{24,8},{1,17},{9,25},{17,1},{25,9},{2,18},{10... | collective-permute-start | bytes 2359304 | tf_op jit(solution)/shard_map/ppermute | solution.py:354
  341.3 30.9 %collective-permute-start.16 = (bf16[176,2048]{1,0:T(8,128)(2,1)}, bf16[176,2048]{1,0:T(8,128)(2,1)S(1)}, u32[]{:S(2)}, u32[]{:S(2)}) collective-permute-start(bf16[176,2048]{1,0:T(8,128)(2,1)} %add_convert_fusion.5.refs_0_), channel_id=1, source_target_pairs={{0,16},{8,24},{16,0},{24,8},{1,17},{9,25},{17,1},{25,9},{2,18},{10... | collective-permute-start | bytes 2162696 | tf_op jit(solution)/shard_map/ppermute | solution.py:354
  342.8 29.4 %collective-permute-start.17 = (bf16[176,2048]{1,0:T(8,128)(2,1)S(1)}, bf16[176,2048]{1,0:T(8,128)(2,1)}, u32[]{:S(2)}, u32[]{:S(2)}) collective-permute-start(bf16[176,2048]{1,0:T(8,128)(2,1)S(1)} %add_convert_fusion.4.refs_4_), channel_id=1, source_target_pairs={{0,8},{8,0},{16,24},{24,16},{1,9},{9,1},{17,25},{25,17},{2,10},{10... | collective-permute-start | bytes 2162696 | tf_op jit(solution)/shard_map/ppermute | solution.py:354
  379.7 12.0 %collective-permute-start.20 = (bf16[256,768]{1,0:T(8,128)(2,1)S(1)}, bf16[256,768]{1,0:T(8,128)(2,1)S(1)}, u32[]{:S(2)}, u32[]{:S(2)}) collective-permute-start(bf16[256,768]{1,0:T(8,128)(2,1)S(1)} %constant_dynamic-slice_fusion.1), channel_id=1, source_target_pairs={{0,16},{8,24},{16,0},{24,8},{1,17},{9,25},{17,1},{25,9},{2,18},{10... | collective-permute-start | bytes 1179656 | tf_op jit(solution)/shard_map/ppermute | solution.py:354
  380.9 12.2 %collective-permute-start.21 = (bf16[256,768]{1,0:T(8,128)(2,1)}, bf16[256,768]{1,0:T(8,128)(2,1)S(1)}, u32[]{:S(2)}, u32[]{:S(2)}) collective-permute-start(bf16[256,768]{1,0:T(8,128)(2,1)} %constant_dynamic-slice_fusion), channel_id=1, source_target_pairs={{0,8},{8,0},{16,24},{24,16},{1,9},{9,1},{17,25},{25,17},{2,10},{10... | collective-permute-start | bytes 1179656 | tf_op jit(solution)/shard_map/ppermute | solution.py:354
  381.7 26.8 %collective-permute-start.18 = (bf16[176,2048]{1,0:T(8,128)(2,1)}, bf16[176,2048]{1,0:T(8,128)(2,1)S(1)}, u32[]{:S(2)}, u32[]{:S(2)}) collective-permute-start(bf16[176,2048]{1,0:T(8,128)(2,1)} %add_convert_fusion.5.refs_0_), channel_id=1, source_target_pairs={{0,8},{8,0},{16,24},{24,16},{1,9},{9,1},{17,25},{25,17},{2,10},{10... | collective-permute-start | bytes 2162696 | tf_op jit(solution)/shard_map/ppermute | solution.py:354
  382.9 25.6 %collective-permute-start.19 = (bf16[176,2048]{1,0:T(8,128)(2,1)}, bf16[176,2048]{1,0:T(8,128)(2,1)S(1)}, u32[]{:S(2)}, u32[]{:S(2)}) collective-permute-start(bf16[176,2048]{1,0:T(8,128)(2,1)} %copy-done.7), channel_id=1, source_target_pairs={{0,16},{8,24},{16,0},{24,8},{1,17},{9,25},{17,1},{25,9},{2,18},{10... | collective-permute-start | bytes 2162696 | tf_op jit(solution)/shard_map/ppermute | solution.py:354
  383.8 45.8 %collective-permute-start.23 = (bf16[176,2048]{1,0:T(8,128)(2,1)}, bf16[176,2048]{1,0:T(8,128)(2,1)}, u32[]{:S(2)}, u32[]{:S(2)}) collective-permute-start(bf16[176,2048]{1,0:T(8,128)(2,1)} %copy-done.18), channel_id=1, source_target_pairs={{0,8},{8,0},{16,24},{24,16},{1,9},{9,1},{17,25},{25,17},{2,10},{10... | collective-permute-start | bytes 2162696 | tf_op jit(solution)/shard_map/ppermute | solution.py:354
  391.7 37.9 %collective-permute-start.24 = (bf16[176,2048]{1,0:T(8,128)(2,1)}, bf16[176,2048]{1,0:T(8,128)(2,1)}, u32[]{:S(2)}, u32[]{:S(2)}) collective-permute-start(bf16[176,2048]{1,0:T(8,128)(2,1)} %collective-permute-done.17.refs_5_), channel_id=1, source_target_pairs={{0,16},{8,24},{16,0},{24,8},{1,17},{9,25},{17,1},{25,9},{2,18},{10... | collective-permute-start | bytes 2162696 | tf_op jit(solution)/shard_map/ppermute | solution.py:354
  393.0 50.7 %copy-start.12 = (bf16[256,768]{1,0:T(8,128)(2,1)}, bf16[256,768]{1,0:T(8,128)(2,1)S(1)}, u32[]{:S(2)}) copy-start(bf16[256,768]{1,0:T(8,128)(2,1)S(1)} %add_convert_fusion.9.refs_0_) | copy-start | bytes 1179652
  393.2 50.5 %copy-start.13 = (bf16[256,768]{1,0:T(8,128)(2,1)}, bf16[256,768]{1,0:T(8,128)(2,1)S(1)}, u32[]{:S(2)}) copy-start(bf16[256,768]{1,0:T(8,128)(2,1)S(1)} %add_convert_fusion.8.refs_4_) | copy-start | bytes 1179652
  409.4 20.2 %collective-permute-start.25 = (bf16[256,768]{1,0:T(8,128)(2,1)S(1)}, bf16[256,768]{1,0:T(8,128)(2,1)S(1)}, u32[]{:S(2)}, u32[]{:S(2)}) collective-permute-start(bf16[256,768]{1,0:T(8,128)(2,1)S(1)} %add_convert_fusion.9.refs_0_), channel_id=1, source_target_pairs={{0,16},{8,24},{16,0},{24,8},{1,17},{9,25},{17,1},{25,9},{2,18},{10... | collective-permute-start | bytes 1179656 | tf_op jit(solution)/shard_map/ppermute | solution.py:354
  410.3 19.4 %collective-permute-start.26 = (bf16[256,768]{1,0:T(8,128)(2,1)S(1)}, bf16[256,768]{1,0:T(8,128)(2,1)S(1)}, u32[]{:S(2)}, u32[]{:S(2)}) collective-permute-start(bf16[256,768]{1,0:T(8,128)(2,1)S(1)} %add_convert_fusion.8.refs_4_), channel_id=1, source_target_pairs={{0,8},{8,0},{16,24},{24,16},{1,9},{9,1},{17,25},{25,17},{2,10},{10... | collective-permute-start | bytes 1179656 | tf_op jit(solution)/shard_map/ppermute | solution.py:354
  411.3 18.3 %collective-permute-start.22 = (f32[6,128]{1,0:T(8,128)S(1)}, f32[6,128]{1,0:T(8,128)S(1)}, u32[]{:S(2)}, u32[]{:S(2)}) collective-permute-start(f32[6,128]{1,0:T(8,128)S(1)} %bitcast.131), channel_id=1, source_target_pairs={{0,8},{8,0},{16,24},{24,16},{1,9},{9,1},{17,25},{25,17},{2,10},{10... | collective-permute-start | bytes 9224 | tf_op jit(solution)/shard_map/ppermute | solution.py:354
  429.6 14.2 %collective-permute-start.28 = (bf16[256,768]{1,0:T(8,128)(2,1)S(1)}, bf16[256,768]{1,0:T(8,128)(2,1)S(1)}, u32[]{:S(2)}, u32[]{:S(2)}) collective-permute-start(bf16[256,768]{1,0:T(8,128)(2,1)S(1)} %add_convert_fusion.9.refs_0_), channel_id=1, source_target_pairs={{0,8},{8,0},{16,24},{24,16},{1,9},{9,1},{17,25},{25,17},{2,10},{10... | collective-permute-start | bytes 1179656 | tf_op jit(solution)/shard_map/ppermute | solution.py:354
  430.0 14.4 %collective-permute-start.29 = (bf16[256,768]{1,0:T(8,128)(2,1)S(1)}, bf16[256,768]{1,0:T(8,128)(2,1)S(1)}, u32[]{:S(2)}, u32[]{:S(2)}) collective-permute-start(bf16[256,768]{1,0:T(8,128)(2,1)S(1)} %collective-permute-done.25.refs_1_), channel_id=1, source_target_pairs={{0,8},{8,0},{16,24},{24,16},{1,9},{9,1},{17,25},{25,17},{2,10},{10... | collective-permute-start | bytes 1179656 | tf_op jit(solution)/shard_map/ppermute | solution.py:354
  431.7 12.6 %collective-permute-start.30 = (bf16[256,768]{1,0:T(8,128)(2,1)S(1)}, bf16[256,768]{1,0:T(8,128)(2,1)S(1)}, u32[]{:S(2)}, u32[]{:S(2)}) collective-permute-start(bf16[256,768]{1,0:T(8,128)(2,1)S(1)} %add_convert_fusion.8.refs_4_), channel_id=1, source_target_pairs={{0,16},{8,24},{16,0},{24,8},{1,17},{9,25},{17,1},{25,9},{2,18},{10... | collective-permute-start | bytes 1179656 | tf_op jit(solution)/shard_map/ppermute | solution.py:354
  432.2 12.1 %collective-permute-start.31 = (bf16[256,768]{1,0:T(8,128)(2,1)S(1)}, bf16[256,768]{1,0:T(8,128)(2,1)S(1)}, u32[]{:S(2)}, u32[]{:S(2)}) collective-permute-start(bf16[256,768]{1,0:T(8,128)(2,1)S(1)} %collective-permute-done.26.refs_5_), channel_id=1, source_target_pairs={{0,16},{8,24},{16,0},{24,8},{1,17},{9,25},{17,1},{25,9},{2,18},{10... | collective-permute-start | bytes 1179656 | tf_op jit(solution)/shard_map/ppermute | solution.py:354
  433.8 10.1 %collective-permute-start.27 = (f32[6,128]{1,0:T(8,128)S(1)}, f32[6,128]{1,0:T(8,128)S(1)}, u32[]{:S(2)}, u32[]{:S(2)}) collective-permute-start(f32[6,128]{1,0:T(8,128)S(1)} %add.369), channel_id=1, source_target_pairs={{0,16},{8,24},{16,0},{24,8},{1,17},{9,25},{17,1},{25,9},{2,18},{10... | collective-permute-start | bytes 9224 | tf_op jit(solution)/shard_map/ppermute | solution.py:354
  446.0 45.4 %copy-start.1 = (bf16[704,2048]{1,0:T(8,128)(2,1)S(1)}, bf16[704,2048]{1,0:T(8,128)(2,1)}, u32[]{:S(2)}) copy-start(bf16[704,2048]{1,0:T(8,128)(2,1)} %param.23) | copy-start | bytes 8650756
  470.0 1.4 collective-permute-start.32
  472.2 4.0 collective-permute-start.33
  476.2 4.9 collective-permute-start.34
  481.0 4.0 collective-permute-start.35
  485.0 4.0 collective-permute-start.36
  (31 other events, 226.5 us)
Sparse Core Ops, SparseCore 0:
  11.5 84.7 all-gather.2
  97.9 80.5 all-gather.4
  180.7 88.0 reduce-scatter.3
  271.5 87.9 reduce-scatter.5
  377.2 87.6 reduce-scatter.7

commit v5 on v4

--- a/solution.py
+++ b/solution.py
@@ -442,6 +442,16 @@
         elif self.held is None:
             self.held = [[(self.state[color][0][0], 0)] for color in range(2)]
 
+    def send_half(self, half):
+        for color in range(2):
+            bit = self.orders[color][2 * self.count - 1 - self.level]
+            blocks = 1 << (self.level - self.count)
+            middle = max(blocks // 2, 1)
+            chosen = self.held[color][:middle] if half == 0 else self.held[color][middle:blocks]
+            self.held[color] += [
+                (swap(piece, "dp", bit), mask ^ (1 << bit)) for piece, mask in chosen
+            ]
+
     def send(self):
         if self.level < self.count:
             self.got = [
@@ -722,31 +732,30 @@
     sum_down.arrive()
     grad_att = fence(grad_att, sum_gate_up, sum_down)
     sum_gate_up.send()
-    sum_down.send()
-    fresh = sum_down.fresh()
+    sum_down.send_half(0)
     grad_proj = attend_back(
         first, queries, key_rows, value_rows, grad_att, attended, lse, start_blocks, tables
     )
     sum_gate_up.arrive()
+    grad_proj, mlp_sum = fence((grad_proj, mlp_sum), sum_gate_up, sum_down)
+    sum_gate_up.send()
+    sum_down.send_half(1)
     sum_down.arrive()
-    grad_proj, mlp_sum, _ = fence((grad_proj, mlp_sum, fresh), sum_gate_up)
-    sum_gate_up.send()
-    sum_qkv = token_sum(gathered, grad_proj)
+    normed_partial = back_products(grad_proj, w_qkv, grad_gate, grad_up, w_gate_up)
     while sum_down.level < 2 * sum_down.count:
         sum_down.send()
         sum_down.arrive()
     sum_gate_up.arrive()
-    sum_qkv = DpSum(sum_qkv)
-    grad_proj = fence(grad_proj, sum_gate_up, sum_down, sum_qkv)
+    grad_proj, normed_partial = fence((grad_proj, normed_partial), sum_gate_up, sum_down)
+    grad_normed = scattered(normed_partial)
+    sum_gate_up.send()
+    sum_qkv = token_sum(gathered, grad_proj)
+    sum_gate_up.arrive()
+    sum_qkv = DpSum(fence(sum_qkv, sum_gate_up))
+    bias_sums = jnp.sum(grad_proj, axis=0, dtype=F32).reshape(-1, 128)
     sum_qkv.send()
-    sum_gate_up.send()
-    normed_partial = back_products(grad_proj, w_qkv, grad_gate, grad_up, w_gate_up)
-    bias_sums = jnp.sum(grad_proj, axis=0, dtype=F32).reshape(-1, 128)
-    sum_gate_up.arrive()
-    sum_qkv.got = fence(sum_qkv.got, sum_gate_up)
     sum_qkv.arrive()
-    normed_partial, attn_sum = fence((normed_partial, attn_sum), sum_qkv)
-    grad_normed = scattered(normed_partial)
+    attn_sum = fence(attn_sum, sum_gate_up, sum_qkv)
     sum_gate_up.send()
     sum_qkv.send()
     mlp_part = mlp_sum.astype(F32)

time: 506 us -> 495 us (0.978)
  waiting for transfers between devices: 150 us -> 131 us
    reduce_scatter x3, waiting for transfers between devices: 12 us -> 0.02 us  [scattered(): return lax.psum_scatter(partial, 'mp', scatter_dimension=0, tiled=True)]
    ppermute x37, waiting for transfers between devices: 61.2 us -> 54.5 us  [swap(): return lax.ppermute(values, name, [(i, i ^ 1 << bit) for i in range(size)])]
  transfers between devices with their start and end apart: 42 -> 42, of which waited for: 19 -> 18; matrix products, arithmetic and copies ran while one was open for 30% -> 32% of each run, Pallas kernels for 25% -> 25%
where the time goes in v5:
time: 495 us; the launch traced here: 490 us
  Pallas kernels  131 us (26%)
  waiting for transfers between devices  131 us (26%)
  matrix products  106 us (21%)
  starting transfers between devices  44.5 us (9%)
  other arithmetic  38.7 us (8%)
  local copies, waits for them, and re-layouts  23.9 us (5%)
  between operations  15.9 us (3%)
    all_gather x1, waiting for transfers between devices, local(): gathered = lax.all_gather(normed, 'mp', axis=0, tiled=True)  73.5 us
    ppermute x37, waiting for transfers between devices, swap(): return lax.ppermute(values, name, [(i, i ^ 1 << bit) for i in range(size)])  54.5 us
    dot_general x5, matrix products, token_sum(): lax.dot_general(left, right, (((0,), (0,)), ((), ())), preferred_element_...  46.1 us
    ppermute x37, starting transfers between devices, swap(): return lax.ppermute(values, name, [(i, i ^ 1 << bit) for i in range(size)])  43.5 us
    dot_general x4, matrix products, turned_product(): lax.dot_general(left, right, (((1,), (1,)), ((), ())), preferred_element_...  43.3 us
    pallas_call x1, Pallas kernels, attend_back(): pl.pallas_call(attend_back_kernel, grid_spec=pltpu.PrefetchScalarGridSpec...  34.9 us
    pallas_call x1, Pallas kernels, back_products(): pl.pallas_call(back_products_kernel, grid=(length // rows,), in_specs=[pl...  26.2 us
    pallas_call x1, Pallas kernels, attend(): pl.pallas_call(attend_kernel, grid_spec=pltpu.PrefetchScalarGridSpec(num_...  24.7 us
  transfers between devices with their start and end apart: 42, of which 18 were waited for; matrix products, arithmetic and copies ran while one was open for 32% of the time, Pallas kernels for 25%

profile of v5, /device:TPU:0, one launch (start us, length us, event | category | flops | bytes accessed | tf_op | source)
XLA Modules:
  0.0 490.3 jit_solution(5140230140804589671)
XLA Ops:
  7.2 4.1 norm.1
  12.6 2.3 bitcast_select_fusion.c_ref
  17.0 5.8 %fusion.13 = (f32[2048,128]{1,0:T(8,128)}, f32[2048,128]{1,0:T(8,128)}, f32[2048,128]{1,0:T(8,128)}) fusion(f32[128]{0:T(128)S(1)} %compare_select_fusion.5, f32[2048]{0:T(1024)S(1)} %fusion.17, pred[128]{0:T(512)(128)(4,1)S(1)} %get-tuple-element.351, pred[128]{0:T(512)(128)(4,1)S(1)} %get-tuple-element.352), kind=kLoop, calls=%fused_computation.42 | loop fusion | flops 1048576 | bytes 3154688 | tf_op jit(solution)/shard_map/jit(_where)/select_n | solution.py:41
  22.8 73.5 %all-gather.3.cloned.1.call-done.x_ref = bf16[2048,2048]{1,0:T(8,128)(2,1)} async-done(((bf16[256,2048]{1,0:T(8,128)(2,1)}), bf16[2048,2048]{1,0:T(8,128)(2,1)}) %all-gather.3.cloned.1.call-update) | async-done | bytes 8388624 | tf_op jit(solution)/shard_map/all_gather | solution.py:673
  96.3 10.1 %fusion.6 = f32[2048,704]{1,0:T(8,128)S(1)} fusion(bf16[2048,2048]{1,0:T(8,128)(2,1)} %all-gather.3.cloned.1.call-done.x_ref, bf16[2,704,2048]{2,1,0:T(8,128)(2,1)} %bitcast.112), kind=kOutput, calls=%fused_computation.20 | convolution fusion | flops 5905580032 | bytes 17039360 | tf_op jit(solution)/shard_map/dot_general | solution.py:690
  106.4 13.1 %multiply_convert_fusion = (bf16[2048,704]{1,0:T(8,128)(2,1)S(1)}, f32[2048,704]{1,0:T(8,128)}) fusion(f32[2048,704]{1,0:T(8,128)S(1)} %fusion.6, bf16[2048,2048]{1,0:T(8,128)(2,1)S(1)} %copy-done.28, bf16[2,704,2048]{2,1,0:T(8,128)(2,1)} %bitcast.113), kind=kOutput, calls=%fused_computation.10 | convolution fusion | flops 5914230784 | bytes 25690112 | tf_op jit(solution)/shard_map/dot_general | solution.py:690
  121.2 8.9 %convolution_convert_fusion.1 = bf16[2048,2048]{1,0:T(8,128)(2,1)} fusion(bf16[2048,704]{1,0:T(8,128)(2,1)S(1)} %get-tuple-element.349, bf16[704,2048]{1,0:T(8,128)(2,1)S(1)} %copy-done), kind=kOutput, calls=%fused_computation.3 | convolution fusion | flops 5909774336 | bytes 14155776 | tf_op jit(solution)/shard_map/dot_general | solution.py:687
  130.4 13.2 %project.1 = (bf16[2048,256]{1,0:T(8,128)(2,1)}, bf16[2048,256]{1,0:T(8,128)(2,1)}, bf16[2048,256]{1,0:T(8,128)(2,1)}) custom-call(bf16[2048,2048]{1,0:T(8,128)(2,1)} %all-gather.3.cloned.1.call-done.x_ref, bf16[3,2048,256]{2,1,0:T(8,128)(2,1)} %bitcast.115, bf16[3,256]{1,0:T(4,128)(2,1)} %b_ref.1, f32[2048,128]{1,0:T(8,128)} %get-tuple-element.168.cos_ref, ...), custom_call_target="tpu_custom_call" | custom-call | flops 6442450944 | bytes 14680064 | tf_op jit(solution)/shard_map/project/pallas_call | solution.py:78
  143.7 24.7 %attend.1 = (bf16[2048,256]{1,0:T(8,128)(2,1)}, f32[16,1,512]{2,1,0:T(1,128)}) custom-call(s32[16]{0:T(128)} %and_select_fusion.first_ref, bf16[2048,256]{1,0:T(8,128)(2,1)} %get-tuple-element.171.q_ref, bf16[2048,256]{1,0:T(8,128)(2,1)} %get-tuple-element.172.k_ref, bf16[2048,256]{1,0:T(8,128)(2,1)} %get-tuple-element.173.v_ref, s32[16,1,128]{2,1,0:T(1,128)} %copy-done.26), custom_call_target="tpu_custom_call" | custom-call | flops 8589934592 | bytes 4194304 | tf_op jit(solution)/shard_map/attend/pallas_call | solution.py:181
  168.4 7.3 %convolution_convert_fusion = bf16[2048,2048]{1,0:T(8,128)(2,1)} fusion(bf16[2048,256]{1,0:T(8,128)(2,1)} %get-tuple-element.175.o_ref, bf16[256,2048]{1,0:T(8,128)(2,1)} %param.21), kind=kOutput, calls=%fused_computation.2 | convolution fusion | flops 2151677952 | bytes 10485760 | tf_op jit(solution)/shard_map/dot_general | solution.py:687
  175.7 2.8 all-gather.5.cloned.1.call-done
  178.4 7.2 %convolution_convert_fusion.8 = bf16[256,2048]{1,0:T(8,128)(2,1)} fusion(bf16[2048,256]{1,0:T(8,128)(2,1)} %get-tuple-element.175.o_ref, bf16[2048,2048]{1,0:T(8,128)(2,1)} %all-gather.5.cloned.1.call-done), kind=kOutput, calls=%fused_computation.29 | convolution fusion | flops 2148007936 | bytes 10485760 | tf_op jit(solution)/shard_map/dot_general | solution.py:695
  185.6 7.6 %convolution_convert_fusion.6 = bf16[704,2048]{1,0:T(8,128)(2,1)} fusion(bf16[2048,704]{1,0:T(8,128)(2,1)S(1)} %copy-done.30, bf16[2048,2048]{1,0:T(8,128)(2,1)S(1)} %copy-done.2), kind=kOutput, calls=%fused_computation.16 | convolution fusion | flops 5907021824 | bytes 14155776 | tf_op jit(solution)/shard_map/dot_general | solution.py:695
  193.8 2.0 constant_dynamic-slice_fusion.9
  195.8 2.1 constant_dynamic-slice_fusion.10
  201.5 4.4 collective-permute-start.1
  205.9 15.3 %fusion.4 = (bf16[2048,704]{1,0:T(8,128)(2,1)}, bf16[2048,704]{1,0:T(8,128)(2,1)S(1)}) fusion(f32[2048,704]{1,0:T(8,128)} %copy-done.31, f32[2048,704]{1,0:T(8,128)} %get-tuple-element.350, bf16[2048,2048]{1,0:T(8,128)(2,1)} %all-gather.5.cloned.1.call-done, bf16[704,2048]{1,0:T(8,128)(2,1)S(1)} %copy-done), kind=kOutput, calls=%fused_computation.8 | convolution fusion | flops 5927206912 | bytes 28573696 | tf_op jit(solution)/shard_map/dot_general | solution.py:690
  222.5 4.7 convolution_convert_fusion.7.do_ref
  230.6 2.8 collective-permute-start.2
  233.7 9.9 %convolution_convert_fusion.5 = bf16[704,2048]{1,0:T(8,128)(2,1)} fusion(bf16[2048,704]{1,0:T(8,128)(2,1)S(1)} %get-tuple-element.181.g_ref, bf16[2048,2048]{1,0:T(8,128)(2,1)} %all-gather.3.cloned.1.call-done.x_ref), kind=kOutput, calls=%fused_computation.15 | convolution fusion | flops 5907021824 | bytes 14155776 | tf_op jit(solution)/shard_map/dot_general | solution.py:695
  248.0 9.8 %convolution_convert_fusion.4 = bf16[704,2048]{1,0:T(8,128)(2,1)S(1)} fusion(bf16[2048,704]{1,0:T(8,128)(2,1)} %get-tuple-element.186.u_ref, bf16[2048,2048]{1,0:T(8,128)(2,1)} %all-gather.3.cloned.1.call-done.x_ref), kind=kOutput, calls=%fused_computation.14 | convolution fusion | flops 5907021824 | bytes 14155776 | tf_op jit(solution)/shard_map/dot_general | solution.py:695
  264.8 34.9 %attend_back.1.p_ref = bf16[2048,768]{1,0:T(8,128)(2,1)} custom-call(s32[16]{0:T(128)} %and_select_fusion.first_ref, bf16[2048,256]{1,0:T(8,128)(2,1)} %get-tuple-element.171.q_ref, bf16[2048,256]{1,0:T(8,128)(2,1)} %get-tuple-element.172.k_ref, bf16[2048,256]{1,0:T(8,128)(2,1)} %get-tuple-element.173.v_ref, ...), custom_call_target="tpu_custom_call" | custom-call | flops 21474836480 | bytes 8388608 | tf_op jit(solution)/shard_map/attend_back/pallas_call | solution.py:312
  299.7 3.2 collective-permute-done.6
  302.9 2.4 add_convert_fusion.1
  305.3 1.9 add_convert_fusion
  309.2 4.9 collective-permute-start.10
  314.0 2.0 collective-permute-start.12
  316.2 26.2 %back_products.1 = bf16[2048,2048]{1,0:T(8,128)(2,1)} custom-call(bf16[2048,768]{1,0:T(8,128)(2,1)} %attend_back.1.p_ref, bf16[3,2048,256]{2,1,0:T(8,128)(2,1)} %bitcast.116, bf16[2048,704]{1,0:T(8,128)(2,1)} %copy-done.4, bf16[2048,704]{1,0:T(8,128)(2,1)} %get-tuple-element.186.u_ref, bf16[2,704,2048]{2,1,0:T(8,128)(2,1)} %bitcast.114), custom_call_target="tpu_custom_call" | custom-call | tf_op jit(solution)/shard_map/back_products/pallas_call | solution.py:632
  342.4 2.2 add_convert_fusion.5.refs_0_
  347.6 2.0 collective-permute-start.14
  349.5 11.6 %convolution_convert_fusion.3 = bf16[2048,768]{1,0:T(8,128)(2,1)} fusion(bf16[2048,2048]{1,0:T(8,128)(2,1)} %all-gather.3.cloned.1.call-done.x_ref, bf16[2048,768]{1,0:T(8,128)(2,1)} %attend_back.1.p_ref), kind=kOutput, calls=%fused_computation.13 | convolution fusion | flops 6444023808 | bytes 14680064 | tf_op jit(solution)/shard_map/dot_general | solution.py:695
  363.2 2.4 constant_dynamic-slice_fusion.1
  366.8 2.4 convert_reduce_fusion
  369.3 10.6 %collective-permute-done.17 = bf16[512,768]{1,0:T(8,128)(2,1)S(1)} collective-permute-done((bf16[512,768]{1,0:T(8,128)(2,1)}, bf16[512,768]{1,0:T(8,128)(2,1)S(1)}, u32[]{:S(2)}, u32[]{:S(2)}) %collective-permute-start.17) | collective-permute-done | bytes 786464 | tf_op jit(solution)/shard_map/ppermute | solution.py:354
  380.8 2.3 add_convert_fusion.2
  389.3 3.0 fusion.8
  392.9 3.3 select_maximum_fusion
  397.6 15.3 %collective-permute-done.18.refs_2_ = bf16[176,2048]{1,0:T(8,128)(2,1)S(1)} collective-permute-done((bf16[176,2048]{1,0:T(8,128)(2,1)}, bf16[176,2048]{1,0:T(8,128)(2,1)S(1)}, u32[]{:S(2)}, u32[]{:S(2)}) %collective-permute-start.18) | collective-permute-done | bytes 720928 | tf_op jit(solution)/shard_map/ppermute | solution.py:354
  417.3 7.2 %place_blocks.3 = (f32[704,2048]{1,0:T(8,128)}, f32[256,2048]{1,0:T(8,128)}) custom-call(s32[8]{0:T(128)} %constant.122.clone.color_ref, s32[8]{0:T(128)} %stack.109.where_ref, bf16[120,2048]{1,0:T(8,128)(2,1)} %copy-done.10, bf16[120,2048]{1,0:T(8,128)(2,1)} %copy-done.17, bf16[120,2048]{1,0:T(8,128)(2,1)} %collective-permute-done.8.refs_2_, ...), custom_call_target="tpu_custom_call" | custom-call | bytes 11796480 | tf_op jit(solution)/shard_map/place_blocks/pallas_call | solution.py:387
  424.5 9.4 %collective-permute-done.22 = f32[6,128]{1,0:T(8,128)S(1)} collective-permute-done((f32[6,128]{1,0:T(8,128)S(1)}, f32[6,128]{1,0:T(8,128)S(1)}, u32[]{:S(2)}, u32[]{:S(2)}) %collective-permute-start.22) | collective-permute-done | bytes 3104 | tf_op jit(solution)/shard_map/ppermute | solution.py:354
  439.1 8.7 %place_blocks.4 = f32[2,704,2048]{2,1,0:T(8,128)} custom-call(s32[8]{0:T(128)} %constant.122.clone.color_ref, s32[8]{0:T(128)} %stack.118.where_ref, bf16[176,2048]{1,0:T(8,128)(2,1)} %add_convert_fusion.5.refs_0_, bf16[176,2048]{1,0:T(8,128)(2,1)} %copy-done.14, bf16[176,2048]{1,0:T(8,128)(2,1)} %copy-done.15, ...), custom_call_target="tpu_custom_call" | custom-call | bytes 17301504 | tf_op jit(solution)/shard_map/place_blocks/pallas_call | solution.py:387
  450.3 6.7 %place_blocks.5 = f32[3,2048,256]{2,1,0:T(8,128)} custom-call(s32[8]{0:T(128)} %constant.122.clone.color_ref, s32[8]{0:T(128)} %stack.127.where_ref, bf16[256,768]{1,0:T(8,128)(2,1)} %copy-done.11, bf16[256,768]{1,0:T(8,128)(2,1)} %copy-done.19, bf16[256,768]{1,0:T(8,128)(2,1)} %copy-done.21, bf16[256,768]{1,0:T(8,128)(2,1)} %copy-done.22, ...), custom_call_target="tpu_custom_call" | custom-call | bytes 9437184 | tf_op jit(solution)/shard_map/place_blocks/pallas_call | solution.py:387
  457.0 5.1 %tail.1 = (f32[256,1,2048]{2,1,0:T(1,128)}, f32[4,2048]{1,0:T(4,128)}) custom-call(bf16[256,2048]{1,0:T(8,128)(2,1)} %bitcast.110, bf16[256,2048]{1,0:T(8,128)(2,1)} %reduce-scatter.8.cloned.1.call-done.g_ref, bf16[256,2048]{1,0:T(8,128)(2,1)} %bitcast_select_fusion.c_ref, f32[1,2048]{1,0:T(1,128)} %bitcast.128, f32[1,2048]{1,0:T(1,128)} %bitcast.129), custom_call_target="tpu_custom_call" | custom-call | tf_op jit(solution)/shard_map/tail/pallas_call | solution.py:596
  464.4 3.9 collective-permute-done.33
  468.3 1.8 collective-permute-start.34
  470.1 3.0 collective-permute-done.34
  474.7 2.4 collective-permute-done.35
  479.3 1.8 collective-permute-done.36
  (191 shorter events, 61.9 us)
Async XLA Ops:
  7.2 114.0 %copy-start = (bf16[704,2048]{1,0:T(8,128)(2,1)S(1)}, bf16[704,2048]{1,0:T(8,128)(2,1)}, u32[]{:S(2)}) copy-start(bf16[704,2048]{1,0:T(8,128)(2,1)} %param.23) | copy-start | bytes 8650756
  7.2 89.1 %all-gather.3.cloned.1.call-start = ((), (), s32[]{:S(2)}) async-start(), calls=%async_computation.3 | async-start | bytes 9437184 | tf_op jit(solution)/shard_map/all_gather | solution.py:673
  11.3 167.1 %all-gather.5.cloned.1.call-start = ((), (), s32[]{:S(2)}) async-start(), calls=%async_computation.4 | async-start | bytes 9437184 | tf_op jit(solution)/shard_map/all_gather | solution.py:674
  14.9 294.2 %reduce-scatter.4.cloned.1.call-start = ((), (), s32[]{:S(2)}) async-start(), calls=%async_computation.5 | async-start | bytes 9437184 | tf_op jit(solution)/shard_map/reduce_scatter | solution.py:700
  16.0 90.4 %copy-start.26 = (s32[16,1,128]{2,1,0:T(1,128)}, s32[16,1,128]{2,1,0:T(1,128)S(1)}, u32[]{:S(2)}) copy-start(s32[16,1,128]{2,1,0:T(1,128)S(1)} %broadcast_maximum_fusion.start_ref) | copy-start | bytes 24580
  130.1 253.9 %reduce-scatter.6.cloned.1.call-start = ((), (), s32[]{:S(2)}) async-start(), calls=%async_computation.6 | async-start | bytes 9437184 | tf_op jit(solution)/shard_map/reduce_scatter | solution.py:700
  193.2 263.8 %reduce-scatter.8.cloned.1.call-start = ((), (), s32[]{:S(2)}) async-start(), calls=%async_computation.7 | async-start | bytes 9437184 | tf_op jit(solution)/shard_map/reduce_scatter | solution.py:700
  199.0 23.5 %slice-start = ((s8[8388608]{0:T(1024)(128)(4,1)}), s8[4194304]{0:T(1024)(128)(4,1)S(1)}, s32[]{:S(2)}) async-start(s8[8388608]{0:T(1024)(128)(4,1)} %bitcast.106), calls=%async_computation.8 | async-start | bytes 8388608
  200.0 27.3 %collective-permute-start = (bf16[240,2048]{1,0:T(8,128)(2,1)}, bf16[240,2048]{1,0:T(8,128)(2,1)}, u32[]{:S(2)}, u32[]{:S(2)}) collective-permute-start(bf16[240,2048]{1,0:T(8,128)(2,1)} %bitcast.15), channel_id=1, source_target_pairs={{0,8},{8,0},{16,24},{24,16},{1,9},{9,1},{17,25},{25,17},{2,10},{10... | collective-permute-start | bytes 2949128 | tf_op jit(solution)/shard_map/ppermute | solution.py:354
  201.5 27.5 %collective-permute-start.1 = (bf16[240,2048]{1,0:T(8,128)(2,1)}, bf16[240,2048]{1,0:T(8,128)(2,1)}, u32[]{:S(2)}, u32[]{:S(2)}) collective-permute-start(bf16[240,2048]{1,0:T(8,128)(2,1)} %bitcast.18), channel_id=1, source_target_pairs={{0,16},{8,24},{16,0},{24,8},{1,17},{9,25},{17,1},{25,9},{2,18},{10... | collective-permute-start | bytes 2949128 | tf_op jit(solution)/shard_map/ppermute | solution.py:354
  230.6 13.5 %collective-permute-start.2 = (bf16[120,2048]{1,0:T(8,128)(2,1)S(1)}, bf16[120,2048]{1,0:T(8,128)(2,1)S(1)}, u32[]{:S(2)}, u32[]{:S(2)}) collective-permute-start(bf16[120,2048]{1,0:T(8,128)(2,1)S(1)} %constant_dynamic-slice_fusion.11), channel_id=1, source_target_pairs={{0,16},{8,24},{16,0},{24,8},{1,17},{9,25},{17,1},{25,9},{2,18},{10... | collective-permute-start | bytes 1474568 | tf_op jit(solution)/shard_map/ppermute | solution.py:354
  233.4 12.1 %collective-permute-start.3 = (bf16[120,2048]{1,0:T(8,128)(2,1)S(1)}, bf16[120,2048]{1,0:T(8,128)(2,1)S(1)}, u32[]{:S(2)}, u32[]{:S(2)}) collective-permute-start(bf16[120,2048]{1,0:T(8,128)(2,1)S(1)} %constant_dynamic-slice_fusion.8), channel_id=1, source_target_pairs={{0,8},{8,0},{16,24},{24,16},{1,9},{9,1},{17,25},{25,17},{2,10},{10... | collective-permute-start | bytes 1474568 | tf_op jit(solution)/shard_map/ppermute | solution.py:354
  246.5 13.5 %collective-permute-start.4 = (bf16[120,2048]{1,0:T(8,128)(2,1)S(1)}, bf16[120,2048]{1,0:T(8,128)(2,1)S(1)}, u32[]{:S(2)}, u32[]{:S(2)}) collective-permute-start(bf16[120,2048]{1,0:T(8,128)(2,1)S(1)} %add_convert_fusion.7.refs_0_), channel_id=1, source_target_pairs={{0,16},{8,24},{16,0},{24,8},{1,17},{9,25},{17,1},{25,9},{2,18},{10... | collective-permute-start | bytes 1474568 | tf_op jit(solution)/shard_map/ppermute | solution.py:354
  246.9 13.9 %collective-permute-start.5 = (bf16[120,2048]{1,0:T(8,128)(2,1)}, bf16[120,2048]{1,0:T(8,128)(2,1)}, u32[]{:S(2)}, u32[]{:S(2)}) collective-permute-start(bf16[120,2048]{1,0:T(8,128)(2,1)} %add_convert_fusion.6.refs_4_), channel_id=1, source_target_pairs={{0,8},{8,0},{16,24},{24,16},{1,9},{9,1},{17,25},{25,17},{2,10},{10... | collective-permute-start | bytes 1474568 | tf_op jit(solution)/shard_map/ppermute | solution.py:354
  260.8 48.4 %collective-permute-start.8 = (bf16[120,2048]{1,0:T(8,128)(2,1)S(1)}, bf16[120,2048]{1,0:T(8,128)(2,1)}, u32[]{:S(2)}, u32[]{:S(2)}) collective-permute-start(bf16[120,2048]{1,0:T(8,128)(2,1)S(1)} %add_convert_fusion.7.refs_0_), channel_id=1, source_target_pairs={{0,8},{8,0},{16,24},{24,16},{1,9},{9,1},{17,25},{25,17},{2,10},{10... | collective-permute-start | bytes 1474568 | tf_op jit(solution)/shard_map/ppermute | solution.py:354
  261.7 47.4 %collective-permute-start.9 = (bf16[120,2048]{1,0:T(8,128)(2,1)}, bf16[120,2048]{1,0:T(8,128)(2,1)}, u32[]{:S(2)}, u32[]{:S(2)}) collective-permute-start(bf16[120,2048]{1,0:T(8,128)(2,1)} %add_convert_fusion.6.refs_4_), channel_id=1, source_target_pairs={{0,16},{8,24},{16,0},{24,8},{1,17},{9,25},{17,1},{25,9},{2,18},{10... | collective-permute-start | bytes 1474568 | tf_op jit(solution)/shard_map/ppermute | solution.py:354
  263.3 39.6 %collective-permute-start.6 = (bf16[352,2048]{1,0:T(8,128)(2,1)}, bf16[352,2048]{1,0:T(8,128)(2,1)}, u32[]{:S(2)}, u32[]{:S(2)}) collective-permute-start(bf16[352,2048]{1,0:T(8,128)(2,1)} %constant_dynamic-slice_fusion.7), channel_id=1, source_target_pairs={{0,8},{8,0},{16,24},{24,16},{1,9},{9,1},{17,25},{25,17},{2,10},{10... | collective-permute-start | bytes 4325384 | tf_op jit(solution)/shard_map/ppermute | solution.py:354
  263.9 41.5 %collective-permute-start.7 = (bf16[352,2048]{1,0:T(8,128)(2,1)S(1)}, bf16[352,2048]{1,0:T(8,128)(2,1)}, u32[]{:S(2)}, u32[]{:S(2)}) collective-permute-start(bf16[352,2048]{1,0:T(8,128)(2,1)S(1)} %constant_dynamic-slice_fusion.6), channel_id=1, source_target_pairs={{0,16},{8,24},{16,0},{24,8},{1,17},{9,25},{17,1},{25,9},{2,18},{10... | collective-permute-start | bytes 4325384 | tf_op jit(solution)/shard_map/ppermute | solution.py:354
  309.2 33.2 %collective-permute-start.10 = (bf16[176,2048]{1,0:T(8,128)(2,1)}, bf16[176,2048]{1,0:T(8,128)(2,1)}, u32[]{:S(2)}, u32[]{:S(2)}) collective-permute-start(bf16[176,2048]{1,0:T(8,128)(2,1)} %constant_dynamic-slice_fusion.5), channel_id=1, source_target_pairs={{0,16},{8,24},{16,0},{24,8},{1,17},{9,25},{17,1},{25,9},{2,18},{10... | collective-permute-start | bytes 2162696 | tf_op jit(solution)/shard_map/ppermute | solution.py:354
  314.0 30.6 %collective-permute-start.11 = (bf16[176,2048]{1,0:T(8,128)(2,1)}, bf16[176,2048]{1,0:T(8,128)(2,1)}, u32[]{:S(2)}, u32[]{:S(2)}) collective-permute-start(bf16[176,2048]{1,0:T(8,128)(2,1)} %constant_dynamic-slice_fusion.4), channel_id=1, source_target_pairs={{0,8},{8,0},{16,24},{24,16},{1,9},{9,1},{17,25},{25,17},{2,10},{10... | collective-permute-start | bytes 2162696 | tf_op jit(solution)/shard_map/ppermute | solution.py:354
  314.0 32.0 %collective-permute-start.12 = (bf16[120,2048]{1,0:T(8,128)(2,1)}, bf16[120,2048]{1,0:T(8,128)(2,1)S(1)}, u32[]{:S(2)}, u32[]{:S(2)}) collective-permute-start(bf16[120,2048]{1,0:T(8,128)(2,1)} %copy-done.17), channel_id=1, source_target_pairs={{0,8},{8,0},{16,24},{24,16},{1,9},{9,1},{17,25},{25,17},{2,10},{10... | collective-permute-start | bytes 1474568 | tf_op jit(solution)/shard_map/ppermute | solution.py:354
  316.1 30.0 %collective-permute-start.13 = (bf16[120,2048]{1,0:T(8,128)(2,1)}, bf16[120,2048]{1,0:T(8,128)(2,1)}, u32[]{:S(2)}, u32[]{:S(2)}) collective-permute-start(bf16[120,2048]{1,0:T(8,128)(2,1)} %collective-permute-done.5.refs_5_), channel_id=1, source_target_pairs={{0,16},{8,24},{16,0},{24,8},{1,17},{9,25},{17,1},{25,9},{2,18},{10... | collective-permute-start | bytes 1474568 | tf_op jit(solution)/shard_map/ppermute | solution.py:354
  347.6 14.1 %collective-permute-start.14 = (bf16[176,2048]{1,0:T(8,128)(2,1)S(1)}, bf16[176,2048]{1,0:T(8,128)(2,1)S(1)}, u32[]{:S(2)}, u32[]{:S(2)}) collective-permute-start(bf16[176,2048]{1,0:T(8,128)(2,1)S(1)} %copy-done.5), channel_id=1, source_target_pairs={{0,16},{8,24},{16,0},{24,8},{1,17},{9,25},{17,1},{25,9},{2,18},{10... | collective-permute-start | bytes 2162696 | tf_op jit(solution)/shard_map/ppermute | solution.py:354
  349.5 13.6 %collective-permute-start.15 = (bf16[176,2048]{1,0:T(8,128)(2,1)S(1)}, bf16[176,2048]{1,0:T(8,128)(2,1)}, u32[]{:S(2)}, u32[]{:S(2)}) collective-permute-start(bf16[176,2048]{1,0:T(8,128)(2,1)S(1)} %add_convert_fusion.4.refs_4_), channel_id=1, source_target_pairs={{0,8},{8,0},{16,24},{24,16},{1,9},{9,1},{17,25},{25,17},{2,10},{10... | collective-permute-start | bytes 2162696 | tf_op jit(solution)/shard_map/ppermute | solution.py:354
  365.5 14.3 %collective-permute-start.17 = (bf16[512,768]{1,0:T(8,128)(2,1)}, bf16[512,768]{1,0:T(8,128)(2,1)S(1)}, u32[]{:S(2)}, u32[]{:S(2)}) collective-permute-start(bf16[512,768]{1,0:T(8,128)(2,1)} %get-tuple-element.330), channel_id=1, source_target_pairs={{0,16},{8,24},{16,0},{24,8},{1,17},{9,25},{17,1},{25,9},{2,18},{10... | collective-permute-start | bytes 2359304 | tf_op jit(solution)/shard_map/ppermute | solution.py:354
  366.6 14.3 %collective-permute-start.16 = (bf16[512,768]{1,0:T(8,128)(2,1)S(1)}, bf16[512,768]{1,0:T(8,128)(2,1)}, u32[]{:S(2)}, u32[]{:S(2)}) collective-permute-start(bf16[512,768]{1,0:T(8,128)(2,1)S(1)} %get-tuple-element.331), channel_id=1, source_target_pairs={{0,8},{8,0},{16,24},{24,16},{1,9},{9,1},{17,25},{25,17},{2,10},{10... | collective-permute-start | bytes 2359304 | tf_op jit(solution)/shard_map/ppermute | solution.py:354
  384.0 12.3 %collective-permute-start.20 = (bf16[256,768]{1,0:T(8,128)(2,1)S(1)}, bf16[256,768]{1,0:T(8,128)(2,1)S(1)}, u32[]{:S(2)}, u32[]{:S(2)}) collective-permute-start(bf16[256,768]{1,0:T(8,128)(2,1)S(1)} %constant_dynamic-slice_fusion.2), channel_id=1, source_target_pairs={{0,16},{8,24},{16,0},{24,8},{1,17},{9,25},{17,1},{25,9},{2,18},{10... | collective-permute-start | bytes 1179656 | tf_op jit(solution)/shard_map/ppermute | solution.py:354
  385.3 12.2 %collective-permute-start.21 = (bf16[256,768]{1,0:T(8,128)(2,1)}, bf16[256,768]{1,0:T(8,128)(2,1)S(1)}, u32[]{:S(2)}, u32[]{:S(2)}) collective-permute-start(bf16[256,768]{1,0:T(8,128)(2,1)} %constant_dynamic-slice_fusion), channel_id=1, source_target_pairs={{0,8},{8,0},{16,24},{24,16},{1,9},{9,1},{17,25},{25,17},{2,10},{10... | collective-permute-start | bytes 1179656 | tf_op jit(solution)/shard_map/ppermute | solution.py:354
  386.0 26.9 %collective-permute-start.18 = (bf16[176,2048]{1,0:T(8,128)(2,1)}, bf16[176,2048]{1,0:T(8,128)(2,1)S(1)}, u32[]{:S(2)}, u32[]{:S(2)}) collective-permute-start(bf16[176,2048]{1,0:T(8,128)(2,1)} %add_convert_fusion.5.refs_0_), channel_id=1, source_target_pairs={{0,8},{8,0},{16,24},{24,16},{1,9},{9,1},{17,25},{25,17},{2,10},{10... | collective-permute-start | bytes 2162696 | tf_op jit(solution)/shard_map/ppermute | solution.py:354
  387.3 25.6 %collective-permute-start.19 = (bf16[176,2048]{1,0:T(8,128)(2,1)}, bf16[176,2048]{1,0:T(8,128)(2,1)S(1)}, u32[]{:S(2)}, u32[]{:S(2)}) collective-permute-start(bf16[176,2048]{1,0:T(8,128)(2,1)} %copy-done.6), channel_id=1, source_target_pairs={{0,16},{8,24},{16,0},{24,8},{1,17},{9,25},{17,1},{25,9},{2,18},{10... | collective-permute-start | bytes 2162696 | tf_op jit(solution)/shard_map/ppermute | solution.py:354
  388.1 45.9 %collective-permute-start.23 = (bf16[176,2048]{1,0:T(8,128)(2,1)}, bf16[176,2048]{1,0:T(8,128)(2,1)}, u32[]{:S(2)}, u32[]{:S(2)}) collective-permute-start(bf16[176,2048]{1,0:T(8,128)(2,1)} %copy-done.14), channel_id=1, source_target_pairs={{0,8},{8,0},{16,24},{24,16},{1,9},{9,1},{17,25},{25,17},{2,10},{10... | collective-permute-start | bytes 2162696 | tf_op jit(solution)/shard_map/ppermute | solution.py:354
  396.2 37.7 %collective-permute-start.24 = (bf16[176,2048]{1,0:T(8,128)(2,1)}, bf16[176,2048]{1,0:T(8,128)(2,1)}, u32[]{:S(2)}, u32[]{:S(2)}) collective-permute-start(bf16[176,2048]{1,0:T(8,128)(2,1)} %collective-permute-done.15.refs_5_), channel_id=1, source_target_pairs={{0,16},{8,24},{16,0},{24,8},{1,17},{9,25},{17,1},{25,9},{2,18},{10... | collective-permute-start | bytes 2162696 | tf_op jit(solution)/shard_map/ppermute | solution.py:354
  397.4 50.5 %copy-start.11 = (bf16[256,768]{1,0:T(8,128)(2,1)}, bf16[256,768]{1,0:T(8,128)(2,1)S(1)}, u32[]{:S(2)}) copy-start(bf16[256,768]{1,0:T(8,128)(2,1)S(1)} %add_convert_fusion.9.refs_0_) | copy-start | bytes 1179652
  397.6 50.3 %copy-start.12 = (bf16[256,768]{1,0:T(8,128)(2,1)}, bf16[256,768]{1,0:T(8,128)(2,1)S(1)}, u32[]{:S(2)}) copy-start(bf16[256,768]{1,0:T(8,128)(2,1)S(1)} %add_convert_fusion.8.refs_4_) | copy-start | bytes 1179652
  413.8 20.2 %collective-permute-start.25 = (bf16[256,768]{1,0:T(8,128)(2,1)S(1)}, bf16[256,768]{1,0:T(8,128)(2,1)S(1)}, u32[]{:S(2)}, u32[]{:S(2)}) collective-permute-start(bf16[256,768]{1,0:T(8,128)(2,1)S(1)} %add_convert_fusion.9.refs_0_), channel_id=1, source_target_pairs={{0,16},{8,24},{16,0},{24,8},{1,17},{9,25},{17,1},{25,9},{2,18},{10... | collective-permute-start | bytes 1179656 | tf_op jit(solution)/shard_map/ppermute | solution.py:354
  414.6 19.4 %collective-permute-start.26 = (bf16[256,768]{1,0:T(8,128)(2,1)S(1)}, bf16[256,768]{1,0:T(8,128)(2,1)S(1)}, u32[]{:S(2)}, u32[]{:S(2)}) collective-permute-start(bf16[256,768]{1,0:T(8,128)(2,1)S(1)} %add_convert_fusion.8.refs_4_), channel_id=1, source_target_pairs={{0,8},{8,0},{16,24},{24,16},{1,9},{9,1},{17,25},{25,17},{2,10},{10... | collective-permute-start | bytes 1179656 | tf_op jit(solution)/shard_map/ppermute | solution.py:354
  415.8 18.2 %collective-permute-start.22 = (f32[6,128]{1,0:T(8,128)S(1)}, f32[6,128]{1,0:T(8,128)S(1)}, u32[]{:S(2)}, u32[]{:S(2)}) collective-permute-start(f32[6,128]{1,0:T(8,128)S(1)} %bitcast.131), channel_id=1, source_target_pairs={{0,8},{8,0},{16,24},{24,16},{1,9},{9,1},{17,25},{25,17},{2,10},{10... | collective-permute-start | bytes 9224 | tf_op jit(solution)/shard_map/ppermute | solution.py:354
  434.0 14.1 %collective-permute-start.28 = (bf16[256,768]{1,0:T(8,128)(2,1)S(1)}, bf16[256,768]{1,0:T(8,128)(2,1)S(1)}, u32[]{:S(2)}, u32[]{:S(2)}) collective-permute-start(bf16[256,768]{1,0:T(8,128)(2,1)S(1)} %add_convert_fusion.9.refs_0_), channel_id=1, source_target_pairs={{0,8},{8,0},{16,24},{24,16},{1,9},{9,1},{17,25},{25,17},{2,10},{10... | collective-permute-start | bytes 1179656 | tf_op jit(solution)/shard_map/ppermute | solution.py:354
  434.8 13.3 %collective-permute-start.29 = (bf16[256,768]{1,0:T(8,128)(2,1)S(1)}, bf16[256,768]{1,0:T(8,128)(2,1)S(1)}, u32[]{:S(2)}, u32[]{:S(2)}) collective-permute-start(bf16[256,768]{1,0:T(8,128)(2,1)S(1)} %collective-permute-done.25.refs_1_), channel_id=1, source_target_pairs={{0,8},{8,0},{16,24},{24,16},{1,9},{9,1},{17,25},{25,17},{2,10},{10... | collective-permute-start | bytes 1179656 | tf_op jit(solution)/shard_map/ppermute | solution.py:354
  436.1 12.1 %collective-permute-start.30 = (bf16[256,768]{1,0:T(8,128)(2,1)S(1)}, bf16[256,768]{1,0:T(8,128)(2,1)S(1)}, u32[]{:S(2)}, u32[]{:S(2)}) collective-permute-start(bf16[256,768]{1,0:T(8,128)(2,1)S(1)} %add_convert_fusion.8.refs_4_), channel_id=1, source_target_pairs={{0,16},{8,24},{16,0},{24,8},{1,17},{9,25},{17,1},{25,9},{2,18},{10... | collective-permute-start | bytes 1179656 | tf_op jit(solution)/shard_map/ppermute | solution.py:354
  436.4 11.8 %collective-permute-start.31 = (bf16[256,768]{1,0:T(8,128)(2,1)S(1)}, bf16[256,768]{1,0:T(8,128)(2,1)S(1)}, u32[]{:S(2)}, u32[]{:S(2)}) collective-permute-start(bf16[256,768]{1,0:T(8,128)(2,1)S(1)} %collective-permute-done.26.refs_5_), channel_id=1, source_target_pairs={{0,16},{8,24},{16,0},{24,8},{1,17},{9,25},{17,1},{25,9},{2,18},{10... | collective-permute-start | bytes 1179656 | tf_op jit(solution)/shard_map/ppermute | solution.py:354
  438.1 10.0 %collective-permute-start.27 = (f32[6,128]{1,0:T(8,128)S(1)}, f32[6,128]{1,0:T(8,128)S(1)}, u32[]{:S(2)}, u32[]{:S(2)}) collective-permute-start(f32[6,128]{1,0:T(8,128)S(1)} %add.369), channel_id=1, source_target_pairs={{0,16},{8,24},{16,0},{24,8},{1,17},{9,25},{17,1},{25,9},{2,18},{10... | collective-permute-start | bytes 9224 | tf_op jit(solution)/shard_map/ppermute | solution.py:354
  450.2 33.3 %copy-start.1 = (bf16[704,2048]{1,0:T(8,128)(2,1)S(1)}, bf16[704,2048]{1,0:T(8,128)(2,1)}, u32[]{:S(2)}) copy-start(bf16[704,2048]{1,0:T(8,128)(2,1)} %param.23) | copy-start | bytes 8650756
  462.1 1.4 collective-permute-start.32
  464.3 4.0 collective-permute-start.33
  468.3 4.9 collective-permute-start.34
  473.2 4.0 collective-permute-start.35
  477.2 4.0 collective-permute-start.36
  (28 other events, 182.9 us)
Sparse Core Ops, SparseCore 0:
  11.5 84.7 all-gather.2
  97.9 80.5 all-gather.4
  180.7 88.0 reduce-scatter.3
  271.5 88.0 reduce-scatter.5
  361.7 88.0 reduce-scatter.7

commit v6 on v5

--- a/solution.py
+++ b/solution.py
@@ -350,8 +350,12 @@
 
 
 def swap(values, name, bit):
+    return swap_mask(values, name, 1 << bit)
+
+
+def swap_mask(values, name, mask):
     size = lax.axis_size(name)
-    return lax.ppermute(values, name, [(i, i ^ (1 << bit)) for i in range(size)])
+    return lax.ppermute(values, name, [(i, i ^ mask) for i in range(size)])
 
 
 def write_stacked(piece, outs):
@@ -372,32 +376,35 @@
         outs[0][part] = piece[:, part * size : (part + 1) * size].astype(F32)
 
 
-def place_kernel(write, count, color_ref, where_ref, *refs):
+def place_kernel(write, count, outs_at, color_ref, where_ref, *refs):
     step = pl.program_id(0)
     for number in range(count):
 
         @pl.when(step == number)
         def _(number=number):
-            write(refs[number][...], refs[count:])
-
-
-def place_blocks(write, color, where, pieces, out_shapes, out_specs):
+            write(refs[number][...], refs[outs_at:])
+
+
+def place_blocks(write, color, where, pieces, out_shapes, out_specs, into):
     rows, columns = pieces[0].shape
     count = len(pieces)
+    outs_at = count + len(into)
     return pl.pallas_call(
-        functools.partial(place_kernel, write, count),
+        functools.partial(place_kernel, write, count, outs_at),
         grid_spec=pltpu.PrefetchScalarGridSpec(
             num_scalar_prefetch=2,
             grid=(count,),
-            in_specs=[pl.BlockSpec((rows, columns), lambda i, c, w: (0, 0))] * count,
+            in_specs=[pl.BlockSpec((rows, columns), lambda i, c, w: (0, 0))] * count
+            + [pl.BlockSpec(memory_space=pl.ANY)] * len(into),
             out_specs=out_specs,
         ),
         out_shape=[jax.ShapeDtypeStruct(shape, F32) for shape in out_shapes],
         cost_estimate=pl.CostEstimate(
             flops=0, bytes_accessed=6 * count * rows * columns, transcendentals=0
         ),
+        input_output_aliases={2 + count + number: number for number in range(len(into))},
         name="place_blocks",
-    )(color, where, *pieces)
+    )(color, where, *pieces, *into)
 
 
 class DpSum:
@@ -483,10 +490,10 @@
     def fresh(self):
         return [held[len(held) // 2][0] for held in self.held]
 
-    def result(self, write):
+    def result(self, write, skip=0, into=()):
         pieces, colors, where = [], [], []
         for color in range(2):
-            for piece, mask in self.held[color]:
+            for piece, mask in self.held[color][skip:]:
                 owner = self.mine ^ mask
                 spot = 0 if self.paired else color
                 for bit in self.orders[color]:
@@ -519,6 +526,7 @@
             pieces,
             shapes,
             [pl.BlockSpec(block, out_map) for block in blocks],
+            into,
         )
 
 
@@ -539,6 +547,16 @@
     for bit in range(count) if bits is None else bits:
         values = values + swap(values, name, bit)
     return values
+
+
+def sum_pairs(values, name):
+    count = bits_of(name)
+    if count is None:
+        return lax.psum(values, name)
+    for bit in range(0, count - 1, 2):
+        one, two, both = (swap_mask(values, name, mask << bit) for mask in (1, 2, 3))
+        values = (values + one) + (two + both)
+    return values + swap(values, name, count - 1) if count % 2 else values
 
 
 def norm_kernel(x_ref, gain_ref, shift_ref, out_ref):
@@ -782,19 +800,21 @@
         sum_gate_up.send()
         sum_gate_up.arrive()
     down_sums, bias_sums = fence((down_sums, bias_sums), sum_gate_up, sum_qkv)
+    placed = len(sum_qkv.held[0])
+    early = sum_qkv.result(write_lanes)
     while sum_qkv.level < 2 * sum_qkv.count:
         sum_qkv.send()
         sum_qkv.arrive()
     (grad_w_gate_up,) = sum_gate_up.result(write_stacked)
     bias_sums = sum_small(bias_sums, "dp", range(1, sum_qkv.count))
-    grad_w_gate_up, bias_sums = fence((grad_w_gate_up, bias_sums), sum_qkv)
-    (grad_w_qkv,) = sum_qkv.result(write_lanes)
+    grad_w_gate_up, bias_sums, early = fence((grad_w_gate_up, bias_sums, early), sum_qkv)
+    (grad_w_qkv,) = sum_qkv.result(write_lanes, placed, early)
     grad_w_down, grad_w_out = down_sums
     grad_normed, grad_w_gate_up, grad_w_qkv = fence(
         (grad_normed, grad_w_gate_up, grad_w_qkv)
     )
     input_grad, small = tail(layer_in, grad_normed, cot_here, norm_gain, stat_row)
-    small = sum_small(sum_small(small, "mp"), "dp")
+    small = sum_pairs(sum_pairs(small, "mp"), "dp")
     totals = small[2]
     return (
         layer_out[:, None],

time: 495 us -> 497 us (level)
  waiting for transfers between devices: 131 us -> 117 us
  Pallas kernels: 131 us -> 142 us
    ppermute x37 -> x39, waiting for transfers between devices: 54.5 us -> 43.5 us  [swap_mask(): return lax.ppermute(values, name, [(i, i ^ mask) for i in range(size)])]
    ppermute x37 -> x39, starting transfers between devices: 43.5 us -> 41.5 us  [swap_mask(): return lax.ppermute(values, name, [(i, i ^ mask) for i in range(size)])]
    pallas_call x3 -> x4, Pallas kernels: 22.7 us -> 24.5 us  [place_blocks(): pl.pallas_call(functools.partial(place_kernel, write, count, outs_at), gr...]
  transfers between devices with their start and end apart: 42 -> 44, of which waited for: 18 -> 13; matrix products, arithmetic and copies ran while one was open for 32% -> 32% of each run, Pallas kernels for 25% -> 27%
where the time goes in v6:
time: 497 us; the launch traced here: 488 us
  Pallas kernels  142 us (29%)
  waiting for transfers between devices  117 us (24%)
  matrix products  105 us (21%)
  starting transfers between devices  42.6 us (9%)
  other arithmetic  40.1 us (8%)
  local copies, waits for them, and re-layouts  25.1 us (5%)
  between operations  15.9 us (3%)
    all_gather x1, waiting for transfers between devices, local(): gathered = lax.all_gather(normed, 'mp', axis=0, tiled=True)  73.5 us
    dot_general x5, matrix products, token_sum(): lax.dot_general(left, right, (((0,), (0,)), ((), ())), preferred_element_...  46 us
    ppermute x39, waiting for transfers between devices, swap_mask(): return lax.ppermute(values, name, [(i, i ^ mask) for i in range(size)])  43.5 us
    dot_general x4, matrix products, turned_product(): lax.dot_general(left, right, (((1,), (1,)), ((), ())), preferred_element_...  43.2 us
    ppermute x39, starting transfers between devices, swap_mask(): return lax.ppermute(values, name, [(i, i ^ mask) for i in range(size)])  41.5 us
    pallas_call x1, Pallas kernels, attend_back(): pl.pallas_call(attend_back_kernel, grid_spec=pltpu.PrefetchScalarGridSpec...  39.8 us
    pallas_call x1, Pallas kernels, attend(): pl.pallas_call(attend_kernel, grid_spec=pltpu.PrefetchScalarGridSpec(num_...  29.1 us
    pallas_call x1, Pallas kernels, back_products(): pl.pallas_call(back_products_kernel, grid=(length // rows,), in_specs=[pl...  26.3 us
  transfers between devices with their start and end apart: 44, of which 13 were waited for; matrix products, arithmetic and copies ran while one was open for 32% of the time, Pallas kernels for 27%

profile of v6, /device:TPU:0, one launch (start us, length us, event | category | flops | bytes accessed | tf_op | source)
XLA Modules:
  0.0 488.2 jit_solution(17283463146399188288)
XLA Ops:
  7.2 4.1 norm.1
  12.6 2.3 bitcast_select_fusion.c_ref
  17.0 5.8 %fusion.13 = (f32[2048,128]{1,0:T(8,128)}, f32[2048,128]{1,0:T(8,128)}, f32[2048,128]{1,0:T(8,128)}) fusion(f32[128]{0:T(128)S(1)} %compare_select_fusion.5, f32[2048]{0:T(1024)S(1)} %fusion.17, pred[128]{0:T(512)(128)(4,1)S(1)} %get-tuple-element.337, pred[128]{0:T(512)(128)(4,1)S(1)} %get-tuple-element.338), kind=kLoop, calls=%fused_computation.42 | loop fusion | flops 1048576 | bytes 3154688 | tf_op jit(solution)/shard_map/jit(_where)/select_n | solution.py:41
  22.8 73.5 %all-gather.3.cloned.1.call-done.x_ref = bf16[2048,2048]{1,0:T(8,128)(2,1)} async-done(((bf16[256,2048]{1,0:T(8,128)(2,1)}), bf16[2048,2048]{1,0:T(8,128)(2,1)}) %all-gather.3.cloned.1.call-update) | async-done | bytes 8388624 | tf_op jit(solution)/shard_map/all_gather | solution.py:691
  96.3 10.1 %fusion.6 = f32[2048,704]{1,0:T(8,128)S(1)} fusion(bf16[2048,2048]{1,0:T(8,128)(2,1)} %all-gather.3.cloned.1.call-done.x_ref, bf16[2,704,2048]{2,1,0:T(8,128)(2,1)} %bitcast.112), kind=kOutput, calls=%fused_computation.20 | convolution fusion | flops 5905580032 | bytes 17039360 | tf_op jit(solution)/shard_map/dot_general | solution.py:708
  106.4 13.1 %multiply_convert_fusion = (bf16[2048,704]{1,0:T(8,128)(2,1)S(1)}, f32[2048,704]{1,0:T(8,128)}) fusion(f32[2048,704]{1,0:T(8,128)S(1)} %fusion.6, bf16[2048,2048]{1,0:T(8,128)(2,1)S(1)} %copy-done.28, bf16[2,704,2048]{2,1,0:T(8,128)(2,1)} %bitcast.113), kind=kOutput, calls=%fused_computation.10 | convolution fusion | flops 5914230784 | bytes 25690112 | tf_op jit(solution)/shard_map/dot_general | solution.py:708
  119.5 1.7 copy-done.29
  121.2 8.9 %convolution_convert_fusion.1 = bf16[2048,2048]{1,0:T(8,128)(2,1)} fusion(bf16[2048,704]{1,0:T(8,128)(2,1)S(1)} %get-tuple-element.335, bf16[704,2048]{1,0:T(8,128)(2,1)S(1)} %copy-done), kind=kOutput, calls=%fused_computation.3 | convolution fusion | flops 5909774336 | bytes 14155776 | tf_op jit(solution)/shard_map/dot_general | solution.py:705
  130.4 13.2 %project.1 = (bf16[2048,256]{1,0:T(8,128)(2,1)}, bf16[2048,256]{1,0:T(8,128)(2,1)}, bf16[2048,256]{1,0:T(8,128)(2,1)}) custom-call(bf16[2048,2048]{1,0:T(8,128)(2,1)} %all-gather.3.cloned.1.call-done.x_ref, bf16[3,2048,256]{2,1,0:T(8,128)(2,1)} %bitcast.115, bf16[3,256]{1,0:T(4,128)(2,1)} %b_ref.1, f32[2048,128]{1,0:T(8,128)} %get-tuple-element.161.cos_ref, ...), custom_call_target="tpu_custom_call" | custom-call | flops 6442450944 | bytes 14680064 | tf_op jit(solution)/shard_map/project/pallas_call | solution.py:78
  143.6 29.1 %attend.1 = (bf16[2048,256]{1,0:T(8,128)(2,1)}, f32[16,1,512]{2,1,0:T(1,128)}) custom-call(s32[16]{0:T(128)} %and_select_fusion.first_ref, bf16[2048,256]{1,0:T(8,128)(2,1)} %get-tuple-element.164.q_ref, bf16[2048,256]{1,0:T(8,128)(2,1)} %get-tuple-element.165.k_ref, bf16[2048,256]{1,0:T(8,128)(2,1)} %get-tuple-element.166.v_ref, s32[16,1,128]{2,1,0:T(1,128)} %copy-done.26), custom_call_target="tpu_custom_call" | custom-call | flops 8589934592 | bytes 4194304 | tf_op jit(solution)/shard_map/attend/pallas_call | solution.py:181
  172.7 7.3 %convolution_convert_fusion = bf16[2048,2048]{1,0:T(8,128)(2,1)} fusion(bf16[2048,256]{1,0:T(8,128)(2,1)} %get-tuple-element.168.o_ref, bf16[256,2048]{1,0:T(8,128)(2,1)} %param.22), kind=kOutput, calls=%fused_computation.2 | convolution fusion | flops 2151677952 | bytes 10485760 | tf_op jit(solution)/shard_map/dot_general | solution.py:705
  180.1 7.2 %convolution_convert_fusion.8 = bf16[256,2048]{1,0:T(8,128)(2,1)} fusion(bf16[2048,256]{1,0:T(8,128)(2,1)} %get-tuple-element.168.o_ref, bf16[2048,2048]{1,0:T(8,128)(2,1)} %all-gather.5.cloned.1.call-done), kind=kOutput, calls=%fused_computation.29 | convolution fusion | flops 2148007936 | bytes 10485760 | tf_op jit(solution)/shard_map/dot_general | solution.py:713
  188.2 7.6 %convolution_convert_fusion.6 = bf16[704,2048]{1,0:T(8,128)(2,1)} fusion(bf16[2048,704]{1,0:T(8,128)(2,1)S(1)} %copy-done.30, bf16[2048,2048]{1,0:T(8,128)(2,1)S(1)} %copy-done.2), kind=kOutput, calls=%fused_computation.16 | convolution fusion | flops 5907021824 | bytes 14155776 | tf_op jit(solution)/shard_map/dot_general | solution.py:713
  196.4 2.0 constant_dynamic-slice_fusion.9
  198.4 2.1 constant_dynamic-slice_fusion.10
  202.7 3.0 collective-permute-start.1
  205.6 15.3 %fusion.4 = (bf16[2048,704]{1,0:T(8,128)(2,1)}, bf16[2048,704]{1,0:T(8,128)(2,1)S(1)}) fusion(f32[2048,704]{1,0:T(8,128)} %copy-done.31, f32[2048,704]{1,0:T(8,128)} %get-tuple-element.336, bf16[2048,2048]{1,0:T(8,128)(2,1)} %all-gather.5.cloned.1.call-done, bf16[704,2048]{1,0:T(8,128)(2,1)S(1)} %copy-done), kind=kOutput, calls=%fused_computation.8 | convolution fusion | flops 5927206912 | bytes 28573696 | tf_op jit(solution)/shard_map/dot_general | solution.py:708
  222.1 4.7 convolution_convert_fusion.7.do_ref
  227.0 1.6 fusion.12
  228.6 1.6 fusion.11
  230.3 1.5 collective-permute-start.2
  233.2 9.8 %convolution_convert_fusion.5 = bf16[704,2048]{1,0:T(8,128)(2,1)} fusion(bf16[2048,704]{1,0:T(8,128)(2,1)S(1)} %get-tuple-element.174.g_ref, bf16[2048,2048]{1,0:T(8,128)(2,1)} %all-gather.3.cloned.1.call-done.x_ref), kind=kOutput, calls=%fused_computation.15 | convolution fusion | flops 5907021824 | bytes 14155776 | tf_op jit(solution)/shard_map/dot_general | solution.py:713
  246.8 9.8 %convolution_convert_fusion.4 = bf16[704,2048]{1,0:T(8,128)(2,1)S(1)} fusion(bf16[2048,704]{1,0:T(8,128)(2,1)} %get-tuple-element.179.u_ref, bf16[2048,2048]{1,0:T(8,128)(2,1)} %all-gather.3.cloned.1.call-done.x_ref), kind=kOutput, calls=%fused_computation.14 | convolution fusion | flops 5907021824 | bytes 14155776 | tf_op jit(solution)/shard_map/dot_general | solution.py:713
  263.6 39.8 %attend_back.1.p_ref = bf16[2048,768]{1,0:T(8,128)(2,1)} custom-call(s32[16]{0:T(128)} %and_select_fusion.first_ref, bf16[2048,256]{1,0:T(8,128)(2,1)} %get-tuple-element.164.q_ref, bf16[2048,256]{1,0:T(8,128)(2,1)} %get-tuple-element.165.k_ref, bf16[2048,256]{1,0:T(8,128)(2,1)} %get-tuple-element.166.v_ref, ...), custom_call_target="tpu_custom_call" | custom-call | flops 21474836480 | bytes 8388608 | tf_op jit(solution)/shard_map/attend_back/pallas_call | solution.py:312
  303.4 2.5 add_convert_fusion.1
  306.1 1.9 add_convert_fusion
  309.8 1.6 collective-permute-start.10
  314.0 26.3 %back_products.1 = bf16[2048,2048]{1,0:T(8,128)(2,1)} custom-call(bf16[2048,768]{1,0:T(8,128)(2,1)} %attend_back.1.p_ref, bf16[3,2048,256]{2,1,0:T(8,128)(2,1)} %bitcast.116, bf16[2048,704]{1,0:T(8,128)(2,1)} %copy-done.4, bf16[2048,704]{1,0:T(8,128)(2,1)} %get-tuple-element.179.u_ref, bf16[2,704,2048]{2,1,0:T(8,128)(2,1)} %bitcast.114), custom_call_target="tpu_custom_call" | custom-call | tf_op jit(solution)/shard_map/back_products/pallas_call | solution.py:650
  340.2 2.2 add_convert_fusion.5.refs_0_
  345.4 1.6 collective-permute-start.14
  347.6 11.6 %convolution_convert_fusion.3 = bf16[2048,768]{1,0:T(8,128)(2,1)} fusion(bf16[2048,2048]{1,0:T(8,128)(2,1)} %all-gather.3.cloned.1.call-done.x_ref, bf16[2048,768]{1,0:T(8,128)(2,1)} %attend_back.1.p_ref), kind=kOutput, calls=%fused_computation.13 | convolution fusion | flops 6444023808 | bytes 14680064 | tf_op jit(solution)/shard_map/dot_general | solution.py:713
  360.2 2.4 constant_dynamic-slice_fusion.1
  364.4 2.6 convert_reduce_fusion
  367.1 10.0 %collective-permute-done.17 = bf16[512,768]{1,0:T(8,128)(2,1)S(1)} collective-permute-done((bf16[512,768]{1,0:T(8,128)(2,1)}, bf16[512,768]{1,0:T(8,128)(2,1)S(1)}, u32[]{:S(2)}, u32[]{:S(2)}) %collective-permute-start.17) | collective-permute-done | bytes 786464 | tf_op jit(solution)/shard_map/ppermute | solution.py:358
  378.0 2.3 add_convert_fusion.2
  386.4 3.0 fusion.8
  390.1 3.3 select_maximum_fusion
  394.4 15.0 %collective-permute-done.18.refs_2_ = bf16[176,2048]{1,0:T(8,128)(2,1)S(1)} collective-permute-done((bf16[176,2048]{1,0:T(8,128)(2,1)}, bf16[176,2048]{1,0:T(8,128)(2,1)S(1)}, u32[]{:S(2)}, u32[]{:S(2)}) %collective-permute-start.18) | collective-permute-done | bytes 720928 | tf_op jit(solution)/shard_map/ppermute | solution.py:358
  414.1 7.3 %place_blocks.4 = (f32[704,2048]{1,0:T(8,128)}, f32[256,2048]{1,0:T(8,128)}) custom-call(s32[8]{0:T(128)} %constant.124.clone.color_ref, s32[8]{0:T(128)} %stack.112.where_ref, bf16[120,2048]{1,0:T(8,128)(2,1)} %copy-done.10, bf16[120,2048]{1,0:T(8,128)(2,1)} %copy-done.17, bf16[120,2048]{1,0:T(8,128)(2,1)} %collective-permute-done.8.refs_2_, ...), custom_call_target="tpu_custom_call" | custom-call | bytes 11796480 | tf_op jit(solution)/shard_map/place_blocks/pallas_call | solution.py:392
  421.3 8.8 %collective-permute-done.22 = f32[6,128]{1,0:T(8,128)S(1)} collective-permute-done((f32[6,128]{1,0:T(8,128)S(1)}, f32[6,128]{1,0:T(8,128)S(1)}, u32[]{:S(2)}, u32[]{:S(2)}) %collective-permute-start.22) | collective-permute-done | bytes 3104 | tf_op jit(solution)/shard_map/ppermute | solution.py:358
  430.2 1.5 collective-permute-start.28
  436.4 4.2 place_blocks.6.refs_4_
  441.2 8.7 %place_blocks.5 = f32[2,704,2048]{2,1,0:T(8,128)} custom-call(s32[8]{0:T(128)} %constant.124.clone.color_ref, s32[8]{0:T(128)} %stack.121.where_ref, bf16[176,2048]{1,0:T(8,128)(2,1)} %add_convert_fusion.5.refs_0_, bf16[176,2048]{1,0:T(8,128)(2,1)} %copy-done.14, bf16[176,2048]{1,0:T(8,128)(2,1)} %copy-done.15, ...), custom_call_target="tpu_custom_call" | custom-call | bytes 17301504 | tf_op jit(solution)/shard_map/place_blocks/pallas_call | solution.py:392
  452.9 4.4 place_blocks.7
  457.3 5.1 %tail.1 = (f32[256,1,2048]{2,1,0:T(1,128)}, f32[4,2048]{1,0:T(4,128)}) custom-call(bf16[256,2048]{1,0:T(8,128)(2,1)} %bitcast.111, bf16[256,2048]{1,0:T(8,128)(2,1)} %reduce-scatter.8.cloned.1.call-done.g_ref, bf16[256,2048]{1,0:T(8,128)(2,1)} %bitcast_select_fusion.c_ref, f32[1,2048]{1,0:T(1,128)} %bitcast.128, f32[1,2048]{1,0:T(1,128)} %bitcast.129), custom_call_target="tpu_custom_call" | custom-call | tf_op jit(solution)/shard_map/tail/pallas_call | solution.py:614
  462.5 1.8 collective-permute-start.32
  464.3 1.7 collective-permute-done.34
  468.8 3.6 collective-permute-done.35
  (195 shorter events, 64.1 us)
Async XLA Ops:
  7.2 114.0 %copy-start = (bf16[704,2048]{1,0:T(8,128)(2,1)S(1)}, bf16[704,2048]{1,0:T(8,128)(2,1)}, u32[]{:S(2)}) copy-start(bf16[704,2048]{1,0:T(8,128)(2,1)} %param.24) | copy-start | bytes 8650756
  7.2 89.1 %all-gather.3.cloned.1.call-start = ((), (), s32[]{:S(2)}) async-start(), calls=%async_computation.3 | async-start | bytes 9437184 | tf_op jit(solution)/shard_map/all_gather | solution.py:691
  11.3 168.7 %all-gather.5.cloned.1.call-start = ((), (), s32[]{:S(2)}) async-start(), calls=%async_computation.4 | async-start | bytes 9437184 | tf_op jit(solution)/shard_map/all_gather | solution.py:692
  14.9 294.9 %reduce-scatter.4.cloned.1.call-start = ((), (), s32[]{:S(2)}) async-start(), calls=%async_computation.5 | async-start | bytes 9437184 | tf_op jit(solution)/shard_map/reduce_scatter | solution.py:718
  16.0 90.4 %copy-start.26 = (s32[16,1,128]{2,1,0:T(1,128)}, s32[16,1,128]{2,1,0:T(1,128)S(1)}, u32[]{:S(2)}) copy-start(s32[16,1,128]{2,1,0:T(1,128)S(1)} %broadcast_maximum_fusion.start_ref) | copy-start | bytes 24580
  130.1 251.0 %reduce-scatter.6.cloned.1.call-start = ((), (), s32[]{:S(2)}) async-start(), calls=%async_computation.6 | async-start | bytes 9437184 | tf_op jit(solution)/shard_map/reduce_scatter | solution.py:718
  195.8 261.5 %reduce-scatter.8.cloned.1.call-start = ((), (), s32[]{:S(2)}) async-start(), calls=%async_computation.7 | async-start | bytes 9437184 | tf_op jit(solution)/shard_map/reduce_scatter | solution.py:718
  202.6 24.3 %collective-permute-start = (bf16[240,2048]{1,0:T(8,128)(2,1)}, bf16[240,2048]{1,0:T(8,128)(2,1)}, u32[]{:S(2)}, u32[]{:S(2)}) collective-permute-start(bf16[240,2048]{1,0:T(8,128)(2,1)} %bitcast.15), channel_id=1, source_target_pairs={{0,8},{8,0},{16,24},{24,16},{1,9},{9,1},{17,25},{25,17},{2,10},{10... | collective-permute-start | bytes 2949128 | tf_op jit(solution)/shard_map/ppermute | solution.py:358
  202.7 25.9 %collective-permute-start.1 = (bf16[240,2048]{1,0:T(8,128)(2,1)}, bf16[240,2048]{1,0:T(8,128)(2,1)}, u32[]{:S(2)}, u32[]{:S(2)}) collective-permute-start(bf16[240,2048]{1,0:T(8,128)(2,1)} %bitcast.18), channel_id=1, source_target_pairs={{0,16},{8,24},{16,0},{24,8},{1,17},{9,25},{17,1},{25,9},{2,18},{10... | collective-permute-start | bytes 2949128 | tf_op jit(solution)/shard_map/ppermute | solution.py:358
  230.3 12.8 %collective-permute-start.2 = (bf16[120,2048]{1,0:T(8,128)(2,1)S(1)}, bf16[120,2048]{1,0:T(8,128)(2,1)S(1)}, u32[]{:S(2)}, u32[]{:S(2)}) collective-permute-start(bf16[120,2048]{1,0:T(8,128)(2,1)S(1)} %constant_dynamic-slice_fusion.11), channel_id=1, source_target_pairs={{0,16},{8,24},{16,0},{24,8},{1,17},{9,25},{17,1},{25,9},{2,18},{10... | collective-permute-start | bytes 1474568 | tf_op jit(solution)/shard_map/ppermute | solution.py:358
  231.8 12.2 %collective-permute-start.3 = (bf16[120,2048]{1,0:T(8,128)(2,1)S(1)}, bf16[120,2048]{1,0:T(8,128)(2,1)S(1)}, u32[]{:S(2)}, u32[]{:S(2)}) collective-permute-start(bf16[120,2048]{1,0:T(8,128)(2,1)S(1)} %constant_dynamic-slice_fusion.8), channel_id=1, source_target_pairs={{0,8},{8,0},{16,24},{24,16},{1,9},{9,1},{17,25},{25,17},{2,10},{10... | collective-permute-start | bytes 1474568 | tf_op jit(solution)/shard_map/ppermute | solution.py:358
  244.9 13.8 %collective-permute-start.4 = (bf16[120,2048]{1,0:T(8,128)(2,1)S(1)}, bf16[120,2048]{1,0:T(8,128)(2,1)S(1)}, u32[]{:S(2)}, u32[]{:S(2)}) collective-permute-start(bf16[120,2048]{1,0:T(8,128)(2,1)S(1)} %add_convert_fusion.7.refs_0_), channel_id=1, source_target_pairs={{0,16},{8,24},{16,0},{24,8},{1,17},{9,25},{17,1},{25,9},{2,18},{10... | collective-permute-start | bytes 1474568 | tf_op jit(solution)/shard_map/ppermute | solution.py:358
  245.7 13.8 %collective-permute-start.5 = (bf16[120,2048]{1,0:T(8,128)(2,1)}, bf16[120,2048]{1,0:T(8,128)(2,1)}, u32[]{:S(2)}, u32[]{:S(2)}) collective-permute-start(bf16[120,2048]{1,0:T(8,128)(2,1)} %add_convert_fusion.6.refs_4_), channel_id=1, source_target_pairs={{0,8},{8,0},{16,24},{24,16},{1,9},{9,1},{17,25},{25,17},{2,10},{10... | collective-permute-start | bytes 1474568 | tf_op jit(solution)/shard_map/ppermute | solution.py:358
  259.5 50.3 %collective-permute-start.8 = (bf16[120,2048]{1,0:T(8,128)(2,1)S(1)}, bf16[120,2048]{1,0:T(8,128)(2,1)}, u32[]{:S(2)}, u32[]{:S(2)}) collective-permute-start(bf16[120,2048]{1,0:T(8,128)(2,1)S(1)} %add_convert_fusion.7.refs_0_), channel_id=1, source_target_pairs={{0,8},{8,0},{16,24},{24,16},{1,9},{9,1},{17,25},{25,17},{2,10},{10... | collective-permute-start | bytes 1474568 | tf_op jit(solution)/shard_map/ppermute | solution.py:358
  260.5 49.4 %collective-permute-start.9 = (bf16[120,2048]{1,0:T(8,128)(2,1)}, bf16[120,2048]{1,0:T(8,128)(2,1)}, u32[]{:S(2)}, u32[]{:S(2)}) collective-permute-start(bf16[120,2048]{1,0:T(8,128)(2,1)} %add_convert_fusion.6.refs_4_), channel_id=1, source_target_pairs={{0,16},{8,24},{16,0},{24,8},{1,17},{9,25},{17,1},{25,9},{2,18},{10... | collective-permute-start | bytes 1474568 | tf_op jit(solution)/shard_map/ppermute | solution.py:358
  261.7 41.7 %collective-permute-start.6 = (bf16[352,2048]{1,0:T(8,128)(2,1)}, bf16[352,2048]{1,0:T(8,128)(2,1)}, u32[]{:S(2)}, u32[]{:S(2)}) collective-permute-start(bf16[352,2048]{1,0:T(8,128)(2,1)} %constant_dynamic-slice_fusion.7), channel_id=1, source_target_pairs={{0,8},{8,0},{16,24},{24,16},{1,9},{9,1},{17,25},{25,17},{2,10},{10... | collective-permute-start | bytes 4325384 | tf_op jit(solution)/shard_map/ppermute | solution.py:358
  263.1 42.8 %collective-permute-start.7 = (bf16[352,2048]{1,0:T(8,128)(2,1)S(1)}, bf16[352,2048]{1,0:T(8,128)(2,1)}, u32[]{:S(2)}, u32[]{:S(2)}) collective-permute-start(bf16[352,2048]{1,0:T(8,128)(2,1)S(1)} %constant_dynamic-slice_fusion.6), channel_id=1, source_target_pairs={{0,16},{8,24},{16,0},{24,8},{1,17},{9,25},{17,1},{25,9},{2,18},{10... | collective-permute-start | bytes 4325384 | tf_op jit(solution)/shard_map/ppermute | solution.py:358
  309.8 30.4 %collective-permute-start.10 = (bf16[176,2048]{1,0:T(8,128)(2,1)}, bf16[176,2048]{1,0:T(8,128)(2,1)}, u32[]{:S(2)}, u32[]{:S(2)}) collective-permute-start(bf16[176,2048]{1,0:T(8,128)(2,1)} %constant_dynamic-slice_fusion.5), channel_id=1, source_target_pairs={{0,16},{8,24},{16,0},{24,8},{1,17},{9,25},{17,1},{25,9},{2,18},{10... | collective-permute-start | bytes 2162696 | tf_op jit(solution)/shard_map/ppermute | solution.py:358
  311.5 31.0 %collective-permute-start.11 = (bf16[176,2048]{1,0:T(8,128)(2,1)}, bf16[176,2048]{1,0:T(8,128)(2,1)}, u32[]{:S(2)}, u32[]{:S(2)}) collective-permute-start(bf16[176,2048]{1,0:T(8,128)(2,1)} %constant_dynamic-slice_fusion.4), channel_id=1, source_target_pairs={{0,8},{8,0},{16,24},{24,16},{1,9},{9,1},{17,25},{25,17},{2,10},{10... | collective-permute-start | bytes 2162696 | tf_op jit(solution)/shard_map/ppermute | solution.py:358
  312.1 31.7 %collective-permute-start.12 = (bf16[120,2048]{1,0:T(8,128)(2,1)}, bf16[120,2048]{1,0:T(8,128)(2,1)S(1)}, u32[]{:S(2)}, u32[]{:S(2)}) collective-permute-start(bf16[120,2048]{1,0:T(8,128)(2,1)} %copy-done.17), channel_id=1, source_target_pairs={{0,8},{8,0},{16,24},{24,16},{1,9},{9,1},{17,25},{25,17},{2,10},{10... | collective-permute-start | bytes 1474568 | tf_op jit(solution)/shard_map/ppermute | solution.py:358
  313.5 30.4 %collective-permute-start.13 = (bf16[120,2048]{1,0:T(8,128)(2,1)}, bf16[120,2048]{1,0:T(8,128)(2,1)}, u32[]{:S(2)}, u32[]{:S(2)}) collective-permute-start(bf16[120,2048]{1,0:T(8,128)(2,1)} %collective-permute-done.5.refs_5_), channel_id=1, source_target_pairs={{0,16},{8,24},{16,0},{24,8},{1,17},{9,25},{17,1},{25,9},{2,18},{10... | collective-permute-start | bytes 1474568 | tf_op jit(solution)/shard_map/ppermute | solution.py:358
  345.4 13.8 %collective-permute-start.14 = (bf16[176,2048]{1,0:T(8,128)(2,1)S(1)}, bf16[176,2048]{1,0:T(8,128)(2,1)S(1)}, u32[]{:S(2)}, u32[]{:S(2)}) collective-permute-start(bf16[176,2048]{1,0:T(8,128)(2,1)S(1)} %copy-done.5), channel_id=1, source_target_pairs={{0,16},{8,24},{16,0},{24,8},{1,17},{9,25},{17,1},{25,9},{2,18},{10... | collective-permute-start | bytes 2162696 | tf_op jit(solution)/shard_map/ppermute | solution.py:358
  346.9 13.3 %collective-permute-start.15 = (bf16[176,2048]{1,0:T(8,128)(2,1)S(1)}, bf16[176,2048]{1,0:T(8,128)(2,1)}, u32[]{:S(2)}, u32[]{:S(2)}) collective-permute-start(bf16[176,2048]{1,0:T(8,128)(2,1)S(1)} %add_convert_fusion.4.refs_4_), channel_id=1, source_target_pairs={{0,8},{8,0},{16,24},{24,16},{1,9},{9,1},{17,25},{25,17},{2,10},{10... | collective-permute-start | bytes 2162696 | tf_op jit(solution)/shard_map/ppermute | solution.py:358
  362.6 14.5 %collective-permute-start.17 = (bf16[512,768]{1,0:T(8,128)(2,1)}, bf16[512,768]{1,0:T(8,128)(2,1)S(1)}, u32[]{:S(2)}, u32[]{:S(2)}) collective-permute-start(bf16[512,768]{1,0:T(8,128)(2,1)} %get-tuple-element.316), channel_id=1, source_target_pairs={{0,16},{8,24},{16,0},{24,8},{1,17},{9,25},{17,1},{25,9},{2,18},{10... | collective-permute-start | bytes 2359304 | tf_op jit(solution)/shard_map/ppermute | solution.py:358
  363.7 14.3 %collective-permute-start.16 = (bf16[512,768]{1,0:T(8,128)(2,1)S(1)}, bf16[512,768]{1,0:T(8,128)(2,1)}, u32[]{:S(2)}, u32[]{:S(2)}) collective-permute-start(bf16[512,768]{1,0:T(8,128)(2,1)S(1)} %get-tuple-element.317), channel_id=1, source_target_pairs={{0,8},{8,0},{16,24},{24,16},{1,9},{9,1},{17,25},{25,17},{2,10},{10... | collective-permute-start | bytes 2359304 | tf_op jit(solution)/shard_map/ppermute | solution.py:358
  381.1 12.3 %collective-permute-start.20 = (bf16[256,768]{1,0:T(8,128)(2,1)}, bf16[256,768]{1,0:T(8,128)(2,1)S(1)}, u32[]{:S(2)}, u32[]{:S(2)}) collective-permute-start(bf16[256,768]{1,0:T(8,128)(2,1)} %constant_dynamic-slice_fusion.2), channel_id=1, source_target_pairs={{0,16},{8,24},{16,0},{24,8},{1,17},{9,25},{17,1},{25,9},{2,18},{10... | collective-permute-start | bytes 1179656 | tf_op jit(solution)/shard_map/ppermute | solution.py:358
  382.0 12.3 %collective-permute-start.21 = (bf16[256,768]{1,0:T(8,128)(2,1)S(1)}, bf16[256,768]{1,0:T(8,128)(2,1)S(1)}, u32[]{:S(2)}, u32[]{:S(2)}) collective-permute-start(bf16[256,768]{1,0:T(8,128)(2,1)S(1)} %constant_dynamic-slice_fusion), channel_id=1, source_target_pairs={{0,8},{8,0},{16,24},{24,16},{1,9},{9,1},{17,25},{25,17},{2,10},{10... | collective-permute-start | bytes 1179656 | tf_op jit(solution)/shard_map/ppermute | solution.py:358
  383.1 26.3 %collective-permute-start.18 = (bf16[176,2048]{1,0:T(8,128)(2,1)}, bf16[176,2048]{1,0:T(8,128)(2,1)S(1)}, u32[]{:S(2)}, u32[]{:S(2)}) collective-permute-start(bf16[176,2048]{1,0:T(8,128)(2,1)} %add_convert_fusion.5.refs_0_), channel_id=1, source_target_pairs={{0,8},{8,0},{16,24},{24,16},{1,9},{9,1},{17,25},{25,17},{2,10},{10... | collective-permute-start | bytes 2162696 | tf_op jit(solution)/shard_map/ppermute | solution.py:358
  384.0 25.4 %collective-permute-start.19 = (bf16[176,2048]{1,0:T(8,128)(2,1)}, bf16[176,2048]{1,0:T(8,128)(2,1)S(1)}, u32[]{:S(2)}, u32[]{:S(2)}) collective-permute-start(bf16[176,2048]{1,0:T(8,128)(2,1)} %copy-done.6), channel_id=1, source_target_pairs={{0,16},{8,24},{16,0},{24,8},{1,17},{9,25},{17,1},{25,9},{2,18},{10... | collective-permute-start | bytes 2162696 | tf_op jit(solution)/shard_map/ppermute | solution.py:358
  385.1 45.0 %collective-permute-start.23 = (bf16[176,2048]{1,0:T(8,128)(2,1)}, bf16[176,2048]{1,0:T(8,128)(2,1)}, u32[]{:S(2)}, u32[]{:S(2)}) collective-permute-start(bf16[176,2048]{1,0:T(8,128)(2,1)} %copy-done.14), channel_id=1, source_target_pairs={{0,8},{8,0},{16,24},{24,16},{1,9},{9,1},{17,25},{25,17},{2,10},{10... | collective-permute-start | bytes 2162696 | tf_op jit(solution)/shard_map/ppermute | solution.py:358
  393.4 36.8 %collective-permute-start.24 = (bf16[176,2048]{1,0:T(8,128)(2,1)}, bf16[176,2048]{1,0:T(8,128)(2,1)}, u32[]{:S(2)}, u32[]{:S(2)}) collective-permute-start(bf16[176,2048]{1,0:T(8,128)(2,1)} %collective-permute-done.15.refs_5_), channel_id=1, source_target_pairs={{0,16},{8,24},{16,0},{24,8},{1,17},{9,25},{17,1},{25,9},{2,18},{10... | collective-permute-start | bytes 2162696 | tf_op jit(solution)/shard_map/ppermute | solution.py:358
  394.3 42.1 %copy-start.11 = (bf16[256,768]{1,0:T(8,128)(2,1)}, bf16[256,768]{1,0:T(8,128)(2,1)S(1)}, u32[]{:S(2)}) copy-start(bf16[256,768]{1,0:T(8,128)(2,1)S(1)} %add_convert_fusion.9.refs_0_) | copy-start | bytes 1179652
  394.4 42.0 %copy-start.12 = (bf16[256,768]{1,0:T(8,128)(2,1)}, bf16[256,768]{1,0:T(8,128)(2,1)S(1)}, u32[]{:S(2)}) copy-start(bf16[256,768]{1,0:T(8,128)(2,1)S(1)} %add_convert_fusion.8.refs_2_) | copy-start | bytes 1179652
  410.3 19.9 %collective-permute-start.25 = (bf16[256,768]{1,0:T(8,128)(2,1)S(1)}, bf16[256,768]{1,0:T(8,128)(2,1)S(1)}, u32[]{:S(2)}, u32[]{:S(2)}) collective-permute-start(bf16[256,768]{1,0:T(8,128)(2,1)S(1)} %add_convert_fusion.9.refs_0_), channel_id=1, source_target_pairs={{0,16},{8,24},{16,0},{24,8},{1,17},{9,25},{17,1},{25,9},{2,18},{10... | collective-permute-start | bytes 1179656 | tf_op jit(solution)/shard_map/ppermute | solution.py:358
  411.4 18.8 %collective-permute-start.26 = (bf16[256,768]{1,0:T(8,128)(2,1)S(1)}, bf16[256,768]{1,0:T(8,128)(2,1)S(1)}, u32[]{:S(2)}, u32[]{:S(2)}) collective-permute-start(bf16[256,768]{1,0:T(8,128)(2,1)S(1)} %add_convert_fusion.8.refs_2_), channel_id=1, source_target_pairs={{0,8},{8,0},{16,24},{24,16},{1,9},{9,1},{17,25},{25,17},{2,10},{10... | collective-permute-start | bytes 1179656 | tf_op jit(solution)/shard_map/ppermute | solution.py:358
  412.7 17.4 %collective-permute-start.22 = (f32[6,128]{1,0:T(8,128)S(1)}, f32[6,128]{1,0:T(8,128)S(1)}, u32[]{:S(2)}, u32[]{:S(2)}) collective-permute-start(f32[6,128]{1,0:T(8,128)S(1)} %bitcast.131), channel_id=1, source_target_pairs={{0,8},{8,0},{16,24},{24,16},{1,9},{9,1},{17,25},{25,17},{2,10},{10... | collective-permute-start | bytes 9224 | tf_op jit(solution)/shard_map/ppermute | solution.py:358
  430.2 19.8 %collective-permute-start.28 = (bf16[256,768]{1,0:T(8,128)(2,1)S(1)}, bf16[256,768]{1,0:T(8,128)(2,1)S(1)}, u32[]{:S(2)}, u32[]{:S(2)}) collective-permute-start(bf16[256,768]{1,0:T(8,128)(2,1)S(1)} %add_convert_fusion.9.refs_0_), channel_id=1, source_target_pairs={{0,8},{8,0},{16,24},{24,16},{1,9},{9,1},{17,25},{25,17},{2,10},{10... | collective-permute-start | bytes 1179656 | tf_op jit(solution)/shard_map/ppermute | solution.py:358
  431.7 18.2 %collective-permute-start.29 = (bf16[256,768]{1,0:T(8,128)(2,1)S(1)}, bf16[256,768]{1,0:T(8,128)(2,1)S(1)}, u32[]{:S(2)}, u32[]{:S(2)}) collective-permute-start(bf16[256,768]{1,0:T(8,128)(2,1)S(1)} %collective-permute-done.25.refs_1_), channel_id=1, source_target_pairs={{0,8},{8,0},{16,24},{24,16},{1,9},{9,1},{17,25},{25,17},{2,10},{10... | collective-permute-start | bytes 1179656 | tf_op jit(solution)/shard_map/ppermute | solution.py:358
  432.3 17.7 %collective-permute-start.30 = (bf16[256,768]{1,0:T(8,128)(2,1)S(1)}, bf16[256,768]{1,0:T(8,128)(2,1)S(1)}, u32[]{:S(2)}, u32[]{:S(2)}) collective-permute-start(bf16[256,768]{1,0:T(8,128)(2,1)S(1)} %add_convert_fusion.8.refs_2_), channel_id=1, source_target_pairs={{0,16},{8,24},{16,0},{24,8},{1,17},{9,25},{17,1},{25,9},{2,18},{10... | collective-permute-start | bytes 1179656 | tf_op jit(solution)/shard_map/ppermute | solution.py:358
  433.7 17.1 %collective-permute-start.31 = (bf16[256,768]{1,0:T(8,128)(2,1)S(1)}, bf16[256,768]{1,0:T(8,128)(2,1)S(1)}, u32[]{:S(2)}, u32[]{:S(2)}) collective-permute-start(bf16[256,768]{1,0:T(8,128)(2,1)S(1)} %collective-permute-done.26.refs_3_), channel_id=1, source_target_pairs={{0,16},{8,24},{16,0},{24,8},{1,17},{9,25},{17,1},{25,9},{2,18},{10... | collective-permute-start | bytes 1179656 | tf_op jit(solution)/shard_map/ppermute | solution.py:358
  434.3 15.6 %collective-permute-start.27 = (f32[6,128]{1,0:T(8,128)S(1)}, f32[6,128]{1,0:T(8,128)S(1)}, u32[]{:S(2)}, u32[]{:S(2)}) collective-permute-start(f32[6,128]{1,0:T(8,128)S(1)} %add.375), channel_id=1, source_target_pairs={{0,16},{8,24},{16,0},{24,8},{1,17},{9,25},{17,1},{25,9},{2,18},{10... | collective-permute-start | bytes 9224 | tf_op jit(solution)/shard_map/ppermute | solution.py:358
  462.4 3.6 collective-permute-start.34
  462.4 4.2 collective-permute-start.33
  462.5 4.2 collective-permute-start.32
  467.4 4.9 %collective-permute-start.35 = (f32[4,2048]{1,0:T(4,128)S(1)}, f32[4,2048]{1,0:T(4,128)S(1)}, u32[]{:S(2)}, u32[]{:S(2)}) collective-permute-start(f32[4,2048]{1,0:T(4,128)S(1)} %add_add_fusion.1), channel_id=1, source_target_pairs={{0,4},{1,5},{2,6},{3,7},{4,0},{5,1},{6,2},{7,3},{8,12},{9,13},{10,... | collective-permute-start | bytes 98312 | tf_op jit(solution)/shard_map/ppermute | solution.py:358
  472.4 4.9 collective-permute-start.38
  473.8 3.9 collective-permute-start.37
  475.1 3.9 collective-permute-start.36
  (30 other events, 215.7 us)
Sparse Core Ops, SparseCore 0:
  11.5 84.7 all-gather.2
  97.9 80.5 all-gather.4
  180.7 88.0 reduce-scatter.3
  271.5 88.0 reduce-scatter.5
  361.7 87.9 reduce-scatter.7

commit v7 on v5

--- a/solution.py
+++ b/solution.py
@@ -350,8 +350,12 @@
 
 
 def swap(values, name, bit):
+    return swap_mask(values, name, 1 << bit)
+
+
+def swap_mask(values, name, mask):
     size = lax.axis_size(name)
-    return lax.ppermute(values, name, [(i, i ^ (1 << bit)) for i in range(size)])
+    return lax.ppermute(values, name, [(i, i ^ mask) for i in range(size)])
 
 
 def write_stacked(piece, outs):
@@ -539,6 +543,16 @@
     for bit in range(count) if bits is None else bits:
         values = values + swap(values, name, bit)
     return values
+
+
+def sum_pairs(values, name):
+    count = bits_of(name)
+    if count is None:
+        return lax.psum(values, name)
+    for bit in range(0, count - 1, 2):
+        one, two, both = (swap_mask(values, name, mask << bit) for mask in (1, 2, 3))
+        values = (values + one) + (two + both)
+    return values + swap(values, name, count - 1) if count % 2 else values
 
 
 def norm_kernel(x_ref, gain_ref, shift_ref, out_ref):
@@ -794,7 +808,7 @@
         (grad_normed, grad_w_gate_up, grad_w_qkv)
     )
     input_grad, small = tail(layer_in, grad_normed, cot_here, norm_gain, stat_row)
-    small = sum_small(sum_small(small, "mp"), "dp")
+    small = sum_pairs(sum_pairs(small, "mp"), "dp")
     totals = small[2]
     return (
         layer_out[:, None],

time: 495 us -> 493 us (level)
  waiting for transfers between devices: 131 us -> 117 us
  Pallas kernels: 131 us -> 141 us
    ppermute x37 -> x39, waiting for transfers between devices: 54.5 us -> 43.4 us  [swap_mask(): return lax.ppermute(values, name, [(i, i ^ mask) for i in range(size)])]
    pallas_call x1, Pallas kernels: 34.9 us -> 40.4 us  [attend_back(): pl.pallas_call(attend_back_kernel, grid_spec=pltpu.PrefetchScalarGridSpec...]
    ppermute x37 -> x39, starting transfers between devices: 43.5 us -> 40.7 us  [swap_mask(): return lax.ppermute(values, name, [(i, i ^ mask) for i in range(size)])]
  transfers between devices with their start and end apart: 42 -> 44, of which waited for: 18 -> 15; matrix products, arithmetic and copies ran while one was open for 32% -> 32% of each run, Pallas kernels for 25% -> 27%
where the time goes in v7:
time: 493 us; the launch traced here: 486 us
  Pallas kernels  141 us (29%)
  waiting for transfers between devices  117 us (24%)
  matrix products  105 us (21%)
  starting transfers between devices  41.7 us (8%)
  other arithmetic  39.4 us (8%)
  local copies, waits for them, and re-layouts  24.9 us (5%)
  between operations  15.9 us (3%)
    all_gather x1, waiting for transfers between devices, local(): gathered = lax.all_gather(normed, 'mp', axis=0, tiled=True)  73.5 us
    dot_general x5, matrix products, token_sum(): lax.dot_general(left, right, (((0,), (0,)), ((), ())), preferred_element_...  46 us
    ppermute x39, waiting for transfers between devices, swap_mask(): return lax.ppermute(values, name, [(i, i ^ mask) for i in range(size)])  43.4 us
    dot_general x4, matrix products, turned_product(): lax.dot_general(left, right, (((1,), (1,)), ((), ())), preferred_element_...  43.2 us
    ppermute x39, starting transfers between devices, swap_mask(): return lax.ppermute(values, name, [(i, i ^ mask) for i in range(size)])  40.7 us
    pallas_call x1, Pallas kernels, attend_back(): pl.pallas_call(attend_back_kernel, grid_spec=pltpu.PrefetchScalarGridSpec...  40.4 us
    pallas_call x1, Pallas kernels, attend(): pl.pallas_call(attend_kernel, grid_spec=pltpu.PrefetchScalarGridSpec(num_...  29.6 us
    pallas_call x1, Pallas kernels, back_products(): pl.pallas_call(back_products_kernel, grid=(length // rows,), in_specs=[pl...  26.2 us
  transfers between devices with their start and end apart: 44, of which 15 were waited for; matrix products, arithmetic and copies ran while one was open for 32% of the time, Pallas kernels for 27%

profile of v7, /device:TPU:0, one launch (start us, length us, event | category | flops | bytes accessed | tf_op | source)
XLA Modules:
  0.0 485.6 jit_solution(12424316307794123451)
XLA Ops:
  7.2 4.1 norm.1
  12.6 2.3 bitcast_select_fusion.c_ref
  17.0 5.8 %fusion.13 = (f32[2048,128]{1,0:T(8,128)}, f32[2048,128]{1,0:T(8,128)}, f32[2048,128]{1,0:T(8,128)}) fusion(f32[128]{0:T(128)S(1)} %compare_select_fusion.5, f32[2048]{0:T(1024)S(1)} %fusion.17, pred[128]{0:T(512)(128)(4,1)S(1)} %get-tuple-element.351, pred[128]{0:T(512)(128)(4,1)S(1)} %get-tuple-element.352), kind=kLoop, calls=%fused_computation.42 | loop fusion | flops 1048576 | bytes 3154688 | tf_op jit(solution)/shard_map/jit(_where)/select_n | solution.py:41
  22.8 73.5 %all-gather.3.cloned.1.call-done.x_ref = bf16[2048,2048]{1,0:T(8,128)(2,1)} async-done(((bf16[256,2048]{1,0:T(8,128)(2,1)}), bf16[2048,2048]{1,0:T(8,128)(2,1)}) %all-gather.3.cloned.1.call-update) | async-done | bytes 8388624 | tf_op jit(solution)/shard_map/all_gather | solution.py:687
  96.3 10.1 %fusion.6 = f32[2048,704]{1,0:T(8,128)S(1)} fusion(bf16[2048,2048]{1,0:T(8,128)(2,1)} %all-gather.3.cloned.1.call-done.x_ref, bf16[2,704,2048]{2,1,0:T(8,128)(2,1)} %bitcast.112), kind=kOutput, calls=%fused_computation.20 | convolution fusion | flops 5905580032 | bytes 17039360 | tf_op jit(solution)/shard_map/dot_general | solution.py:704
  106.4 13.1 %multiply_convert_fusion = (bf16[2048,704]{1,0:T(8,128)(2,1)S(1)}, f32[2048,704]{1,0:T(8,128)}) fusion(f32[2048,704]{1,0:T(8,128)S(1)} %fusion.6, bf16[2048,2048]{1,0:T(8,128)(2,1)S(1)} %copy-done.28, bf16[2,704,2048]{2,1,0:T(8,128)(2,1)} %bitcast.113), kind=kOutput, calls=%fused_computation.10 | convolution fusion | flops 5914230784 | bytes 25690112 | tf_op jit(solution)/shard_map/dot_general | solution.py:704
  119.5 1.7 copy-done.29
  121.2 8.9 %convolution_convert_fusion.1 = bf16[2048,2048]{1,0:T(8,128)(2,1)} fusion(bf16[2048,704]{1,0:T(8,128)(2,1)S(1)} %get-tuple-element.349, bf16[704,2048]{1,0:T(8,128)(2,1)S(1)} %copy-done), kind=kOutput, calls=%fused_computation.3 | convolution fusion | flops 5909774336 | bytes 14155776 | tf_op jit(solution)/shard_map/dot_general | solution.py:701
  130.4 13.2 %project.1 = (bf16[2048,256]{1,0:T(8,128)(2,1)}, bf16[2048,256]{1,0:T(8,128)(2,1)}, bf16[2048,256]{1,0:T(8,128)(2,1)}) custom-call(bf16[2048,2048]{1,0:T(8,128)(2,1)} %all-gather.3.cloned.1.call-done.x_ref, bf16[3,2048,256]{2,1,0:T(8,128)(2,1)} %bitcast.115, bf16[3,256]{1,0:T(4,128)(2,1)} %b_ref.1, f32[2048,128]{1,0:T(8,128)} %get-tuple-element.168.cos_ref, ...), custom_call_target="tpu_custom_call" | custom-call | flops 6442450944 | bytes 14680064 | tf_op jit(solution)/shard_map/project/pallas_call | solution.py:78
  143.6 29.6 %attend.1 = (bf16[2048,256]{1,0:T(8,128)(2,1)}, f32[16,1,512]{2,1,0:T(1,128)}) custom-call(s32[16]{0:T(128)} %and_select_fusion.first_ref, bf16[2048,256]{1,0:T(8,128)(2,1)} %get-tuple-element.171.q_ref, bf16[2048,256]{1,0:T(8,128)(2,1)} %get-tuple-element.172.k_ref, bf16[2048,256]{1,0:T(8,128)(2,1)} %get-tuple-element.173.v_ref, s32[16,1,128]{2,1,0:T(1,128)} %copy-done.26), custom_call_target="tpu_custom_call" | custom-call | flops 8589934592 | bytes 4194304 | tf_op jit(solution)/shard_map/attend/pallas_call | solution.py:181
  173.2 7.3 %convolution_convert_fusion = bf16[2048,2048]{1,0:T(8,128)(2,1)} fusion(bf16[2048,256]{1,0:T(8,128)(2,1)} %get-tuple-element.175.o_ref, bf16[256,2048]{1,0:T(8,128)(2,1)} %param.21), kind=kOutput, calls=%fused_computation.2 | convolution fusion | flops 2151677952 | bytes 10485760 | tf_op jit(solution)/shard_map/dot_general | solution.py:701
  180.5 7.2 %convolution_convert_fusion.8 = bf16[256,2048]{1,0:T(8,128)(2,1)} fusion(bf16[2048,256]{1,0:T(8,128)(2,1)} %get-tuple-element.175.o_ref, bf16[2048,2048]{1,0:T(8,128)(2,1)} %all-gather.5.cloned.1.call-done), kind=kOutput, calls=%fused_computation.29 | convolution fusion | flops 2148007936 | bytes 10485760 | tf_op jit(solution)/shard_map/dot_general | solution.py:709
  188.6 7.6 %convolution_convert_fusion.6 = bf16[704,2048]{1,0:T(8,128)(2,1)} fusion(bf16[2048,704]{1,0:T(8,128)(2,1)S(1)} %copy-done.30, bf16[2048,2048]{1,0:T(8,128)(2,1)S(1)} %copy-done.2), kind=kOutput, calls=%fused_computation.16 | convolution fusion | flops 5907021824 | bytes 14155776 | tf_op jit(solution)/shard_map/dot_general | solution.py:709
  196.9 2.0 constant_dynamic-slice_fusion.9
  198.9 2.1 constant_dynamic-slice_fusion.10
  203.1 2.6 collective-permute-start.1
  205.7 15.3 %fusion.4 = (bf16[2048,704]{1,0:T(8,128)(2,1)}, bf16[2048,704]{1,0:T(8,128)(2,1)S(1)}) fusion(f32[2048,704]{1,0:T(8,128)} %copy-done.31, f32[2048,704]{1,0:T(8,128)} %get-tuple-element.350, bf16[2048,2048]{1,0:T(8,128)(2,1)} %all-gather.5.cloned.1.call-done, bf16[704,2048]{1,0:T(8,128)(2,1)S(1)} %copy-done), kind=kOutput, calls=%fused_computation.8 | convolution fusion | flops 5927206912 | bytes 28573696 | tf_op jit(solution)/shard_map/dot_general | solution.py:704
  222.2 4.7 convolution_convert_fusion.7.do_ref
  229.1 1.6 fusion.11
  231.5 1.8 collective-permute-start.3
  233.3 9.8 %convolution_convert_fusion.5 = bf16[704,2048]{1,0:T(8,128)(2,1)} fusion(bf16[2048,704]{1,0:T(8,128)(2,1)S(1)} %get-tuple-element.181.g_ref, bf16[2048,2048]{1,0:T(8,128)(2,1)} %all-gather.3.cloned.1.call-done.x_ref), kind=kOutput, calls=%fused_computation.15 | convolution fusion | flops 5907021824 | bytes 14155776 | tf_op jit(solution)/shard_map/dot_general | solution.py:709
  246.9 9.8 %convolution_convert_fusion.4 = bf16[704,2048]{1,0:T(8,128)(2,1)S(1)} fusion(bf16[2048,704]{1,0:T(8,128)(2,1)} %get-tuple-element.186.u_ref, bf16[2048,2048]{1,0:T(8,128)(2,1)} %all-gather.3.cloned.1.call-done.x_ref), kind=kOutput, calls=%fused_computation.14 | convolution fusion | flops 5907021824 | bytes 14155776 | tf_op jit(solution)/shard_map/dot_general | solution.py:709
  263.7 40.4 %attend_back.1.p_ref = bf16[2048,768]{1,0:T(8,128)(2,1)} custom-call(s32[16]{0:T(128)} %and_select_fusion.first_ref, bf16[2048,256]{1,0:T(8,128)(2,1)} %get-tuple-element.171.q_ref, bf16[2048,256]{1,0:T(8,128)(2,1)} %get-tuple-element.172.k_ref, bf16[2048,256]{1,0:T(8,128)(2,1)} %get-tuple-element.173.v_ref, ...), custom_call_target="tpu_custom_call" | custom-call | flops 21474836480 | bytes 8388608 | tf_op jit(solution)/shard_map/attend_back/pallas_call | solution.py:312
  304.1 2.5 add_convert_fusion.1
  306.8 1.9 add_convert_fusion
  312.8 1.9 collective-permute-start.13
  314.7 26.2 %back_products.1 = bf16[2048,2048]{1,0:T(8,128)(2,1)} custom-call(bf16[2048,768]{1,0:T(8,128)(2,1)} %attend_back.1.p_ref, bf16[3,2048,256]{2,1,0:T(8,128)(2,1)} %bitcast.116, bf16[2048,704]{1,0:T(8,128)(2,1)} %copy-done.4, bf16[2048,704]{1,0:T(8,128)(2,1)} %get-tuple-element.186.u_ref, bf16[2,704,2048]{2,1,0:T(8,128)(2,1)} %bitcast.114), custom_call_target="tpu_custom_call" | custom-call | tf_op jit(solution)/shard_map/back_products/pallas_call | solution.py:646
  341.0 2.2 add_convert_fusion.5.refs_0_
  347.6 11.6 %convolution_convert_fusion.3 = bf16[2048,768]{1,0:T(8,128)(2,1)} fusion(bf16[2048,2048]{1,0:T(8,128)(2,1)} %all-gather.3.cloned.1.call-done.x_ref, bf16[2048,768]{1,0:T(8,128)(2,1)} %attend_back.1.p_ref), kind=kOutput, calls=%fused_computation.13 | convolution fusion | flops 6444023808 | bytes 14680064 | tf_op jit(solution)/shard_map/dot_general | solution.py:709
  360.8 2.4 constant_dynamic-slice_fusion.1
  365.0 3.1 convert_reduce_fusion
  368.1 9.8 %collective-permute-done.17 = bf16[512,768]{1,0:T(8,128)(2,1)S(1)} collective-permute-done((bf16[512,768]{1,0:T(8,128)(2,1)}, bf16[512,768]{1,0:T(8,128)(2,1)S(1)}, u32[]{:S(2)}, u32[]{:S(2)}) %collective-permute-start.17) | collective-permute-done | bytes 786464 | tf_op jit(solution)/shard_map/ppermute | solution.py:358
  378.8 2.3 add_convert_fusion.2
  386.8 3.1 fusion.8
  390.5 3.3 select_maximum_fusion
  395.3 15.1 %collective-permute-done.18.refs_2_ = bf16[176,2048]{1,0:T(8,128)(2,1)S(1)} collective-permute-done((bf16[176,2048]{1,0:T(8,128)(2,1)}, bf16[176,2048]{1,0:T(8,128)(2,1)S(1)}, u32[]{:S(2)}, u32[]{:S(2)}) %collective-permute-start.18) | collective-permute-done | bytes 720928 | tf_op jit(solution)/shard_map/ppermute | solution.py:358
  415.2 7.2 %place_blocks.3 = (f32[704,2048]{1,0:T(8,128)}, f32[256,2048]{1,0:T(8,128)}) custom-call(s32[8]{0:T(128)} %constant.122.clone.color_ref, s32[8]{0:T(128)} %stack.109.where_ref, bf16[120,2048]{1,0:T(8,128)(2,1)} %copy-done.10, bf16[120,2048]{1,0:T(8,128)(2,1)} %copy-done.17, bf16[120,2048]{1,0:T(8,128)(2,1)} %collective-permute-done.8.refs_2_, ...), custom_call_target="tpu_custom_call" | custom-call | bytes 11796480 | tf_op jit(solution)/shard_map/place_blocks/pallas_call | solution.py:391
  422.4 8.6 %collective-permute-done.22 = f32[6,128]{1,0:T(8,128)S(1)} collective-permute-done((f32[6,128]{1,0:T(8,128)S(1)}, f32[6,128]{1,0:T(8,128)S(1)}, u32[]{:S(2)}, u32[]{:S(2)}) %collective-permute-start.22) | collective-permute-done | bytes 3104 | tf_op jit(solution)/shard_map/ppermute | solution.py:358
  431.0 1.8 collective-permute-start.28
  433.1 1.8 collective-permute-start.30
  435.1 1.8 collective-permute-start.27
  437.5 8.7 %place_blocks.4 = f32[2,704,2048]{2,1,0:T(8,128)} custom-call(s32[8]{0:T(128)} %constant.122.clone.color_ref, s32[8]{0:T(128)} %stack.118.where_ref, bf16[176,2048]{1,0:T(8,128)(2,1)} %add_convert_fusion.5.refs_0_, bf16[176,2048]{1,0:T(8,128)(2,1)} %copy-done.14, bf16[176,2048]{1,0:T(8,128)(2,1)} %copy-done.15, ...), custom_call_target="tpu_custom_call" | custom-call | bytes 17301504 | tf_op jit(solution)/shard_map/place_blocks/pallas_call | solution.py:391
  448.4 6.8 %place_blocks.5 = f32[3,2048,256]{2,1,0:T(8,128)} custom-call(s32[8]{0:T(128)} %constant.122.clone.color_ref, s32[8]{0:T(128)} %stack.127.where_ref, bf16[256,768]{1,0:T(8,128)(2,1)} %copy-done.11, bf16[256,768]{1,0:T(8,128)(2,1)} %copy-done.19, bf16[256,768]{1,0:T(8,128)(2,1)} %copy-done.21, bf16[256,768]{1,0:T(8,128)(2,1)} %copy-done.22, ...), custom_call_target="tpu_custom_call" | custom-call | bytes 9437184 | tf_op jit(solution)/shard_map/place_blocks/pallas_call | solution.py:391
  455.2 5.1 %tail.1 = (f32[256,1,2048]{2,1,0:T(1,128)}, f32[4,2048]{1,0:T(4,128)}) custom-call(bf16[256,2048]{1,0:T(8,128)(2,1)} %bitcast.110, bf16[256,2048]{1,0:T(8,128)(2,1)} %reduce-scatter.8.cloned.1.call-done.g_ref, bf16[256,2048]{1,0:T(8,128)(2,1)} %bitcast_select_fusion.c_ref, f32[1,2048]{1,0:T(1,128)} %bitcast.128, f32[1,2048]{1,0:T(1,128)} %bitcast.129), custom_call_target="tpu_custom_call" | custom-call | tf_op jit(solution)/shard_map/tail/pallas_call | solution.py:610
  460.4 1.8 collective-permute-start.32
  462.1 1.7 collective-permute-done.34
  465.3 1.7 collective-permute-start.35
  467.0 3.2 collective-permute-done.35
  (193 shorter events, 59.9 us)
Async XLA Ops:
  7.2 114.0 %copy-start = (bf16[704,2048]{1,0:T(8,128)(2,1)S(1)}, bf16[704,2048]{1,0:T(8,128)(2,1)}, u32[]{:S(2)}) copy-start(bf16[704,2048]{1,0:T(8,128)(2,1)} %param.23) | copy-start | bytes 8650756
  7.2 89.1 %all-gather.3.cloned.1.call-start = ((), (), s32[]{:S(2)}) async-start(), calls=%async_computation.3 | async-start | bytes 9437184 | tf_op jit(solution)/shard_map/all_gather | solution.py:687
  11.3 169.2 %all-gather.5.cloned.1.call-start = ((), (), s32[]{:S(2)}) async-start(), calls=%async_computation.4 | async-start | bytes 9437184 | tf_op jit(solution)/shard_map/all_gather | solution.py:688
  14.9 295.7 %reduce-scatter.4.cloned.1.call-start = ((), (), s32[]{:S(2)}) async-start(), calls=%async_computation.5 | async-start | bytes 9437184 | tf_op jit(solution)/shard_map/reduce_scatter | solution.py:714
  16.0 90.4 %copy-start.26 = (s32[16,1,128]{2,1,0:T(1,128)}, s32[16,1,128]{2,1,0:T(1,128)S(1)}, u32[]{:S(2)}) copy-start(s32[16,1,128]{2,1,0:T(1,128)S(1)} %broadcast_maximum_fusion.start_ref) | copy-start | bytes 24580
  130.1 251.8 %reduce-scatter.6.cloned.1.call-start = ((), (), s32[]{:S(2)}) async-start(), calls=%async_computation.6 | async-start | bytes 9437184 | tf_op jit(solution)/shard_map/reduce_scatter | solution.py:714
  196.3 258.9 %reduce-scatter.8.cloned.1.call-start = ((), (), s32[]{:S(2)}) async-start(), calls=%async_computation.7 | async-start | bytes 9437184 | tf_op jit(solution)/shard_map/reduce_scatter | solution.py:714
  203.1 24.3 %collective-permute-start = (bf16[240,2048]{1,0:T(8,128)(2,1)}, bf16[240,2048]{1,0:T(8,128)(2,1)}, u32[]{:S(2)}, u32[]{:S(2)}) collective-permute-start(bf16[240,2048]{1,0:T(8,128)(2,1)} %bitcast.15), channel_id=1, source_target_pairs={{0,8},{8,0},{16,24},{24,16},{1,9},{9,1},{17,25},{25,17},{2,10},{10... | collective-permute-start | bytes 2949128 | tf_op jit(solution)/shard_map/ppermute | solution.py:358
  203.1 26.0 %collective-permute-start.1 = (bf16[240,2048]{1,0:T(8,128)(2,1)}, bf16[240,2048]{1,0:T(8,128)(2,1)}, u32[]{:S(2)}, u32[]{:S(2)}) collective-permute-start(bf16[240,2048]{1,0:T(8,128)(2,1)} %bitcast.18), channel_id=1, source_target_pairs={{0,16},{8,24},{16,0},{24,8},{1,17},{9,25},{17,1},{25,9},{2,18},{10... | collective-permute-start | bytes 2949128 | tf_op jit(solution)/shard_map/ppermute | solution.py:358
  230.7 12.7 %collective-permute-start.2 = (bf16[120,2048]{1,0:T(8,128)(2,1)S(1)}, bf16[120,2048]{1,0:T(8,128)(2,1)S(1)}, u32[]{:S(2)}, u32[]{:S(2)}) collective-permute-start(bf16[120,2048]{1,0:T(8,128)(2,1)S(1)} %constant_dynamic-slice_fusion.11), channel_id=1, source_target_pairs={{0,16},{8,24},{16,0},{24,8},{1,17},{9,25},{17,1},{25,9},{2,18},{10... | collective-permute-start | bytes 1474568 | tf_op jit(solution)/shard_map/ppermute | solution.py:358
  231.5 12.5 %collective-permute-start.3 = (bf16[120,2048]{1,0:T(8,128)(2,1)S(1)}, bf16[120,2048]{1,0:T(8,128)(2,1)S(1)}, u32[]{:S(2)}, u32[]{:S(2)}) collective-permute-start(bf16[120,2048]{1,0:T(8,128)(2,1)S(1)} %constant_dynamic-slice_fusion.8), channel_id=1, source_target_pairs={{0,8},{8,0},{16,24},{24,16},{1,9},{9,1},{17,25},{25,17},{2,10},{10... | collective-permute-start | bytes 1474568 | tf_op jit(solution)/shard_map/ppermute | solution.py:358
  245.0 13.9 %collective-permute-start.4 = (bf16[120,2048]{1,0:T(8,128)(2,1)S(1)}, bf16[120,2048]{1,0:T(8,128)(2,1)S(1)}, u32[]{:S(2)}, u32[]{:S(2)}) collective-permute-start(bf16[120,2048]{1,0:T(8,128)(2,1)S(1)} %add_convert_fusion.7.refs_0_), channel_id=1, source_target_pairs={{0,16},{8,24},{16,0},{24,8},{1,17},{9,25},{17,1},{25,9},{2,18},{10... | collective-permute-start | bytes 1474568 | tf_op jit(solution)/shard_map/ppermute | solution.py:358
  246.0 13.6 %collective-permute-start.5 = (bf16[120,2048]{1,0:T(8,128)(2,1)}, bf16[120,2048]{1,0:T(8,128)(2,1)}, u32[]{:S(2)}, u32[]{:S(2)}) collective-permute-start(bf16[120,2048]{1,0:T(8,128)(2,1)} %add_convert_fusion.6.refs_4_), channel_id=1, source_target_pairs={{0,8},{8,0},{16,24},{24,16},{1,9},{9,1},{17,25},{25,17},{2,10},{10... | collective-permute-start | bytes 1474568 | tf_op jit(solution)/shard_map/ppermute | solution.py:358
  259.7 50.9 %collective-permute-start.8 = (bf16[120,2048]{1,0:T(8,128)(2,1)S(1)}, bf16[120,2048]{1,0:T(8,128)(2,1)}, u32[]{:S(2)}, u32[]{:S(2)}) collective-permute-start(bf16[120,2048]{1,0:T(8,128)(2,1)S(1)} %add_convert_fusion.7.refs_0_), channel_id=1, source_target_pairs={{0,8},{8,0},{16,24},{24,16},{1,9},{9,1},{17,25},{25,17},{2,10},{10... | collective-permute-start | bytes 1474568 | tf_op jit(solution)/shard_map/ppermute | solution.py:358
  260.8 49.8 %collective-permute-start.9 = (bf16[120,2048]{1,0:T(8,128)(2,1)}, bf16[120,2048]{1,0:T(8,128)(2,1)}, u32[]{:S(2)}, u32[]{:S(2)}) collective-permute-start(bf16[120,2048]{1,0:T(8,128)(2,1)} %add_convert_fusion.6.refs_4_), channel_id=1, source_target_pairs={{0,16},{8,24},{16,0},{24,8},{1,17},{9,25},{17,1},{25,9},{2,18},{10... | collective-permute-start | bytes 1474568 | tf_op jit(solution)/shard_map/ppermute | solution.py:358
  261.7 42.4 %collective-permute-start.6 = (bf16[352,2048]{1,0:T(8,128)(2,1)}, bf16[352,2048]{1,0:T(8,128)(2,1)}, u32[]{:S(2)}, u32[]{:S(2)}) collective-permute-start(bf16[352,2048]{1,0:T(8,128)(2,1)} %constant_dynamic-slice_fusion.7), channel_id=1, source_target_pairs={{0,8},{8,0},{16,24},{24,16},{1,9},{9,1},{17,25},{25,17},{2,10},{10... | collective-permute-start | bytes 4325384 | tf_op jit(solution)/shard_map/ppermute | solution.py:358
  263.2 43.4 %collective-permute-start.7 = (bf16[352,2048]{1,0:T(8,128)(2,1)S(1)}, bf16[352,2048]{1,0:T(8,128)(2,1)}, u32[]{:S(2)}, u32[]{:S(2)}) collective-permute-start(bf16[352,2048]{1,0:T(8,128)(2,1)S(1)} %constant_dynamic-slice_fusion.6), channel_id=1, source_target_pairs={{0,16},{8,24},{16,0},{24,8},{1,17},{9,25},{17,1},{25,9},{2,18},{10... | collective-permute-start | bytes 4325384 | tf_op jit(solution)/shard_map/ppermute | solution.py:358
  310.6 30.4 %collective-permute-start.10 = (bf16[176,2048]{1,0:T(8,128)(2,1)}, bf16[176,2048]{1,0:T(8,128)(2,1)}, u32[]{:S(2)}, u32[]{:S(2)}) collective-permute-start(bf16[176,2048]{1,0:T(8,128)(2,1)} %constant_dynamic-slice_fusion.5), channel_id=1, source_target_pairs={{0,16},{8,24},{16,0},{24,8},{1,17},{9,25},{17,1},{25,9},{2,18},{10... | collective-permute-start | bytes 2162696 | tf_op jit(solution)/shard_map/ppermute | solution.py:358
  310.7 32.5 %collective-permute-start.11 = (bf16[176,2048]{1,0:T(8,128)(2,1)}, bf16[176,2048]{1,0:T(8,128)(2,1)}, u32[]{:S(2)}, u32[]{:S(2)}) collective-permute-start(bf16[176,2048]{1,0:T(8,128)(2,1)} %constant_dynamic-slice_fusion.4), channel_id=1, source_target_pairs={{0,8},{8,0},{16,24},{24,16},{1,9},{9,1},{17,25},{25,17},{2,10},{10... | collective-permute-start | bytes 2162696 | tf_op jit(solution)/shard_map/ppermute | solution.py:358
  312.1 32.4 %collective-permute-start.12 = (bf16[120,2048]{1,0:T(8,128)(2,1)}, bf16[120,2048]{1,0:T(8,128)(2,1)S(1)}, u32[]{:S(2)}, u32[]{:S(2)}) collective-permute-start(bf16[120,2048]{1,0:T(8,128)(2,1)} %copy-done.17), channel_id=1, source_target_pairs={{0,8},{8,0},{16,24},{24,16},{1,9},{9,1},{17,25},{25,17},{2,10},{10... | collective-permute-start | bytes 1474568 | tf_op jit(solution)/shard_map/ppermute | solution.py:358
  312.8 31.8 %collective-permute-start.13 = (bf16[120,2048]{1,0:T(8,128)(2,1)}, bf16[120,2048]{1,0:T(8,128)(2,1)}, u32[]{:S(2)}, u32[]{:S(2)}) collective-permute-start(bf16[120,2048]{1,0:T(8,128)(2,1)} %collective-permute-done.5.refs_5_), channel_id=1, source_target_pairs={{0,16},{8,24},{16,0},{24,8},{1,17},{9,25},{17,1},{25,9},{2,18},{10... | collective-permute-start | bytes 1474568 | tf_op jit(solution)/shard_map/ppermute | solution.py:358
  346.1 13.8 %collective-permute-start.14 = (bf16[176,2048]{1,0:T(8,128)(2,1)S(1)}, bf16[176,2048]{1,0:T(8,128)(2,1)S(1)}, u32[]{:S(2)}, u32[]{:S(2)}) collective-permute-start(bf16[176,2048]{1,0:T(8,128)(2,1)S(1)} %copy-done.5), channel_id=1, source_target_pairs={{0,16},{8,24},{16,0},{24,8},{1,17},{9,25},{17,1},{25,9},{2,18},{10... | collective-permute-start | bytes 2162696 | tf_op jit(solution)/shard_map/ppermute | solution.py:358
  346.2 14.6 %collective-permute-start.15 = (bf16[176,2048]{1,0:T(8,128)(2,1)S(1)}, bf16[176,2048]{1,0:T(8,128)(2,1)}, u32[]{:S(2)}, u32[]{:S(2)}) collective-permute-start(bf16[176,2048]{1,0:T(8,128)(2,1)S(1)} %add_convert_fusion.4.refs_4_), channel_id=1, source_target_pairs={{0,8},{8,0},{16,24},{24,16},{1,9},{9,1},{17,25},{25,17},{2,10},{10... | collective-permute-start | bytes 2162696 | tf_op jit(solution)/shard_map/ppermute | solution.py:358
  363.2 14.7 %collective-permute-start.17 = (bf16[512,768]{1,0:T(8,128)(2,1)}, bf16[512,768]{1,0:T(8,128)(2,1)S(1)}, u32[]{:S(2)}, u32[]{:S(2)}) collective-permute-start(bf16[512,768]{1,0:T(8,128)(2,1)} %get-tuple-element.330), channel_id=1, source_target_pairs={{0,16},{8,24},{16,0},{24,8},{1,17},{9,25},{17,1},{25,9},{2,18},{10... | collective-permute-start | bytes 2359304 | tf_op jit(solution)/shard_map/ppermute | solution.py:358
  364.1 14.6 %collective-permute-start.16 = (bf16[512,768]{1,0:T(8,128)(2,1)S(1)}, bf16[512,768]{1,0:T(8,128)(2,1)}, u32[]{:S(2)}, u32[]{:S(2)}) collective-permute-start(bf16[512,768]{1,0:T(8,128)(2,1)S(1)} %get-tuple-element.331), channel_id=1, source_target_pairs={{0,8},{8,0},{16,24},{24,16},{1,9},{9,1},{17,25},{25,17},{2,10},{10... | collective-permute-start | bytes 2359304 | tf_op jit(solution)/shard_map/ppermute | solution.py:358
  381.9 12.1 %collective-permute-start.20 = (bf16[256,768]{1,0:T(8,128)(2,1)S(1)}, bf16[256,768]{1,0:T(8,128)(2,1)S(1)}, u32[]{:S(2)}, u32[]{:S(2)}) collective-permute-start(bf16[256,768]{1,0:T(8,128)(2,1)S(1)} %constant_dynamic-slice_fusion.2), channel_id=1, source_target_pairs={{0,16},{8,24},{16,0},{24,8},{1,17},{9,25},{17,1},{25,9},{2,18},{10... | collective-permute-start | bytes 1179656 | tf_op jit(solution)/shard_map/ppermute | solution.py:358
  382.7 12.4 %collective-permute-start.21 = (bf16[256,768]{1,0:T(8,128)(2,1)}, bf16[256,768]{1,0:T(8,128)(2,1)S(1)}, u32[]{:S(2)}, u32[]{:S(2)}) collective-permute-start(bf16[256,768]{1,0:T(8,128)(2,1)} %constant_dynamic-slice_fusion), channel_id=1, source_target_pairs={{0,8},{8,0},{16,24},{24,16},{1,9},{9,1},{17,25},{25,17},{2,10},{10... | collective-permute-start | bytes 1179656 | tf_op jit(solution)/shard_map/ppermute | solution.py:358
  384.0 26.4 %collective-permute-start.18 = (bf16[176,2048]{1,0:T(8,128)(2,1)}, bf16[176,2048]{1,0:T(8,128)(2,1)S(1)}, u32[]{:S(2)}, u32[]{:S(2)}) collective-permute-start(bf16[176,2048]{1,0:T(8,128)(2,1)} %add_convert_fusion.5.refs_0_), channel_id=1, source_target_pairs={{0,8},{8,0},{16,24},{24,16},{1,9},{9,1},{17,25},{25,17},{2,10},{10... | collective-permute-start | bytes 2162696 | tf_op jit(solution)/shard_map/ppermute | solution.py:358
  384.8 25.6 %collective-permute-start.19 = (bf16[176,2048]{1,0:T(8,128)(2,1)}, bf16[176,2048]{1,0:T(8,128)(2,1)S(1)}, u32[]{:S(2)}, u32[]{:S(2)}) collective-permute-start(bf16[176,2048]{1,0:T(8,128)(2,1)} %copy-done.6), channel_id=1, source_target_pairs={{0,16},{8,24},{16,0},{24,8},{1,17},{9,25},{17,1},{25,9},{2,18},{10... | collective-permute-start | bytes 2162696 | tf_op jit(solution)/shard_map/ppermute | solution.py:358
  386.0 44.9 %collective-permute-start.23 = (bf16[176,2048]{1,0:T(8,128)(2,1)}, bf16[176,2048]{1,0:T(8,128)(2,1)}, u32[]{:S(2)}, u32[]{:S(2)}) collective-permute-start(bf16[176,2048]{1,0:T(8,128)(2,1)} %copy-done.14), channel_id=1, source_target_pairs={{0,8},{8,0},{16,24},{24,16},{1,9},{9,1},{17,25},{25,17},{2,10},{10... | collective-permute-start | bytes 2162696 | tf_op jit(solution)/shard_map/ppermute | solution.py:358
  394.0 37.0 %collective-permute-start.24 = (bf16[176,2048]{1,0:T(8,128)(2,1)}, bf16[176,2048]{1,0:T(8,128)(2,1)}, u32[]{:S(2)}, u32[]{:S(2)}) collective-permute-start(bf16[176,2048]{1,0:T(8,128)(2,1)} %collective-permute-done.15.refs_5_), channel_id=1, source_target_pairs={{0,16},{8,24},{16,0},{24,8},{1,17},{9,25},{17,1},{25,9},{2,18},{10... | collective-permute-start | bytes 2162696 | tf_op jit(solution)/shard_map/ppermute | solution.py:358
  395.1 51.0 %copy-start.11 = (bf16[256,768]{1,0:T(8,128)(2,1)}, bf16[256,768]{1,0:T(8,128)(2,1)S(1)}, u32[]{:S(2)}) copy-start(bf16[256,768]{1,0:T(8,128)(2,1)S(1)} %add_convert_fusion.9.refs_0_) | copy-start | bytes 1179652
  395.2 50.9 %copy-start.12 = (bf16[256,768]{1,0:T(8,128)(2,1)}, bf16[256,768]{1,0:T(8,128)(2,1)S(1)}, u32[]{:S(2)}) copy-start(bf16[256,768]{1,0:T(8,128)(2,1)S(1)} %add_convert_fusion.8.refs_4_) | copy-start | bytes 1179652
  411.2 19.7 %collective-permute-start.25 = (bf16[256,768]{1,0:T(8,128)(2,1)S(1)}, bf16[256,768]{1,0:T(8,128)(2,1)S(1)}, u32[]{:S(2)}, u32[]{:S(2)}) collective-permute-start(bf16[256,768]{1,0:T(8,128)(2,1)S(1)} %add_convert_fusion.9.refs_0_), channel_id=1, source_target_pairs={{0,16},{8,24},{16,0},{24,8},{1,17},{9,25},{17,1},{25,9},{2,18},{10... | collective-permute-start | bytes 1179656 | tf_op jit(solution)/shard_map/ppermute | solution.py:358
  412.5 18.5 %collective-permute-start.26 = (bf16[256,768]{1,0:T(8,128)(2,1)S(1)}, bf16[256,768]{1,0:T(8,128)(2,1)S(1)}, u32[]{:S(2)}, u32[]{:S(2)}) collective-permute-start(bf16[256,768]{1,0:T(8,128)(2,1)S(1)} %add_convert_fusion.8.refs_4_), channel_id=1, source_target_pairs={{0,8},{8,0},{16,24},{24,16},{1,9},{9,1},{17,25},{25,17},{2,10},{10... | collective-permute-start | bytes 1179656 | tf_op jit(solution)/shard_map/ppermute | solution.py:358
  413.3 17.6 %collective-permute-start.22 = (f32[6,128]{1,0:T(8,128)S(1)}, f32[6,128]{1,0:T(8,128)S(1)}, u32[]{:S(2)}, u32[]{:S(2)}) collective-permute-start(f32[6,128]{1,0:T(8,128)S(1)} %bitcast.131), channel_id=1, source_target_pairs={{0,8},{8,0},{16,24},{24,16},{1,9},{9,1},{17,25},{25,17},{2,10},{10... | collective-permute-start | bytes 9224 | tf_op jit(solution)/shard_map/ppermute | solution.py:358
  431.0 15.2 %collective-permute-start.28 = (bf16[256,768]{1,0:T(8,128)(2,1)S(1)}, bf16[256,768]{1,0:T(8,128)(2,1)S(1)}, u32[]{:S(2)}, u32[]{:S(2)}) collective-permute-start(bf16[256,768]{1,0:T(8,128)(2,1)S(1)} %add_convert_fusion.9.refs_0_), channel_id=1, source_target_pairs={{0,8},{8,0},{16,24},{24,16},{1,9},{9,1},{17,25},{25,17},{2,10},{10... | collective-permute-start | bytes 1179656 | tf_op jit(solution)/shard_map/ppermute | solution.py:358
  432.8 13.4 %collective-permute-start.29 = (bf16[256,768]{1,0:T(8,128)(2,1)S(1)}, bf16[256,768]{1,0:T(8,128)(2,1)S(1)}, u32[]{:S(2)}, u32[]{:S(2)}) collective-permute-start(bf16[256,768]{1,0:T(8,128)(2,1)S(1)} %collective-permute-done.25.refs_1_), channel_id=1, source_target_pairs={{0,8},{8,0},{16,24},{24,16},{1,9},{9,1},{17,25},{25,17},{2,10},{10... | collective-permute-start | bytes 1179656 | tf_op jit(solution)/shard_map/ppermute | solution.py:358
  433.1 13.2 %collective-permute-start.30 = (bf16[256,768]{1,0:T(8,128)(2,1)S(1)}, bf16[256,768]{1,0:T(8,128)(2,1)S(1)}, u32[]{:S(2)}, u32[]{:S(2)}) collective-permute-start(bf16[256,768]{1,0:T(8,128)(2,1)S(1)} %add_convert_fusion.8.refs_4_), channel_id=1, source_target_pairs={{0,16},{8,24},{16,0},{24,8},{1,17},{9,25},{17,1},{25,9},{2,18},{10... | collective-permute-start | bytes 1179656 | tf_op jit(solution)/shard_map/ppermute | solution.py:358
  434.8 11.4 %collective-permute-start.31 = (bf16[256,768]{1,0:T(8,128)(2,1)S(1)}, bf16[256,768]{1,0:T(8,128)(2,1)S(1)}, u32[]{:S(2)}, u32[]{:S(2)}) collective-permute-start(bf16[256,768]{1,0:T(8,128)(2,1)S(1)} %collective-permute-done.26.refs_5_), channel_id=1, source_target_pairs={{0,16},{8,24},{16,0},{24,8},{1,17},{9,25},{17,1},{25,9},{2,18},{10... | collective-permute-start | bytes 1179656 | tf_op jit(solution)/shard_map/ppermute | solution.py:358
  435.1 11.1 %collective-permute-start.27 = (f32[6,128]{1,0:T(8,128)S(1)}, f32[6,128]{1,0:T(8,128)S(1)}, u32[]{:S(2)}, u32[]{:S(2)}) collective-permute-start(f32[6,128]{1,0:T(8,128)S(1)} %add.375), channel_id=1, source_target_pairs={{0,16},{8,24},{16,0},{24,8},{1,17},{9,25},{17,1},{25,9},{2,18},{10... | collective-permute-start | bytes 9224 | tf_op jit(solution)/shard_map/ppermute | solution.py:358
  460.3 3.6 collective-permute-start.34
  460.3 4.2 collective-permute-start.33
  460.4 4.2 collective-permute-start.32
  465.3 4.9 %collective-permute-start.35 = (f32[4,2048]{1,0:T(4,128)S(1)}, f32[4,2048]{1,0:T(4,128)S(1)}, u32[]{:S(2)}, u32[]{:S(2)}) collective-permute-start(f32[4,2048]{1,0:T(4,128)S(1)} %add_add_fusion.1), channel_id=1, source_target_pairs={{0,4},{1,5},{2,6},{3,7},{4,0},{5,1},{6,2},{7,3},{8,12},{9,13},{10,... | collective-permute-start | bytes 98312 | tf_op jit(solution)/shard_map/ppermute | solution.py:358
  470.2 4.9 %collective-permute-start.38 = (f32[4,2048]{1,0:T(4,128)S(1)}, f32[4,2048]{1,0:T(4,128)S(1)}, u32[]{:S(2)}, u32[]{:S(2)}) collective-permute-start(f32[4,2048]{1,0:T(4,128)S(1)} %add.400), channel_id=1, source_target_pairs={{0,24},{8,16},{16,8},{24,0},{1,25},{9,17},{17,9},{25,1},{2,26},{10... | collective-permute-start | bytes 98312 | tf_op jit(solution)/shard_map/ppermute | solution.py:358
  471.8 3.9 collective-permute-start.37
  472.6 3.9 collective-permute-start.36
  (30 other events, 231.0 us)
Sparse Core Ops, SparseCore 0:
  11.5 84.7 all-gather.2
  97.9 80.5 all-gather.4
  180.7 88.0 reduce-scatter.3
  271.5 88.1 reduce-scatter.5
  361.8 87.7 reduce-scatter.7
